TPU v7x, 768 devices: a whole 4x8x12 slice. The times are simulated.
768 devices in a mesh: dp: 48 (over z, y_lo), fsdp: 16 (over x, y_hi, core).
Axes of the slice: x: 4, y: 8 (y_hi: 2, y_lo: 4; y = y_hi * 4 + y_lo), z: 12, core: 2. Of those that a mesh axis runs over, the one named last changes fastest.
Arguments:
- inputs: float32 [640, 49152], P('fsdp', 'dp'), may hold values from -26 to 26, as said below
- norm_gain: float32 [640], P('fsdp'), may hold values from 0.1 to 1.9
- norm_bias: float32 [640], P('fsdp'), may hold values from -3 to 3
- conv_weight: float32 [9, 640, 640], P(None, 'fsdp'), may hold values from -0.078125 to 0.078125
- moment_one: float32 [9, 640, 640], P(None, 'fsdp'), may hold values from -3 to 3
- moment_two: float32 [9, 640, 640], P(None, 'fsdp'), may hold values from 0.5 to 4
- out_grad: float32 [640, 49152], P('fsdp', 'dp'), may hold values from -6 to 6
Outputs:
- block_out: float32 [640, 49152], P('fsdp', 'dp')
- input_grad: float32 [640, 49152], P('fsdp', 'dp')
- new_weight: float32 [9, 640, 640], P(None, 'fsdp')
- new_moment_one: float32 [9, 640, 640], P(None, 'fsdp')
- new_moment_two: float32 [9, 640, 640], P(None, 'fsdp')
Inputs may be any that keep to these rules, and one draw needn't show every extreme that they name: `inputs`: activations of mixed channel and pixel scales.
All inputs are finite; a program needn't handle non-finite values.
Results may differ from a plain program's by a relative error of at most 0.0027.
Values may be sent and summed in bfloat16 or wider, within the bound.
No kernel may reach another device: no remote copies, remote signals or barrier semaphores. Data moves between devices by JAX's collectives and lax.ppermute only.
A program may use at most 32 MiB of HBM per device.

v0:
```python
import jax
import jax.numpy as jnp
from jax import lax
from jax.sharding import PartitionSpec as P

GROUP_CH = 40
SIDE = 32


EPS_NORM = 1e-05
BETA_ONE = 0.9
BETA_TWO = 0.999
CORRECT_ONE = 1.0 - 0.9**10
CORRECT_TWO = 1.0 - 0.999**10
LEARN_RATE = 0.001
EPS_ADAM = 1e-08
OFFSETS = ((-1, -1), (-1, 0), (-1, 1), (0, -1), (0, 0), (0, 1), (1, -1), (1, 0), (1, 1))


def shifted(source, row_step, col_step):
    width_all = source.shape[-1]
    position = jnp.arange(width_all, dtype=jnp.int32)
    row_pos = position // SIDE % SIDE
    col_pos = position % SIDE
    inside = (
        (row_pos + row_step >= 0)
        & (row_pos + row_step < SIDE)
        & (col_pos + col_step >= 0)
        & (col_pos + col_step < SIDE)
    )
    margin = SIDE + 1
    padded = jnp.pad(source, ((0, 0), (margin, margin)))
    start_at = margin + row_step * SIDE + col_step
    moved = padded[:, start_at : start_at + width_all]
    return jnp.where(inside[None, :], moved, jnp.zeros_like(moved))


def group_stats(source, norm_gain, norm_bias):
    channels, width_all = source.shape
    images = width_all // (SIDE * SIDE)
    blocks = source.reshape(channels // GROUP_CH, GROUP_CH, images, SIDE * SIDE)
    mean_val = jnp.mean(blocks, axis=(1, 3), keepdims=True)
    centred = blocks - mean_val
    var_val = jnp.mean(centred * centred, axis=(1, 3), keepdims=True)
    inv_dev = lax.rsqrt(var_val + EPS_NORM)
    normed = (centred * inv_dev).reshape(channels, width_all)
    pre_act = normed * norm_gain[:, None] + norm_bias[:, None]
    return (normed, inv_dev, pre_act)


def group_backward(grad_act, pre_act, normed, inv_dev, norm_gain):
    channels, width_all = grad_act.shape
    images = width_all // (SIDE * SIDE)
    shape_four = (channels // GROUP_CH, GROUP_CH, images, SIDE * SIDE)
    sigmoid_val = jax.nn.sigmoid(pre_act)
    grad_pre = grad_act * sigmoid_val * (1.0 + pre_act * (1.0 - sigmoid_val))
    grad_norm = (grad_pre * norm_gain[:, None]).reshape(shape_four)
    normed_four = normed.reshape(shape_four)
    mean_first = jnp.mean(grad_norm, axis=(1, 3), keepdims=True)
    mean_second = jnp.mean(grad_norm * normed_four, axis=(1, 3), keepdims=True)
    return (inv_dev * (grad_norm - mean_first - normed_four * mean_second)).reshape(
        channels, width_all
    )


def body(inputs, norm_gain, norm_bias, conv_weight, moment_one, moment_two, out_grad):
    local_ch, group_width = inputs.shape
    images = group_width // (SIDE * SIDE)
    normed, inv_dev, pre_act = group_stats(inputs, norm_gain, norm_bias)
    activation = jax.nn.silu(pre_act).astype(jnp.bfloat16)
    weight_half = conv_weight.astype(jnp.bfloat16)
    grad_half = out_grad.astype(jnp.bfloat16)
    gathered = lax.all_gather(activation, "fsdp", axis=0, tiled=True)
    conv_out = jnp.zeros((local_ch, group_width), jnp.float32)
    grad_taps = []
    for tap_index, (row_step, col_step) in enumerate(OFFSETS):
        moved = shifted(gathered, row_step, col_step)
        conv_out = conv_out + jnp.dot(
            weight_half[tap_index], moved, preferred_element_type=jnp.float32
        )
        grad_taps.append(
            lax.dot_general(
                grad_half, moved, (((1,), (1,)), ((), ())), preferred_element_type=jnp.float32
            )
        )
    block_out = inputs + conv_out
    summed = lax.psum(jnp.stack(grad_taps), "dp")
    gradient = summed / (images * lax.axis_size("dp"))
    running = jnp.zeros((local_ch * lax.axis_size("fsdp"), group_width), jnp.float32)
    for tap_index, (row_step, col_step) in enumerate(OFFSETS):
        weight_part = weight_half[tap_index]
        back_term = lax.dot_general(
            weight_part, grad_half, (((0,), (0,)), ((), ())), preferred_element_type=jnp.float32
        )
        running = running + shifted(back_term, -row_step, -col_step)
    grad_act = lax.psum_scatter(running, "fsdp", scatter_dimension=0, tiled=True)
    input_grad = out_grad + group_backward(grad_act, pre_act, normed, inv_dev, norm_gain)
    first_new = BETA_ONE * moment_one + (1.0 - BETA_ONE) * gradient
    second_new = BETA_TWO * moment_two + (1.0 - BETA_TWO) * gradient * gradient
    weight_new = conv_weight - LEARN_RATE * (first_new / CORRECT_ONE) / (
        jnp.sqrt(second_new / CORRECT_TWO) + EPS_ADAM
    )
    return (block_out, input_grad, weight_new, first_new, second_new)


def solution(mesh):
    placed = (
        P("fsdp", "dp"),
        P("fsdp"),
        P("fsdp"),
        P(None, "fsdp", None),
        P(None, "fsdp", None),
        P(None, "fsdp", None),
        P("fsdp", "dp"),
    )
    return jax.shard_map(
        body,
        mesh=mesh,
        in_specs=placed,
        out_specs=(
            P("fsdp", "dp"),
            P("fsdp", "dp"),
            P(None, "fsdp", None),
            P(None, "fsdp", None),
            P(None, "fsdp", None),
        ),
        check_vma=False,
    )
```

profile of v0, /device:TPU:6, one launch (start us, length us, event | category | flops | bytes accessed | tf_op | source)
XLA Modules:
  0.0 672.6 jit_solution(7453944921245610216)
XLA Ops:
  7.2 1.6 reduce_sum.36
  9.4 1.6 multiply_reduce_fusion.1
  11.7 1.7 multiply_convert_fusion
  13.5 0.9 convert_element_type.31
  14.5 73.2 %all-gather.2.cloned.1.call-done = bf16[640,1024]{1,0:T(8,128)(2,1)} async-done(((bf16[40,1024]{1,0:T(8,128)(2,1)}), bf16[640,1024]{1,0:T(8,128)(2,1)}) %all-gather.2.cloned.1.call-update) | async-done | bytes 1310736 | tf_op jit(solution)/shard_map/all_gather | solution.py:73
  87.7 2.7 fusion.28
  90.4 1.3 fusion.27
  91.7 1.3 fusion.26
  93.0 1.3 fusion.25
  94.3 1.1 fusion.30
  95.5 1.3 fusion.24
  96.8 1.3 fusion.23
  98.1 1.3 fusion.22
  99.4 1.3 fusion.21
  100.9 441.6 %all-reduce.11.cloned.1.call-done = f32[9,40,640]{2,1,0:T(8,128)} async-done(((f32[9,40,640]{2,1,0:T(8,128)}), f32[9,40,640]{2,1,0:T(8,128)}) %all-reduce.11.cloned.1.call-update) | async-done | bytes 921616 | tf_op jit(solution)/shard_map/psum | solution.py:87
  542.6 3.1 divide_subtract_fusion
  549.9 6.9 %fusion.8 = f32[640,1024]{1,0:T(8,128)} fusion(f32[640,1024]{1,0:T(8,128)S(1)} %fusion.66, f32[640,1024]{1,0:T(8,128)S(1)} %fusion.67, f32[640,1024]{1,0:T(8,128)S(1)} %fusion.68, f32[640,1024]{1,0:T(8,128)S(1)} %fusion.69, f32[640,1024]{1,0:T(8,128)S(1)} %fusion.70, f32[640,1024]{1,0:T(8,128)S(1)} %fusion.71, f32[640,1024]{1,0:T(8,128)S(1)} %fusion.72, ...), kind=kOutput, calls=%fused_computation.16 | convolution fusion | flops 63569920 | bytes 23735296 | tf_op jit(solution)/shard_map/dot_general | solution.py:92
  556.8 1.3 copy-done.8
  558.7 0.6 convolution_add_fusion.6
  560.2 0.6 fusion.20
  563.0 1.3 fusion.19
  564.2 98.0 %reduce-scatter.2.cloned.1.call-done = f32[40,1024]{1,0:T(8,128)} async-done(((f32[640,1024]{1,0:T(8,128)}), f32[40,1024]{1,0:T(8,128)}) %reduce-scatter.2.cloned.1.call-update) | async-done | bytes 163856 | tf_op jit(solution)/shard_map/reduce_scatter | solution.py:96
  662.2 1.8 fusion.108
  665.4 0.7 multiply_add_fusion.2
  (42 shorter events, 8.2 us)
Async XLA Ops:
  7.2 80.5 %all-gather.2.cloned.1.call-start = ((), (), s32[]{:S(2)}) async-start(), calls=%async_computation.1 | async-start | bytes 1392640 | tf_op jit(solution)/shard_map/all_gather | solution.py:73
  13.4 529.1 %all-reduce.11.cloned.1.call-start = ((), (), s32[]{:S(2)}) async-start(), calls=%async_computation.3 | async-start | bytes 1843200 | tf_op jit(solution)/shard_map/psum | solution.py:87
  87.7 2.7 copy-start.7
  99.4 443.2 %copy-start.1 = (f32[9,40,640]{2,1,0:T(8,128)S(1)}, f32[9,40,640]{2,1,0:T(8,128)}, u32[]{:S(2)}) copy-start(f32[9,40,640]{2,1,0:T(8,128)} %param.10) | copy-start | bytes 2764804
  99.4 443.2 %copy-start.2 = (f32[9,40,640]{2,1,0:T(8,128)S(1)}, f32[9,40,640]{2,1,0:T(8,128)}, u32[]{:S(2)}) copy-start(f32[9,40,640]{2,1,0:T(8,128)} %param.11) | copy-start | bytes 2764804
  99.4 443.2 %copy-start.3 = (f32[9,40,640]{2,1,0:T(8,128)S(1)}, f32[9,40,640]{2,1,0:T(8,128)}, u32[]{:S(2)}) copy-start(f32[9,40,640]{2,1,0:T(8,128)} %param.12) | copy-start | bytes 2764804
  100.7 561.5 %reduce-scatter.2.cloned.1.call-start = ((), (), s32[]{:S(2)}) async-start(), calls=%async_computation.2 | async-start | bytes 2785280 | tf_op jit(solution)/shard_map/reduce_scatter | solution.py:96
  556.8 1.3 copy-start.8
  562.0 0.9 copy-start
  563.0 99.3 %copy-start.5 = (f32[40]{0:T(128)S(1)}, f32[40]{0:T(128)}, u32[]{:S(2)}) copy-start(f32[40]{0:T(128)} %param.9) | copy-start | bytes 484
  563.0 99.3 %copy-start.6 = (f32[40]{0:T(128)S(1)}, f32[40]{0:T(128)}, u32[]{:S(2)}) copy-start(f32[40]{0:T(128)} %param.8) | copy-start | bytes 484
  563.0 102.4 %copy-start.4 = (f32[40,1024]{1,0:T(8,128)S(1)}, f32[40,1024]{1,0:T(8,128)}, u32[]{:S(2)}) copy-start(f32[40,1024]{1,0:T(8,128)} %param.13) | copy-start | bytes 491524
Sparse Core Ops, SparseCore 0:
  13.5 74.1 all-gather.1
  100.8 441.6 all-reduce.10
  556.9 105.2 reduce-scatter.1
where the time goes:
time: 673 us
  waiting for transfers between devices  613 us (91%)
  matrix products  29.8 us (4%)
  between operations  16.6 us (2%)
  other arithmetic  11.4 us (2%)
    psum x1, waiting for transfers between devices, body(): summed = lax.psum(jnp.stack(grad_taps), 'dp')  442 us
    reduce_scatter x1, waiting for transfers between devices, body(): lax.psum_scatter(running, 'fsdp', scatter_dimension=0, tiled=True)  98 us
    all_gather x1, waiting for transfers between devices, body(): gathered = lax.all_gather(activation, 'fsdp', axis=0, tiled=True)  73.2 us
  transfers between devices with their start and end apart: 3, of which 3 were waited for; matrix products, arithmetic and copies ran while one was open for 1% of the time, Pallas kernels for 0%

commit v1 on v0

v1 whole, which is shorter than its diff:
```python
import jax
import jax.numpy as jnp
from jax import lax
from jax.experimental import pallas as pl
from jax.experimental.pallas import tpu as pltpu
from jax.sharding import Mesh, PartitionSpec as P

GROUP_CH = 40
SIDE = 32
ROWS_PAD = 32

EPS_NORM = 1e-05
BETA_ONE = 0.9
BETA_TWO = 0.999
CORRECT_ONE = 1.0 - 0.9**10
CORRECT_TWO = 1.0 - 0.999**10
LEARN_RATE = 0.001
EPS_ADAM = 1e-08
OFFSETS = ((-1, -1), (-1, 0), (-1, 1), (0, -1), (0, 0), (0, 1), (1, -1), (1, 0), (1, 1))

DP = ("z", "yl")
FSDP = ("x", "yh", "c")


def shifted(source, a, b):
    if a == 0 and b == 0:
        return source
    width = source.shape[-1]
    position = lax.broadcasted_iota(jnp.int32, (1, width), 1)
    row, col = position // SIDE, position % SIDE
    inside = (row + a >= 0) & (row + a < SIDE) & (col + b >= 0) & (col + b < SIDE)
    moved = pltpu.roll(source, (-(a * SIDE + b)) % width, 1)
    return jnp.where(inside, moved, 0.0)


def column(row):
    n = row.shape[1]
    eye = lax.broadcasted_iota(jnp.int32, (n, n), 0) == lax.broadcasted_iota(jnp.int32, (n, n), 1)
    return jnp.sum(jnp.where(eye, row, 0.0), axis=1, keepdims=True)


def norm_kernel(x_ref, gain_ref, bias_ref, act_ref, normed_ref, pre_ref, inv_ref):
    x = x_ref[...]
    count = x.shape[0] * x.shape[1]
    mean = jnp.sum(jnp.sum(x, axis=0, keepdims=True), axis=1, keepdims=True) / count
    centred = x - mean
    var = jnp.sum(jnp.sum(centred * centred, axis=0, keepdims=True), axis=1, keepdims=True) / count
    inv = lax.rsqrt(var + EPS_NORM)
    normed = centred * inv
    pre = normed * column(gain_ref[...]) + column(bias_ref[...])
    normed_ref[...] = normed
    pre_ref[...] = pre
    inv_ref[...] = jnp.broadcast_to(inv, inv_ref.shape)
    act_ref[...] = (pre * jax.nn.sigmoid(pre)).astype(jnp.bfloat16)


def nine_kernel(g_ref, out_ref):
    g = g_ref[...].astype(jnp.bfloat16).astype(jnp.float32)
    rows = g.shape[0]
    for tap, (a, b) in enumerate(OFFSETS):
        out_ref[tap * rows : (tap + 1) * rows, :] = shifted(g, -a, -b).astype(jnp.bfloat16)
    rest = out_ref.shape[0] - 9 * rows
    out_ref[9 * rows :, :] = jnp.zeros((rest, g.shape[1]), jnp.bfloat16)


def forward_kernel(w_ref, act_ref, x_ref, out_ref):
    rows = x_ref.shape[0]
    products = jnp.dot(w_ref[...], act_ref[...], preferred_element_type=jnp.float32)
    total = x_ref[...]
    for tap, (a, b) in enumerate(OFFSETS):
        total = total + shifted(products[tap * rows : (tap + 1) * rows, :], a, b)
    out_ref[...] = total


def back_kernel(parts_ref, normed_ref, pre_ref, inv_ref, gain_ref, grad_ref, out_ref):
    grad_act = jnp.sum(parts_ref[...].astype(jnp.float32), axis=0)
    pre, normed = pre_ref[...], normed_ref[...]
    s = jax.nn.sigmoid(pre)
    gn = grad_act * s * (1.0 + pre * (1.0 - s)) * column(gain_ref[...])
    count = gn.shape[0] * gn.shape[1]
    first = jnp.sum(jnp.sum(gn, axis=0, keepdims=True), axis=1, keepdims=True) / count
    second = jnp.sum(jnp.sum(gn * normed, axis=0, keepdims=True), axis=1, keepdims=True) / count
    out_ref[...] = grad_ref[...] + inv_ref[0:1, 0:1] * (gn - first - normed * second)


def body(inputs, norm_gain, norm_bias, conv_weight, moment_one, moment_two, out_grad):
    local_ch, width = inputs.shape
    n_fsdp = lax.axis_size(FSDP)
    n_z, n_yl, n_x = lax.axis_size("z"), lax.axis_size("yl"), lax.axis_size("x")
    n_dp = n_z * n_yl
    all_ch = local_ch * n_fsdp
    f32, bf16 = jnp.float32, jnp.bfloat16
    chunk_rows = -(-(9 * local_ch) // (8 * n_z)) * 8
    pad_rows = chunk_rows * n_z
    swap = [(0, 1), (1, 0)]
    gain_row, bias_row = norm_gain[None, :], norm_bias[None, :]

    tile = jax.ShapeDtypeStruct((local_ch, width), f32)
    act, normed, pre_act, inv = pl.pallas_call(
        norm_kernel,
        out_shape=(
            jax.ShapeDtypeStruct((local_ch, width), bf16), tile, tile,
            jax.ShapeDtypeStruct((8, 128), f32),
        ),
        name="norm",
    )(inputs, gain_row, bias_row)

    grad_rows = pl.pallas_call(
        nine_kernel, out_shape=jax.ShapeDtypeStruct((pad_rows, width), bf16), name="nine"
    )(out_grad)
    weight_nine = conv_weight.astype(bf16).reshape(9 * local_ch, all_ch)

    with jax.named_scope("act_yh"):
        other = lax.ppermute(act, "yh", swap)
    other, grad_rows, weight_nine = lax.optimization_barrier((other, grad_rows, weight_nine))
    mine = jnp.arange(2) == lax.axis_index("yh")
    pair = jnp.where(mine[:, None, None], act[None], other[None])
    with jax.named_scope("act_x"):
        by_x = lax.all_to_all(
            jnp.broadcast_to(pair[None], (n_x,) + pair.shape), "x", 0, 0, tiled=True
        )
    partial = lax.dot_general(
        weight_nine, grad_rows[: 9 * local_ch], (((0,), (0,)), ((), ())),
        preferred_element_type=f32,
    )
    partial = partial.astype(bf16).reshape(n_fsdp, local_ch, width)
    by_x, partial = lax.optimization_barrier((by_x, partial))
    by_x = by_x.reshape(n_x * 2, local_ch, width)
    with jax.named_scope("act_c"):
        other = lax.ppermute(by_x, "c", swap)
    mine = jnp.arange(2) == lax.axis_index("c")
    gathered = jnp.where(mine[None, :, None, None], by_x[:, None], other[:, None])
    gathered = gathered.reshape(all_ch, width)

    taps = lax.dot_general(
        grad_rows, gathered, (((1,), (1,)), ((), ())), preferred_element_type=f32
    )
    taps = taps.astype(bf16).reshape(n_z, chunk_rows, all_ch)
    with jax.named_scope("grad_z"):
        by_z = lax.all_to_all(taps, "z", 0, 0, tiled=True)

    block_out = pl.pallas_call(forward_kernel, out_shape=tile, name="forward")(
        weight_nine, gathered, inputs
    )
    by_z, block_out, partial = lax.optimization_barrier((by_z, block_out, partial))
    with jax.named_scope("back_f"):
        parts = lax.all_to_all(partial, FSDP, 0, 0, tiled=True)

    z_sum = jnp.sum(by_z.astype(f32), axis=0)
    with jax.named_scope("gather_yl"):
        by_yl = lax.all_gather(z_sum, "yl", axis=0)
    total = (jnp.sum(by_yl, axis=0) / n_dp).astype(bf16)
    with jax.named_scope("gather_z"):
        total = lax.all_gather(total, "z", axis=0, tiled=True)
    gradient = total[: 9 * local_ch].reshape(9, local_ch, all_ch).astype(f32)

    first_new = BETA_ONE * moment_one + (1.0 - BETA_ONE) * gradient
    second_new = BETA_TWO * moment_two + (1.0 - BETA_TWO) * gradient * gradient
    weight_new = conv_weight - LEARN_RATE * (first_new / CORRECT_ONE) / (
        jnp.sqrt(second_new / CORRECT_TWO) + EPS_ADAM
    )
    normed, weight_new = lax.optimization_barrier((normed, weight_new))
    input_grad = pl.pallas_call(back_kernel, out_shape=tile, name="back")(
        parts, normed, pre_act, inv, gain_row, out_grad
    )
    return (block_out, input_grad, weight_new, first_new, second_new)


def solution(mesh):
    five = Mesh(mesh.devices.reshape(12, 4, 4, 2, 2), ("z", "yl", "x", "yh", "c"))
    act, chan, wgt = P(FSDP, DP), P(FSDP), P(None, FSDP, None)
    return jax.shard_map(
        body,
        mesh=five,
        in_specs=(act, chan, chan, wgt, wgt, wgt, act),
        out_specs=(act, act, wgt, wgt, wgt),
        check_vma=False,
    )
```

time: 673 us -> 157 us (0.23)
  waiting for transfers between devices: 613 us -> 27 us
  blocking collectives: 0 us -> 66.2 us
  starting transfers between devices: 0.3 us -> 39.9 us
  matrix products: 29.8 us -> 3.57 us
  between operations: 16.6 us -> 0.75 us
  Pallas kernels: 0 us -> 9.71 us
    psum x1 -> x0, waiting for transfers between devices: 442 us -> none  [body(): summed = lax.psum(jnp.stack(grad_taps), 'dp')]
    reduce_scatter x1 -> x0, waiting for transfers between devices: 98 us -> none  [body(): lax.psum_scatter(running, 'fsdp', scatter_dimension=0, tiled=True)]
    all_gather x1 -> x0, waiting for transfers between devices: 73.2 us -> none  [body(): gathered = lax.all_gather(activation, 'fsdp', axis=0, tiled=True)]
    all_gather x0 -> x2, blocking collectives: none -> 66.2 us  [the longest x1 41.3 us: body(): by_yl = lax.all_gather(z_sum, 'yl', axis=0)]
    all_to_all x0 -> x3, starting transfers between devices: none -> 30.2 us  [the longest x1 11.7 us: body(): lax.all_to_all(jnp.broadcast_to(pair[None], (n_x,) + pair.shape), 'x', 0,...]
    dot_general x27 -> x2, matrix products: 29.8 us -> 3.57 us  [the longest x1 1.97 us: body(): lax.dot_general(weight_nine, grad_rows[:9 * local_ch], (((0,), (0,)), (()...]
    all_to_all x0 -> x3, waiting for transfers between devices: none -> 24.5 us  [the longest x1 19.8 us: body(): by_z = lax.all_to_all(taps, 'z', 0, 0, tiled=True)]
    ppermute x0 -> x2, starting transfers between devices: none -> 9.76 us  [the longest x1 7.85 us: body(): other = lax.ppermute(act, 'yh', swap)]
  transfers between devices with their start and end apart: 3 -> 5, of which waited for: 3 -> 4; matrix products, arithmetic and copies ran while one was open for 1% -> 5% of each run, Pallas kernels for 0% -> 3%
where the time goes in v1:
time: 157 us
  blocking collectives  66.2 us (42%)
  starting transfers between devices  39.9 us (25%)
  waiting for transfers between devices  27 us (17%)
  Pallas kernels  9.71 us (6%)
  other arithmetic  7.27 us (5%)
  matrix products  3.57 us (2%)
  local copies, waits for them, and re-layouts  2.25 us (1%)
    all_gather x1, blocking collectives, body(): by_yl = lax.all_gather(z_sum, 'yl', axis=0)  41.3 us
    all_gather x1, blocking collectives, body(): total = lax.all_gather(total, 'z', axis=0, tiled=True)  24.9 us
    all_to_all x1, waiting for transfers between devices, body(): by_z = lax.all_to_all(taps, 'z', 0, 0, tiled=True)  19.8 us
    all_to_all x1, starting transfers between devices, body(): lax.all_to_all(jnp.broadcast_to(pair[None], (n_x,) + pair.shape), 'x', 0,...  11.7 us
    all_to_all x1, starting transfers between devices, body(): by_z = lax.all_to_all(taps, 'z', 0, 0, tiled=True)  9.6 us
    all_to_all x1, starting transfers between devices, body(): parts = lax.all_to_all(partial, FSDP, 0, 0, tiled=True)  8.86 us
    ppermute x1, starting transfers between devices, body(): other = lax.ppermute(act, 'yh', swap)  7.85 us
    all_to_all x1, waiting for transfers between devices, body(): lax.all_to_all(jnp.broadcast_to(pair[None], (n_x,) + pair.shape), 'x', 0,...  4.74 us
  transfers between devices with their start and end apart: 5, of which 4 were waited for; matrix products, arithmetic and copies ran while one was open for 5% of the time, Pallas kernels for 3%

profile of v1, /device:TPU:6, one launch (start us, length us, event | category | flops | bytes accessed | tf_op | source)
XLA Modules:
  0.0 156.7 jit_solution(12053037765113709977)
XLA Ops:
  0.6 1.9 %norm.1 = (bf16[40,1024]{1,0:T(8,128)(2,1)}, f32[40,1024]{1,0:T(8,128)}, f32[40,1024]{1,0:T(8,128)}, f32[8,128]{1,0:T(8,128)}) custom-call(f32[40,1024]{1,0:T(8,128)} %x_ref.3, f32[1,40]{1,0:T(1,128)} %bitcast.22, f32[1,40]{1,0:T(1,128)} %bitcast.24), custom_call_target="tpu_custom_call" | custom-call | tf_op jit(solution)/shard_map/norm/pallas_call | solution.py:99
  2.5 7.9 %collective-permute-start = (bf16[40,1024]{1,0:T(8,128)(2,1)}, bf16[40,1024]{1,0:T(8,128)(2,1)S(1)}, u32[]{:S(2)}, u32[]{:S(2)}) collective-permute-start(bf16[40,1024]{1,0:T(8,128)(2,1)} %get-tuple-element.19), channel_id=1, source_target_pairs={{0,2},{2,0},{1,3},{3,1},{4,6},{6,4},{5,7},{7,5},{8,10},{10,8},{9,1... | collective-permute-start | bytes 245768 | tf_op jit(solution)/shard_map/act_yh/ppermute | solution.py:114
  10.4 1.2 convert_element_type.21
  11.7 2.2 %nine.1 = bf16[384,1024]{1,0:T(8,128)(2,1)} custom-call(f32[40,1024]{1,0:T(8,128)} %grad_ref.1), custom_call_target="tpu_custom_call" | custom-call | tf_op jit(solution)/shard_map/nine/pallas_call | solution.py:108
  13.9 0.5 collective-permute-done
  14.4 0.9 broadcast_in_dim.83
  15.4 11.7 %all-to-all-start = ((bf16[4,2,40,1024]{3,2,1,0:T(8,128)(2,1)}), bf16[4,2,40,1024]{3,2,1,0:T(8,128)(2,1)S(1)}, u32[]{:S(2)}, u32[]{:S(2)}) async-start(bf16[4,2,40,1024]{3,2,1,0:T(8,128)(2,1)} %broadcast_in_dim.83), calls=%async_computation | async-start | bytes 1310720 | tf_op jit(solution)/shard_map/act_x/all_to_all | solution.py:119
  27.0 2.0 %convolution_convert_fusion = bf16[640,1024]{1,0:T(8,128)(2,1)} fusion(bf16[360,640]{1,0:T(8,128)(2,1)S(1)} %bitcast.18, bf16[384,1024]{1,0:T(8,128)(2,1)S(1)} %copy-done.5), kind=kOutput, calls=%fused_computation | convolution fusion | flops 472514560 | bytes 2508800 | tf_op jit(solution)/shard_map/dot_general | solution.py:122
  29.0 4.7 %all-to-all-done = bf16[4,2,40,1024]{3,2,1,0:T(8,128)(2,1)S(1)} async-done(((bf16[4,2,40,1024]{3,2,1,0:T(8,128)(2,1)}), bf16[4,2,40,1024]{3,2,1,0:T(8,128)(2,1)S(1)}, u32[]{:S(2)}, u32[]{:S(2)}) %all-to-all-start) | async-done | bytes 655392 | tf_op jit(solution)/shard_map/act_x/all_to_all | solution.py:119
  33.8 1.9 %collective-permute-start.1 = (bf16[8,40,1024]{2,1,0:T(8,128)(2,1)S(1)}, bf16[8,40,1024]{2,1,0:T(8,128)(2,1)}, u32[]{:S(2)}, u32[]{:S(2)}) collective-permute-start(bf16[8,40,1024]{2,1,0:T(8,128)(2,1)S(1)} %bitcast.16), channel_id=1, source_target_pairs={{0,1},{1,0},{2,3},{3,2},{4,5},{5,4},{6,7},{7,6},{8,9},{9,8},{10,11... | collective-permute-start | bytes 1966088 | tf_op jit(solution)/shard_map/act_c/ppermute | solution.py:130
  35.9 2.0 %collective-permute-done.1 = bf16[8,40,1024]{2,1,0:T(8,128)(2,1)} collective-permute-done((bf16[8,40,1024]{2,1,0:T(8,128)(2,1)S(1)}, bf16[8,40,1024]{2,1,0:T(8,128)(2,1)}, u32[]{:S(2)}, u32[]{:S(2)}) %collective-permute-start.1) | collective-permute-done | bytes 655392 | tf_op jit(solution)/shard_map/act_c/ppermute | solution.py:130
  37.9 1.2 bitcast_select_fusion.act_ref
  39.1 1.6 %convolution_convert_fusion.1 = bf16[384,640]{1,0:T(8,128)(2,1)} fusion(bf16[384,1024]{1,0:T(8,128)(2,1)S(1)} %copy-done.5, bf16[640,1024]{1,0:T(8,128)(2,1)S(1)} %bitcast_select_fusion.act_ref), kind=kOutput, calls=%fused_computation.5 | convolution fusion | flops 503562240 | bytes 2588672 | tf_op jit(solution)/shard_map/dot_general | solution.py:135
  40.7 9.6 %all-to-all-start.1 = ((bf16[12,32,640]{2,1,0:T(8,128)(2,1)}), bf16[12,32,640]{2,1,0:T(8,128)(2,1)S(1)}, u32[]{:S(2)}, u32[]{:S(2)}) async-start(bf16[12,32,640]{2,1,0:T(8,128)(2,1)} %bitcast.7), calls=%async_computation.1 | async-start | bytes 983040 | tf_op jit(solution)/shard_map/grad_z/all_to_all | solution.py:140
  50.3 3.0 %forward.1 = f32[40,1024]{1,0:T(8,128)} custom-call(bf16[360,640]{1,0:T(8,128)(2,1)} %bitcast.19, bf16[640,1024]{1,0:T(8,128)(2,1)} %copy-done.1, f32[40,1024]{1,0:T(8,128)} %x_ref.3), custom_call_target="tpu_custom_call" | custom-call | tf_op jit(solution)/shard_map/forward/pallas_call | solution.py:142
  53.4 19.8 %all-to-all-done.1 = bf16[12,32,640]{2,1,0:T(8,128)(2,1)S(1)} async-done(((bf16[12,32,640]{2,1,0:T(8,128)(2,1)}), bf16[12,32,640]{2,1,0:T(8,128)(2,1)S(1)}, u32[]{:S(2)}, u32[]{:S(2)}) %all-to-all-start.1) | async-done | bytes 491552 | tf_op jit(solution)/shard_map/grad_z/all_to_all | solution.py:140
  73.1 8.9 %all-to-all-start.2 = ((bf16[16,40,1024]{2,1,0:T(8,128)(2,1)}), bf16[16,40,1024]{2,1,0:T(8,128)(2,1)S(1)}, u32[]{:S(2)}, u32[]{:S(2)}) async-start(bf16[16,40,1024]{2,1,0:T(8,128)(2,1)} %bitcast.3), calls=%async_computation.2 | async-start | bytes 2621440 | tf_op jit(solution)/shard_map/back_f/all_to_all | solution.py:147
  82.1 41.3 %all-gather = f32[128,640]{1,0:T(8,128)S(1)} all-gather(f32[32,640]{1,0:T(8,128)S(1)} %convert_reduce_fusion), channel_id=2, replica_groups=mesh['z'=12,'yl'=4,'x'=4,'yh'=2,'c'=2] {'yl'}, dimensions={0}, use_global_device_ids=true | all-gather | bytes 409600 | tf_op jit(solution)/shard_map/gather_yl/all_gather | solution.py:151
  123.4 0.7 reduce_sum.19
  124.0 0.9 multiply_convert_fusion
  124.9 24.9 %all_gather.11 = bf16[384,640]{1,0:T(8,128)(2,1)S(1)} all-gather(bf16[32,640]{1,0:T(8,128)(2,1)S(1)} %multiply_convert_fusion), channel_id=1, replica_groups=mesh['z'=12,'yl'=4,'x'=4,'yh'=2,'c'=2] {'z'}, dimensions={0}, use_global_device_ids=true | all-gather | bytes 532480 | tf_op jit(solution)/shard_map/gather_z/all_gather | solution.py:154
  149.9 3.1 %divide_subtract_fusion = (f32[9,40,640]{2,1,0:T(8,128)}, f32[9,40,640]{2,1,0:T(8,128)}, f32[9,40,640]{2,1,0:T(8,128)}) fusion(f32[9,40,640]{2,1,0:T(8,128)S(1)} %copy-done.2, bf16[9,40,640]{2,1,0:T(8,128)(2,1)S(1)} %bitcast.20, f32[9,40,640]{2,1,0:T(8,128)S(1)} %copy-done.4, f32[9,40,640]{2,1,0:T(8,128)} %param.12), kind=kLoop, calls=%fused_computation.9 | loop fusion | flops 2995200 | bytes 5990400 | tf_op jit(solution)/shard_map/sub | solution.py:159
  153.0 1.1 copy-done
  154.1 2.6 %back.1 = f32[40,1024]{1,0:T(8,128)} custom-call(bf16[16,40,1024]{2,1,0:T(8,128)(2,1)} %copy-done, f32[40,1024]{1,0:T(8,128)} %get-tuple-element.29.normed_ref, f32[40,1024]{1,0:T(8,128)} %get-tuple-element.30.pre_ref, f32[8,128]{1,0:T(8,128)} %get-tuple-element.31.inv_ref, f32[1,40]{1,0:T(1,128)} %bitcast.23, f32[40,1024]{1,0:T(8,128)} %grad_ref.1), custom_call_target="tpu_custom_call" | custom-call | tf_op jit(solution)/shard_map/back/pallas_call | solution.py:163
  (21 shorter events, 0.4 us)
Async XLA Ops:
  2.5 11.8 %copy-start.6 = (bf16[40,1024]{1,0:T(8,128)(2,1)S(1)}, bf16[40,1024]{1,0:T(8,128)(2,1)}, u32[]{:S(2)}) copy-start(bf16[40,1024]{1,0:T(8,128)(2,1)} %get-tuple-element.19) | copy-start | bytes 245764
  2.5 11.8 %collective-permute-start = (bf16[40,1024]{1,0:T(8,128)(2,1)}, bf16[40,1024]{1,0:T(8,128)(2,1)S(1)}, u32[]{:S(2)}, u32[]{:S(2)}) collective-permute-start(bf16[40,1024]{1,0:T(8,128)(2,1)} %get-tuple-element.19), channel_id=1, source_target_pairs={{0,2},{2,0},{1,3},{3,1},{4,6},{6,4},{5,7},{7,5},{8,10},{10,8},{9,1... | collective-permute-start | bytes 245768 | tf_op jit(solution)/shard_map/act_yh/ppermute | solution.py:114
  11.7 15.4 %copy-start.3 = (bf16[9,40,640]{2,1,0:T(8,128)(2,1)}, bf16[9,40,640]{2,1,0:T(8,128)(2,1)S(1)}, u32[]{:S(2)}) copy-start(bf16[9,40,640]{2,1,0:T(8,128)(2,1)S(1)} %convert_element_type.21) | copy-start | bytes 1382404
  13.9 13.2 %copy-start.5 = (bf16[384,1024]{1,0:T(8,128)(2,1)S(1)}, bf16[384,1024]{1,0:T(8,128)(2,1)}, u32[]{:S(2)}) copy-start(bf16[384,1024]{1,0:T(8,128)(2,1)} %nine.1) | copy-start | bytes 2359300
  15.4 18.4 %all-to-all-start = ((bf16[4,2,40,1024]{3,2,1,0:T(8,128)(2,1)}), bf16[4,2,40,1024]{3,2,1,0:T(8,128)(2,1)S(1)}, u32[]{:S(2)}, u32[]{:S(2)}) async-start(bf16[4,2,40,1024]{3,2,1,0:T(8,128)(2,1)} %broadcast_in_dim.83), calls=%async_computation | async-start | bytes 1310720 | tf_op jit(solution)/shard_map/act_x/all_to_all | solution.py:119
  33.8 4.1 %collective-permute-start.1 = (bf16[8,40,1024]{2,1,0:T(8,128)(2,1)S(1)}, bf16[8,40,1024]{2,1,0:T(8,128)(2,1)}, u32[]{:S(2)}, u32[]{:S(2)}) collective-permute-start(bf16[8,40,1024]{2,1,0:T(8,128)(2,1)S(1)} %bitcast.16), channel_id=1, source_target_pairs={{0,1},{1,0},{2,3},{3,2},{4,5},{5,4},{6,7},{7,6},{8,9},{9,8},{10,11... | collective-permute-start | bytes 1966088 | tf_op jit(solution)/shard_map/act_c/ppermute | solution.py:130
  39.1 1.6 %copy-start.1 = (bf16[640,1024]{1,0:T(8,128)(2,1)}, bf16[640,1024]{1,0:T(8,128)(2,1)S(1)}, u32[]{:S(2)}) copy-start(bf16[640,1024]{1,0:T(8,128)(2,1)S(1)} %bitcast_select_fusion.act_ref) | copy-start | bytes 3932164
  40.7 32.4 %all-to-all-start.1 = ((bf16[12,32,640]{2,1,0:T(8,128)(2,1)}), bf16[12,32,640]{2,1,0:T(8,128)(2,1)S(1)}, u32[]{:S(2)}, u32[]{:S(2)}) async-start(bf16[12,32,640]{2,1,0:T(8,128)(2,1)} %bitcast.7), calls=%async_computation.1 | async-start | bytes 983040 | tf_op jit(solution)/shard_map/grad_z/all_to_all | solution.py:140
  73.1 79.9 %all-to-all-start.2 = ((bf16[16,40,1024]{2,1,0:T(8,128)(2,1)}), bf16[16,40,1024]{2,1,0:T(8,128)(2,1)S(1)}, u32[]{:S(2)}, u32[]{:S(2)}) async-start(bf16[16,40,1024]{2,1,0:T(8,128)(2,1)} %bitcast.3), calls=%async_computation.2 | async-start | bytes 2621440 | tf_op jit(solution)/shard_map/back_f/all_to_all | solution.py:147
  82.1 67.8 %copy-start.2 = (f32[9,40,640]{2,1,0:T(8,128)S(1)}, f32[9,40,640]{2,1,0:T(8,128)}, u32[]{:S(2)}) copy-start(f32[9,40,640]{2,1,0:T(8,128)} %param.10) | copy-start | bytes 2764804
  82.1 67.8 %copy-start.4 = (f32[9,40,640]{2,1,0:T(8,128)S(1)}, f32[9,40,640]{2,1,0:T(8,128)}, u32[]{:S(2)}) copy-start(f32[9,40,640]{2,1,0:T(8,128)} %param.11) | copy-start | bytes 2764804
  153.0 1.1 copy-start

commit v2 on v1

--- a/solution.py
+++ b/solution.py
@@ -5,9 +5,7 @@
 from jax.experimental.pallas import tpu as pltpu
 from jax.sharding import Mesh, PartitionSpec as P
 
-GROUP_CH = 40
 SIDE = 32
-ROWS_PAD = 32
 
 EPS_NORM = 1e-05
 BETA_ONE = 0.9
@@ -20,6 +18,7 @@
 
 DP = ("z", "yl")
 FSDP = ("x", "yh", "c")
+XY = ("x", "yh")
 
 
 def shifted(source, a, b):
@@ -51,7 +50,9 @@
     normed_ref[...] = normed
     pre_ref[...] = pre
     inv_ref[...] = jnp.broadcast_to(inv, inv_ref.shape)
-    act_ref[...] = (pre * jax.nn.sigmoid(pre)).astype(jnp.bfloat16)
+    act = (pre * jax.nn.sigmoid(pre)).astype(jnp.bfloat16)
+    for copy in range(act_ref.shape[0]):
+        act_ref[copy] = act
 
 
 def nine_kernel(g_ref, out_ref):
@@ -83,11 +84,11 @@
     out_ref[...] = grad_ref[...] + inv_ref[0:1, 0:1] * (gn - first - normed * second)
 
 
-def body(inputs, norm_gain, norm_bias, conv_weight, moment_one, moment_two, out_grad):
+def step(inputs, norm_gain, norm_bias, conv_weight, moment_one, moment_two, out_grad):
     local_ch, width = inputs.shape
     n_fsdp = lax.axis_size(FSDP)
-    n_z, n_yl, n_x = lax.axis_size("z"), lax.axis_size("yl"), lax.axis_size("x")
-    n_dp = n_z * n_yl
+    n_z, n_yl = lax.axis_size("z"), lax.axis_size("yl")
+    n_dp, n_xy = n_z * n_yl, lax.axis_size(XY)
     all_ch = local_ch * n_fsdp
     f32, bf16 = jnp.float32, jnp.bfloat16
     chunk_rows = -(-(9 * local_ch) // (8 * n_z)) * 8
@@ -99,7 +100,7 @@
     act, normed, pre_act, inv = pl.pallas_call(
         norm_kernel,
         out_shape=(
-            jax.ShapeDtypeStruct((local_ch, width), bf16), tile, tile,
+            jax.ShapeDtypeStruct((n_xy, local_ch, width), bf16), tile, tile,
             jax.ShapeDtypeStruct((8, 128), f32),
         ),
         name="norm",
@@ -110,48 +111,38 @@
     )(out_grad)
     weight_nine = conv_weight.astype(bf16).reshape(9 * local_ch, all_ch)
 
-    with jax.named_scope("act_yh"):
-        other = lax.ppermute(act, "yh", swap)
-    other, grad_rows, weight_nine = lax.optimization_barrier((other, grad_rows, weight_nine))
-    mine = jnp.arange(2) == lax.axis_index("yh")
-    pair = jnp.where(mine[:, None, None], act[None], other[None])
-    with jax.named_scope("act_x"):
-        by_x = lax.all_to_all(
-            jnp.broadcast_to(pair[None], (n_x,) + pair.shape), "x", 0, 0, tiled=True
-        )
+    by_xy = lax.all_to_all(act, XY, 0, 0, tiled=True)
     partial = lax.dot_general(
         weight_nine, grad_rows[: 9 * local_ch], (((0,), (0,)), ((), ())),
         preferred_element_type=f32,
-    )
-    partial = partial.astype(bf16).reshape(n_fsdp, local_ch, width)
-    by_x, partial = lax.optimization_barrier((by_x, partial))
-    by_x = by_x.reshape(n_x * 2, local_ch, width)
-    with jax.named_scope("act_c"):
-        other = lax.ppermute(by_x, "c", swap)
-    mine = jnp.arange(2) == lax.axis_index("c")
-    gathered = jnp.where(mine[None, :, None, None], by_x[:, None], other[:, None])
+    ).reshape(n_xy, 2, local_ch, width)
+    core = lax.axis_index("c")
+    keep = lax.dynamic_index_in_dim(partial, core, 1, keepdims=False)
+    give = lax.dynamic_index_in_dim(partial, 1 - core, 1, keepdims=False)
+    taken = lax.ppermute(give, "c", swap)
+    partial = (keep + taken).astype(bf16)
+    by_xy, partial = lax.optimization_barrier((by_xy, partial))
+    other = lax.ppermute(by_xy, "c", swap)
+    mine = jnp.arange(2) == core
+    gathered = jnp.where(mine[None, :, None, None], by_xy[:, None], other[:, None])
     gathered = gathered.reshape(all_ch, width)
 
     taps = lax.dot_general(
         grad_rows, gathered, (((1,), (1,)), ((), ())), preferred_element_type=f32
     )
     taps = taps.astype(bf16).reshape(n_z, chunk_rows, all_ch)
-    with jax.named_scope("grad_z"):
-        by_z = lax.all_to_all(taps, "z", 0, 0, tiled=True)
+    by_z = lax.all_to_all(taps, "z", 0, 0, tiled=True)
 
     block_out = pl.pallas_call(forward_kernel, out_shape=tile, name="forward")(
         weight_nine, gathered, inputs
     )
-    by_z, block_out, partial = lax.optimization_barrier((by_z, block_out, partial))
-    with jax.named_scope("back_f"):
-        parts = lax.all_to_all(partial, FSDP, 0, 0, tiled=True)
-
+    by_z, block_out = lax.optimization_barrier((by_z, block_out))
     z_sum = jnp.sum(by_z.astype(f32), axis=0)
-    with jax.named_scope("gather_yl"):
-        by_yl = lax.all_gather(z_sum, "yl", axis=0)
+    by_yl = lax.all_gather(z_sum, "yl", axis=0)
+    by_yl, partial = lax.optimization_barrier((by_yl, partial))
+    parts = lax.all_to_all(partial, XY, 0, 0, tiled=True)
     total = (jnp.sum(by_yl, axis=0) / n_dp).astype(bf16)
-    with jax.named_scope("gather_z"):
-        total = lax.all_gather(total, "z", axis=0, tiled=True)
+    total = lax.all_gather(total, "z", axis=0, tiled=True)
     gradient = total[: 9 * local_ch].reshape(9, local_ch, all_ch).astype(f32)
 
     first_new = BETA_ONE * moment_one + (1.0 - BETA_ONE) * gradient
@@ -170,7 +161,7 @@
     five = Mesh(mesh.devices.reshape(12, 4, 4, 2, 2), ("z", "yl", "x", "yh", "c"))
     act, chan, wgt = P(FSDP, DP), P(FSDP), P(None, FSDP, None)
     return jax.shard_map(
-        body,
+        step,
         mesh=five,
         in_specs=(act, chan, chan, wgt, wgt, wgt, act),
         out_specs=(act, act, wgt, wgt, wgt),

time: 157 us -> 139 us (0.89); the launches traced: 157 us -> 136 us
  blocking collectives: 66.2 us -> 40.8 us
  waiting for transfers between devices: 27 us -> 35.6 us
  starting transfers between devices: 39.9 us -> 36 us
    all_gather x2, blocking collectives: 66.2 us -> 40.8 us  [the longest x1 24.3 us: step(): total = lax.all_gather(total, 'z', axis=0, tiled=True)]
    all_to_all x3, waiting for transfers between devices: 24.5 us -> 33.7 us  [the longest x1 19.8 us: step(): by_z = lax.all_to_all(taps, 'z', 0, 0, tiled=True)]
    ppermute x2, starting transfers between devices: 9.76 us -> 3.82 us  [the longest x1 1.91 us: step(): taken = lax.ppermute(give, 'c', swap)]
    all_to_all x3, starting transfers between devices: 30.2 us -> 32.1 us  [the longest x1 13.4 us: step(): by_z = lax.all_to_all(taps, 'z', 0, 0, tiled=True)]
    convert_element_type x2 -> x3, other arithmetic: 2.13 us -> 3.58 us  [the longest x1 2.33 us: step(): partial = (keep + taken).astype(bf16)]
  transfers between devices with their start and end apart: 5 -> 5, of which waited for: 4 -> 3; matrix products, arithmetic and copies ran while one was open for 5% -> 4% of each run, Pallas kernels for 3% -> 4%
where the time goes in v2:
time: 139 us; the launch traced here: 136 us
  blocking collectives  40.8 us (29%)
  starting transfers between devices  36 us (26%)
  waiting for transfers between devices  35.6 us (26%)
  Pallas kernels  9.43 us (7%)
  other arithmetic  6.91 us (5%)
  matrix products  3.72 us (3%)
  local copies, waits for them, and re-layouts  3.25 us (2%)
    all_gather x1, blocking collectives, step(): total = lax.all_gather(total, 'z', axis=0, tiled=True)  24.3 us
    all_to_all x1, waiting for transfers between devices, step(): by_z = lax.all_to_all(taps, 'z', 0, 0, tiled=True)  19.8 us
    all_gather x1, blocking collectives, step(): by_yl = lax.all_gather(z_sum, 'yl', axis=0)  16.5 us
    all_to_all x1, waiting for transfers between devices, step(): by_xy = lax.all_to_all(act, XY, 0, 0, tiled=True)  13.9 us
    all_to_all x1, starting transfers between devices, step(): by_z = lax.all_to_all(taps, 'z', 0, 0, tiled=True)  13.4 us
    all_to_all x1, starting transfers between devices, step(): by_xy = lax.all_to_all(act, XY, 0, 0, tiled=True)  12.9 us
    all_to_all x1, starting transfers between devices, step(): parts = lax.all_to_all(partial, XY, 0, 0, tiled=True)  5.84 us
    sub x1, other arithmetic, step(): conv_weight - LEARN_RATE * (first_new / CORRECT_ONE) / (jnp.sqrt(second_n...  3.08 us
  transfers between devices with their start and end apart: 5, of which 3 were waited for; matrix products, arithmetic and copies ran while one was open for 4% of the time, Pallas kernels for 4%

profile of v2, /device:TPU:6, one launch (start us, length us, event | category | flops | bytes accessed | tf_op | source)
XLA Modules:
  0.0 136.4 jit_solution(6809737937835548657)
XLA Ops:
  0.6 1.2 convert_element_type.24
  1.9 1.0 copy.13
  2.9 2.0 %nine.1 = bf16[384,1024]{1,0:T(8,128)(2,1)} custom-call(f32[40,1024]{1,0:T(8,128)} %grad_ref.1), custom_call_target="tpu_custom_call" | custom-call | tf_op jit(solution)/shard_map/nine/pallas_call | solution.py:109
  4.9 2.1 %fusion.3 = f32[8,2,40,1024]{3,2,1,0:T(8,128)S(1)} fusion(bf16[8,2,40,360]{3,2,1,0:T(8,128)(2,1)} %bitcast.32, bf16[384,1024]{1,0:T(8,128)(2,1)} %nine.1), kind=kOutput, calls=%fused_computation.13 | convolution fusion | flops 471859200 | bytes 3850240 | tf_op jit(solution)/shard_map/dot_general | solution.py:115
  7.1 1.2 dynamic-slice_bitcast_fusion
  8.2 1.9 %collective-permute-start = (f32[8,40,1024]{2,1,0:T(8,128)}, f32[8,40,1024]{2,1,0:T(8,128)}, u32[]{:S(2)}, u32[]{:S(2)}) collective-permute-start(f32[8,40,1024]{2,1,0:T(8,128)} %dynamic-slice_bitcast_fusion), channel_id=1, source_target_pairs={{0,1},{1,0},{2,3},{3,2},{4,5},{5,4},{6,7},{7,6},{8,9},{9,8},{10,11... | collective-permute-start | bytes 3932168 | tf_op jit(solution)/shard_map/ppermute | solution.py:122
  10.1 2.1 %norm.1 = (bf16[8,40,1024]{2,1,0:T(8,128)(2,1)}, f32[40,1024]{1,0:T(8,128)}, f32[40,1024]{1,0:T(8,128)}, f32[8,128]{1,0:T(8,128)}) custom-call(f32[40,1024]{1,0:T(8,128)} %x_ref.3, f32[1,40]{1,0:T(1,128)} %bitcast.35, f32[1,40]{1,0:T(1,128)} %bitcast.37), custom_call_target="tpu_custom_call" | custom-call | tf_op jit(solution)/shard_map/norm/pallas_call | solution.py:100
  12.3 12.9 %all-to-all-start = ((bf16[8,40,1024]{2,1,0:T(8,128)(2,1)}), bf16[8,40,1024]{2,1,0:T(8,128)(2,1)S(1)}, u32[]{:S(2)}, u32[]{:S(2)}) async-start(bf16[8,40,1024]{2,1,0:T(8,128)(2,1)} %get-tuple-element.17), calls=%async_computation | async-start | bytes 1310720 | tf_op jit(solution)/shard_map/all_to_all | solution.py:114
  25.2 2.3 %fusion = bf16[8,40,1024]{2,1,0:T(8,128)(2,1)} fusion(f32[8,40,1024]{2,1,0:T(8,128)} %collective-permute-done, f32[8,2,40,1024]{3,2,1,0:T(8,128)S(1)} %fusion.3, s32[]{:T(128)S(6)} %select_n.12), kind=kLoop, calls=%fused_computation.5 | loop fusion | flops 655360 | bytes 3276804 | tf_op jit(solution)/shard_map/convert_element_type | solution.py:123
  27.5 13.9 %all-to-all-done = bf16[8,40,1024]{2,1,0:T(8,128)(2,1)S(1)} async-done(((bf16[8,40,1024]{2,1,0:T(8,128)(2,1)}), bf16[8,40,1024]{2,1,0:T(8,128)(2,1)S(1)}, u32[]{:S(2)}, u32[]{:S(2)}) %all-to-all-start) | async-done | bytes 655392 | tf_op jit(solution)/shard_map/all_to_all | solution.py:114
  41.5 1.9 %collective-permute-start.1 = (bf16[8,40,1024]{2,1,0:T(8,128)(2,1)S(1)}, bf16[8,40,1024]{2,1,0:T(8,128)(2,1)S(1)}, u32[]{:S(2)}, u32[]{:S(2)}) collective-permute-start(bf16[8,40,1024]{2,1,0:T(8,128)(2,1)S(1)} %all-to-all-done), channel_id=1, source_target_pairs={{0,1},{1,0},{2,3},{3,2},{4,5},{5,4},{6,7},{7,6},{8,9},{9,8},{10,11... | collective-permute-start | bytes 1966088 | tf_op jit(solution)/shard_map/ppermute | solution.py:125
  43.5 0.1 broadcast_in_dim.42
  43.6 1.9 %collective-permute-done.1 = bf16[8,40,1024]{2,1,0:T(8,128)(2,1)S(1)} collective-permute-done((bf16[8,40,1024]{2,1,0:T(8,128)(2,1)S(1)}, bf16[8,40,1024]{2,1,0:T(8,128)(2,1)S(1)}, u32[]{:S(2)}, u32[]{:S(2)}) %collective-permute-start.1) | collective-permute-done | bytes 655392 | tf_op jit(solution)/shard_map/ppermute | solution.py:125
  45.5 0.2 bitcast_select_fusion.act_ref
  45.6 1.6 %convolution_convert_fusion = bf16[640,384]{0,1:T(8,128)(2,1)} fusion(bf16[640,1024]{1,0:T(8,128)(2,1)S(1)} %bitcast_select_fusion.act_ref, bf16[384,1024]{1,0:T(8,128)(2,1)S(1)} %copy-done.3), kind=kOutput, calls=%fused_computation.7 | convolution fusion | flops 503562240 | bytes 2588672 | tf_op jit(solution)/shard_map/dot_general | solution.py:130
  47.2 13.4 %all-to-all-start.1 = ((bf16[12,32,640]{2,1,0:T(8,128)(2,1)}), bf16[12,32,640]{2,1,0:T(8,128)(2,1)S(1)}, u32[]{:S(2)}, u32[]{:S(2)}) async-start(bf16[12,32,640]{2,1,0:T(8,128)(2,1)} %bitcast.12), calls=%async_computation.1 | async-start | bytes 983040 | tf_op jit(solution)/shard_map/all_to_all | solution.py:134
  60.6 3.0 %forward.1 = f32[40,1024]{1,0:T(8,128)} custom-call(bf16[360,640]{1,0:T(8,128)(2,1)} %bitcast.31, bf16[640,1024]{1,0:T(8,128)(2,1)} %copy-done, f32[40,1024]{1,0:T(8,128)} %x_ref.3), custom_call_target="tpu_custom_call" | custom-call | tf_op jit(solution)/shard_map/forward/pallas_call | solution.py:136
  63.6 19.8 %all-to-all-done.1 = bf16[12,32,640]{2,1,0:T(8,128)(2,1)S(1)} async-done(((bf16[12,32,640]{2,1,0:T(8,128)(2,1)}), bf16[12,32,640]{2,1,0:T(8,128)(2,1)S(1)}, u32[]{:S(2)}, u32[]{:S(2)}) %all-to-all-start.1) | async-done | bytes 491552 | tf_op jit(solution)/shard_map/all_to_all | solution.py:134
  83.5 16.5 %all-gather = f32[128,640]{1,0:T(8,128)S(1)} all-gather(f32[32,640]{1,0:T(8,128)S(1)} %convert_reduce_fusion), channel_id=2, replica_groups=mesh['z'=12,'yl'=4,'x'=4,'yh'=2,'c'=2] {'yl'}, dimensions={0}, use_global_device_ids=true | all-gather | bytes 409600 | tf_op jit(solution)/shard_map/all_gather | solution.py:141
  100.0 5.8 %all-to-all-start.2 = ((bf16[8,40,1024]{2,1,0:T(8,128)(2,1)}), bf16[8,40,1024]{2,1,0:T(8,128)(2,1)S(1)}, u32[]{:S(2)}, u32[]{:S(2)}) async-start(bf16[8,40,1024]{2,1,0:T(8,128)(2,1)} %fusion), calls=%async_computation.2 | async-start | bytes 1310720 | tf_op jit(solution)/shard_map/all_to_all | solution.py:143
  105.9 24.3 %all_gather.11 = bf16[384,640]{1,0:T(8,128)(2,1)S(1)} all-gather(bf16[32,640]{1,0:T(8,128)(2,1)S(1)} %multiply_convert_fusion), channel_id=1, replica_groups=mesh['z'=12,'yl'=4,'x'=4,'yh'=2,'c'=2] {'z'}, dimensions={0}, use_global_device_ids=true | all-gather | bytes 532480 | tf_op jit(solution)/shard_map/all_gather | solution.py:145
  130.2 3.1 %divide_subtract_fusion = (f32[9,40,640]{2,1,0:T(8,128)}, f32[9,40,640]{2,1,0:T(8,128)}, f32[9,40,640]{2,1,0:T(8,128)}) fusion(f32[9,40,640]{2,1,0:T(8,128)S(1)} %copy-done.2, bf16[9,40,640]{2,1,0:T(8,128)(2,1)S(1)} %bitcast.33, f32[9,40,640]{2,1,0:T(8,128)S(1)} %copy-done.5, f32[9,40,640]{2,1,0:T(8,128)} %param.12), kind=kLoop, calls=%fused_computation.11 | loop fusion | flops 2995200 | bytes 5990400 | tf_op jit(solution)/shard_map/sub | solution.py:150
  133.3 0.8 copy-done.4
  134.1 2.2 %back.1 = f32[40,1024]{1,0:T(8,128)} custom-call(bf16[8,40,1024]{2,1,0:T(8,128)(2,1)} %copy-done.4, f32[40,1024]{1,0:T(8,128)} %get-tuple-element.25.normed_ref, f32[40,1024]{1,0:T(8,128)} %get-tuple-element.26.pre_ref, f32[8,128]{1,0:T(8,128)} %get-tuple-element.27.inv_ref, f32[1,40]{1,0:T(1,128)} %bitcast.36, f32[40,1024]{1,0:T(8,128)} %grad_ref.1), custom_call_target="tpu_custom_call" | custom-call | tf_op jit(solution)/shard_map/back/pallas_call | solution.py:154
  (19 shorter events, 0.3 us)
Async XLA Ops:
  1.9 5.2 %copy-start.1 = (bf16[9,40,640]{2,1,0:T(8,128)(2,1)}, bf16[9,40,640]{2,1,0:T(8,128)(2,1)S(1)}, u32[]{:S(2)}) copy-start(bf16[9,40,640]{2,1,0:T(8,128)(2,1)S(1)} %convert_element_type.24) | copy-start | bytes 1382404
  8.2 17.0 %collective-permute-start = (f32[8,40,1024]{2,1,0:T(8,128)}, f32[8,40,1024]{2,1,0:T(8,128)}, u32[]{:S(2)}, u32[]{:S(2)}) collective-permute-start(f32[8,40,1024]{2,1,0:T(8,128)} %dynamic-slice_bitcast_fusion), channel_id=1, source_target_pairs={{0,1},{1,0},{2,3},{3,2},{4,5},{5,4},{6,7},{7,6},{8,9},{9,8},{10,11... | collective-permute-start | bytes 3932168 | tf_op jit(solution)/shard_map/ppermute | solution.py:122
  12.3 29.2 %all-to-all-start = ((bf16[8,40,1024]{2,1,0:T(8,128)(2,1)}), bf16[8,40,1024]{2,1,0:T(8,128)(2,1)S(1)}, u32[]{:S(2)}, u32[]{:S(2)}) async-start(bf16[8,40,1024]{2,1,0:T(8,128)(2,1)} %get-tuple-element.17), calls=%async_computation | async-start | bytes 1310720 | tf_op jit(solution)/shard_map/all_to_all | solution.py:114
  41.5 4.0 %collective-permute-start.1 = (bf16[8,40,1024]{2,1,0:T(8,128)(2,1)S(1)}, bf16[8,40,1024]{2,1,0:T(8,128)(2,1)S(1)}, u32[]{:S(2)}, u32[]{:S(2)}) collective-permute-start(bf16[8,40,1024]{2,1,0:T(8,128)(2,1)S(1)} %all-to-all-done), channel_id=1, source_target_pairs={{0,1},{1,0},{2,3},{3,2},{4,5},{5,4},{6,7},{7,6},{8,9},{9,8},{10,11... | collective-permute-start | bytes 1966088 | tf_op jit(solution)/shard_map/ppermute | solution.py:125
  43.6 2.0 %copy-start.3 = (bf16[384,1024]{1,0:T(8,128)(2,1)S(1)}, bf16[384,1024]{1,0:T(8,128)(2,1)}, u32[]{:S(2)}) copy-start(bf16[384,1024]{1,0:T(8,128)(2,1)} %nine.1) | copy-start | bytes 2359300
  45.6 1.6 %copy-start = (bf16[640,1024]{1,0:T(8,128)(2,1)}, bf16[640,1024]{1,0:T(8,128)(2,1)S(1)}, u32[]{:S(2)}) copy-start(bf16[640,1024]{1,0:T(8,128)(2,1)S(1)} %bitcast_select_fusion.act_ref) | copy-start | bytes 3932164
  47.2 36.2 %all-to-all-start.1 = ((bf16[12,32,640]{2,1,0:T(8,128)(2,1)}), bf16[12,32,640]{2,1,0:T(8,128)(2,1)S(1)}, u32[]{:S(2)}, u32[]{:S(2)}) async-start(bf16[12,32,640]{2,1,0:T(8,128)(2,1)} %bitcast.12), calls=%async_computation.1 | async-start | bytes 983040 | tf_op jit(solution)/shard_map/all_to_all | solution.py:134
  100.0 33.3 %all-to-all-start.2 = ((bf16[8,40,1024]{2,1,0:T(8,128)(2,1)}), bf16[8,40,1024]{2,1,0:T(8,128)(2,1)S(1)}, u32[]{:S(2)}, u32[]{:S(2)}) async-start(bf16[8,40,1024]{2,1,0:T(8,128)(2,1)} %fusion), calls=%async_computation.2 | async-start | bytes 1310720 | tf_op jit(solution)/shard_map/all_to_all | solution.py:143
  105.8 24.4 %copy-start.2 = (f32[9,40,640]{2,1,0:T(8,128)S(1)}, f32[9,40,640]{2,1,0:T(8,128)}, u32[]{:S(2)}) copy-start(f32[9,40,640]{2,1,0:T(8,128)} %param.10) | copy-start | bytes 2764804
  105.8 24.4 %copy-start.5 = (f32[9,40,640]{2,1,0:T(8,128)S(1)}, f32[9,40,640]{2,1,0:T(8,128)}, u32[]{:S(2)}) copy-start(f32[9,40,640]{2,1,0:T(8,128)} %param.11) | copy-start | bytes 2764804
  133.3 0.8 copy-start.4

commit v3 on v2

--- a/solution.py
+++ b/solution.py
@@ -73,8 +73,8 @@
     out_ref[...] = total
 
 
-def back_kernel(parts_ref, normed_ref, pre_ref, inv_ref, gain_ref, grad_ref, out_ref):
-    grad_act = jnp.sum(parts_ref[...].astype(jnp.float32), axis=0)
+def back_kernel(keep_ref, taken_ref, normed_ref, pre_ref, inv_ref, gain_ref, grad_ref, out_ref):
+    grad_act = keep_ref[...].astype(jnp.float32) + taken_ref[...].astype(jnp.float32)
     pre, normed = pre_ref[...], normed_ref[...]
     s = jax.nn.sigmoid(pre)
     gn = grad_act * s * (1.0 + pre * (1.0 - s)) * column(gain_ref[...])
@@ -87,7 +87,7 @@
 def step(inputs, norm_gain, norm_bias, conv_weight, moment_one, moment_two, out_grad):
     local_ch, width = inputs.shape
     n_fsdp = lax.axis_size(FSDP)
-    n_z, n_yl = lax.axis_size("z"), lax.axis_size("yl")
+    n_z, n_yl, n_x = lax.axis_size("z"), lax.axis_size("yl"), lax.axis_size("x")
     n_dp, n_xy = n_z * n_yl, lax.axis_size(XY)
     all_ch = local_ch * n_fsdp
     f32, bf16 = jnp.float32, jnp.bfloat16
@@ -136,11 +136,27 @@
     block_out = pl.pallas_call(forward_kernel, out_shape=tile, name="forward")(
         weight_nine, gathered, inputs
     )
-    by_z, block_out = lax.optimization_barrier((by_z, block_out))
+    at = lax.axis_index("x")
+    by_chip = partial.reshape(n_x, 2, local_ch, width)
+    pick = lambda k: lax.dynamic_index_in_dim(by_chip, lax.rem(at + k, n_x), 0, keepdims=False)
+    moved = [
+        lax.ppermute(pick(k), "x", [(i, (i + k) % n_x) for i in range(n_x)])
+        for k in range(1, n_x)
+    ]
+    pair = sum((m.astype(f32) for m in moved), pick(0).astype(f32)).astype(bf16)
+    row = lax.axis_index("yh")
+    taken = lax.ppermute(
+        lax.dynamic_index_in_dim(pair, 1 - row, 0, keepdims=False), "yh", swap
+    )
+    keep = lax.dynamic_index_in_dim(pair, row, 0, keepdims=False)
+    input_grad = pl.pallas_call(back_kernel, out_shape=tile, name="back")(
+        keep, taken, normed, pre_act, inv, gain_row, out_grad
+    )
+
     z_sum = jnp.sum(by_z.astype(f32), axis=0)
-    by_yl = lax.all_gather(z_sum, "yl", axis=0)
-    by_yl, partial = lax.optimization_barrier((by_yl, partial))
-    parts = lax.all_to_all(partial, XY, 0, 0, tiled=True)
+    by_yl = lax.all_to_all(
+        jnp.broadcast_to(z_sum[None], (n_yl,) + z_sum.shape), "yl", 0, 0, tiled=True
+    )
     total = (jnp.sum(by_yl, axis=0) / n_dp).astype(bf16)
     total = lax.all_gather(total, "z", axis=0, tiled=True)
     gradient = total[: 9 * local_ch].reshape(9, local_ch, all_ch).astype(f32)
@@ -149,10 +165,6 @@
     second_new = BETA_TWO * moment_two + (1.0 - BETA_TWO) * gradient * gradient
     weight_new = conv_weight - LEARN_RATE * (first_new / CORRECT_ONE) / (
         jnp.sqrt(second_new / CORRECT_TWO) + EPS_ADAM
-    )
-    normed, weight_new = lax.optimization_barrier((normed, weight_new))
-    input_grad = pl.pallas_call(back_kernel, out_shape=tile, name="back")(
-        parts, normed, pre_act, inv, gain_row, out_grad
     )
     return (block_out, input_grad, weight_new, first_new, second_new)
 

time: 139 us -> 139 us (level)
  the two profiles are of different devices: /device:TPU:6 before, /device:TPU:16 now
where the time goes in v3:
time: 139 us; the launch traced here: 138 us
  starting transfers between devices  49 us (35%)
  waiting for transfers between devices  38 us (27%)
  blocking collectives  25.6 us (18%)
  Pallas kernels  9.25 us (7%)
  other arithmetic  6.99 us (5%)
  local copies, waits for them, and re-layouts  4.49 us (3%)
  matrix products  3.71 us (3%)
    all_gather x1, blocking collectives, step(): total = lax.all_gather(total, 'z', axis=0, tiled=True)  25.6 us
    all_to_all x1, starting transfers between devices, step(): by_z = lax.all_to_all(taps, 'z', 0, 0, tiled=True)  22.1 us
    all_to_all x1, waiting for transfers between devices, step(): by_xy = lax.all_to_all(act, XY, 0, 0, tiled=True)  13.9 us
    all_to_all x1, waiting for transfers between devices, step(): by_z = lax.all_to_all(taps, 'z', 0, 0, tiled=True)  13.5 us
    ppermute x3, starting transfers between devices, step(): lax.ppermute(pick(k), 'x', [(i, (i + k) % n_x) for i in range(n_x)])  9.21 us
    ppermute x1, waiting for transfers between devices, step(): lax.ppermute(lax.dynamic_index_in_dim(pair, 1 - row, 0, keepdims=False),...  8.68 us
    all_to_all x1, starting transfers between devices, step(): by_xy = lax.all_to_all(act, XY, 0, 0, tiled=True)  7.77 us
    all_to_all x1, starting transfers between devices, step(): lax.all_to_all(jnp.broadcast_to(z_sum[None], (n_yl,) + z_sum.shape), 'yl'...  4.19 us
  transfers between devices with their start and end apart: 9, of which 4 were waited for; matrix products, arithmetic and copies ran while one was open for 3% of the time, Pallas kernels for 5%

profile of v3, /device:TPU:16, one launch (start us, length us, event | category | flops | bytes accessed | tf_op | source)
XLA Modules:
  0.0 137.8 jit_solution(2841002462729104610)
XLA Ops:
  0.6 1.2 convert_element_type.42
  2.9 2.0 %nine.1 = bf16[384,1024]{1,0:T(8,128)(2,1)} custom-call(f32[40,1024]{1,0:T(8,128)} %grad_ref.1), custom_call_target="tpu_custom_call" | custom-call | tf_op jit(solution)/shard_map/nine/pallas_call | solution.py:109
  4.9 2.1 %fusion.3 = f32[8,2,40,1024]{3,2,1,0:T(8,128)S(1)} fusion(bf16[8,2,40,360]{3,2,1,0:T(8,128)(2,1)} %bitcast.47, bf16[384,1024]{1,0:T(8,128)(2,1)} %nine.1), kind=kOutput, calls=%fused_computation.13 | convolution fusion | flops 471859200 | bytes 3850240 | tf_op jit(solution)/shard_map/dot_general | solution.py:115
  7.0 1.2 dynamic-slice_bitcast_fusion
  8.2 1.9 %collective-permute-start = (f32[8,40,1024]{2,1,0:T(8,128)}, f32[8,40,1024]{2,1,0:T(8,128)}, u32[]{:S(2)}, u32[]{:S(2)}) collective-permute-start(f32[8,40,1024]{2,1,0:T(8,128)} %dynamic-slice_bitcast_fusion), channel_id=1, source_target_pairs={{0,1},{1,0},{2,3},{3,2},{4,5},{5,4},{6,7},{7,6},{8,9},{9,8},{10,11... | collective-permute-start | bytes 3932168 | tf_op jit(solution)/shard_map/ppermute | solution.py:122
  10.1 2.1 %norm.1 = (bf16[8,40,1024]{2,1,0:T(8,128)(2,1)}, f32[40,1024]{1,0:T(8,128)}, f32[40,1024]{1,0:T(8,128)}, f32[8,128]{1,0:T(8,128)}) custom-call(f32[40,1024]{1,0:T(8,128)} %x_ref.3, f32[1,40]{1,0:T(1,128)} %bitcast.49, f32[1,40]{1,0:T(1,128)} %bitcast.51), custom_call_target="tpu_custom_call" | custom-call | tf_op jit(solution)/shard_map/norm/pallas_call | solution.py:100
  12.3 7.8 %all-to-all-start = ((bf16[8,40,1024]{2,1,0:T(8,128)(2,1)}), bf16[8,40,1024]{2,1,0:T(8,128)(2,1)S(1)}, u32[]{:S(2)}, u32[]{:S(2)}) async-start(bf16[8,40,1024]{2,1,0:T(8,128)(2,1)} %get-tuple-element.11), calls=%async_computation | async-start | bytes 1310720 | tf_op jit(solution)/shard_map/all_to_all | solution.py:114
  20.0 2.3 %fusion = bf16[8,40,1024]{2,1,0:T(8,128)(2,1)} fusion(f32[8,40,1024]{2,1,0:T(8,128)} %collective-permute-done, f32[8,2,40,1024]{3,2,1,0:T(8,128)S(1)} %fusion.3, s32[]{:T(128)S(6)} %select_n.32), kind=kLoop, calls=%fused_computation.5 | loop fusion | flops 655360 | bytes 3276804 | tf_op jit(solution)/shard_map/convert_element_type | solution.py:123
  22.4 13.9 %all-to-all-done = bf16[8,40,1024]{2,1,0:T(8,128)(2,1)S(1)} async-done(((bf16[8,40,1024]{2,1,0:T(8,128)(2,1)}), bf16[8,40,1024]{2,1,0:T(8,128)(2,1)S(1)}, u32[]{:S(2)}, u32[]{:S(2)}) %all-to-all-start) | async-done | bytes 655392 | tf_op jit(solution)/shard_map/all_to_all | solution.py:114
  36.3 1.9 %collective-permute-start.1 = (bf16[8,40,1024]{2,1,0:T(8,128)(2,1)S(1)}, bf16[8,40,1024]{2,1,0:T(8,128)(2,1)S(1)}, u32[]{:S(2)}, u32[]{:S(2)}) collective-permute-start(bf16[8,40,1024]{2,1,0:T(8,128)(2,1)S(1)} %all-to-all-done), channel_id=1, source_target_pairs={{0,1},{1,0},{2,3},{3,2},{4,5},{5,4},{6,7},{7,6},{8,9},{9,8},{10,11... | collective-permute-start | bytes 1966088 | tf_op jit(solution)/shard_map/ppermute | solution.py:125
  38.4 1.9 %collective-permute-done.1 = bf16[8,40,1024]{2,1,0:T(8,128)(2,1)S(1)} collective-permute-done((bf16[8,40,1024]{2,1,0:T(8,128)(2,1)S(1)}, bf16[8,40,1024]{2,1,0:T(8,128)(2,1)S(1)}, u32[]{:S(2)}, u32[]{:S(2)}) %collective-permute-start.1) | collective-permute-done | bytes 655392 | tf_op jit(solution)/shard_map/ppermute | solution.py:125
  40.5 1.6 %convolution_convert_fusion = bf16[640,384]{0,1:T(8,128)(2,1)} fusion(bf16[640,1024]{1,0:T(8,128)(2,1)S(1)} %bitcast_select_fusion.act_ref, bf16[384,1024]{1,0:T(8,128)(2,1)S(1)} %copy-done.3), kind=kOutput, calls=%fused_computation.7 | convolution fusion | flops 503562240 | bytes 2588672 | tf_op jit(solution)/shard_map/dot_general | solution.py:130
  42.1 22.1 %all-to-all-start.1 = ((bf16[12,32,640]{2,1,0:T(8,128)(2,1)}), bf16[12,32,640]{2,1,0:T(8,128)(2,1)S(1)}, u32[]{:S(2)}, u32[]{:S(2)}) async-start(bf16[12,32,640]{2,1,0:T(8,128)(2,1)} %bitcast.19), calls=%async_computation.1 | async-start | bytes 983040 | tf_op jit(solution)/shard_map/all_to_all | solution.py:134
  64.3 1.9 %collective-permute-start.2 = (bf16[2,40,1024]{2,1,0:T(8,128)(2,1)S(1)}, bf16[2,40,1024]{2,1,0:T(8,128)(2,1)S(1)}, u32[]{:S(2)}, u32[]{:S(2)}) collective-permute-start(bf16[2,40,1024]{2,1,0:T(8,128)(2,1)S(1)} %get-tuple-element.20), channel_id=1, source_target_pairs={{0,4},{4,8},{8,12},{12,0},{1,5},{5,9},{9,13},{13,1},{2,6},{6,10},{... | collective-permute-start | bytes 491528 | tf_op jit(solution)/shard_map/ppermute | solution.py:143
  66.2 4.2 %collective-permute-start.3 = (bf16[2,40,1024]{2,1,0:T(8,128)(2,1)S(1)}, bf16[2,40,1024]{2,1,0:T(8,128)(2,1)S(1)}, u32[]{:S(2)}, u32[]{:S(2)}) collective-permute-start(bf16[2,40,1024]{2,1,0:T(8,128)(2,1)S(1)} %get-tuple-element.22), channel_id=1, source_target_pairs={{0,8},{4,12},{8,0},{12,4},{1,9},{5,13},{9,1},{13,5},{2,10},{6,14},... | collective-permute-start | bytes 491528 | tf_op jit(solution)/shard_map/ppermute | solution.py:143
  70.4 3.1 %collective-permute-start.4 = (bf16[2,40,1024]{2,1,0:T(8,128)(2,1)S(1)}, bf16[2,40,1024]{2,1,0:T(8,128)(2,1)S(1)}, u32[]{:S(2)}, u32[]{:S(2)}) collective-permute-start(bf16[2,40,1024]{2,1,0:T(8,128)(2,1)S(1)} %get-tuple-element.21), channel_id=1, source_target_pairs={{0,12},{4,0},{8,4},{12,8},{1,13},{5,1},{9,5},{13,9},{2,14},{6,2},{... | collective-permute-start | bytes 491528 | tf_op jit(solution)/shard_map/ppermute | solution.py:143
  73.5 13.5 %all-to-all-done.1 = bf16[12,32,640]{2,1,0:T(8,128)(2,1)S(1)} async-done(((bf16[12,32,640]{2,1,0:T(8,128)(2,1)}), bf16[12,32,640]{2,1,0:T(8,128)(2,1)S(1)}, u32[]{:S(2)}, u32[]{:S(2)}) %all-to-all-start.1) | async-done | bytes 491552 | tf_op jit(solution)/shard_map/all_to_all | solution.py:134
  87.8 4.2 %all-to-all-start.2 = ((f32[4,32,640]{2,1,0:T(8,128)}), f32[4,32,640]{2,1,0:T(8,128)S(1)}, u32[]{:S(2)}, u32[]{:S(2)}) async-start(f32[4,32,640]{2,1,0:T(8,128)} %broadcast_in_dim.56), calls=%async_computation.2 | async-start | bytes 655360 | tf_op jit(solution)/shard_map/all_to_all | solution.py:157
  92.8 1.9 %collective-permute-start.5 = (bf16[40,1024]{1,0:T(8,128)(2,1)S(1)}, bf16[40,1024]{1,0:T(8,128)(2,1)S(1)}, u32[]{:S(2)}, u32[]{:S(2)}) collective-permute-start(bf16[40,1024]{1,0:T(8,128)(2,1)S(1)} %get-tuple-element.23), channel_id=1, source_target_pairs={{0,2},{2,0},{1,3},{3,1},{4,6},{6,4},{5,7},{7,5},{8,10},{10,8},{9,1... | collective-permute-start | bytes 245768 | tf_op jit(solution)/shard_map/ppermute | solution.py:148
  94.7 8.7 %collective-permute-done.5.taken_ref = bf16[40,1024]{1,0:T(8,128)(2,1)S(1)} collective-permute-done((bf16[40,1024]{1,0:T(8,128)(2,1)S(1)}, bf16[40,1024]{1,0:T(8,128)(2,1)S(1)}, u32[]{:S(2)}, u32[]{:S(2)}) %collective-permute-start.5) | collective-permute-done | bytes 81952 | tf_op jit(solution)/shard_map/ppermute | solution.py:148
  104.0 2.1 %back.1 = f32[40,1024]{1,0:T(8,128)} custom-call(bf16[40,1024]{1,0:T(8,128)(2,1)} %get-tuple-element.24.keep_ref, bf16[40,1024]{1,0:T(8,128)(2,1)} %copy-done.6, f32[40,1024]{1,0:T(8,128)} %get-tuple-element.14.normed_ref, f32[40,1024]{1,0:T(8,128)} %get-tuple-element.15.pre_ref, f32[8,128]{1,0:T(8,128)} %get-tuple-element.16.inv_ref, f32[1,40]{1,0:T(1,128)} %bitcast.50, ...), custom_call_target="tpu_custom_call" | custom-call | tf_op jit(solution)/shard_map/back/pallas_call | solution.py:152
  106.1 3.0 %forward.1 = f32[40,1024]{1,0:T(8,128)} custom-call(bf16[360,640]{1,0:T(8,128)(2,1)} %bitcast.44, bf16[640,1024]{1,0:T(8,128)(2,1)} %copy-done, f32[40,1024]{1,0:T(8,128)} %x_ref.3), custom_call_target="tpu_custom_call" | custom-call | tf_op jit(solution)/shard_map/forward/pallas_call | solution.py:136
  109.1 25.6 %all_gather.3 = bf16[384,640]{1,0:T(8,128)(2,1)S(1)} all-gather(bf16[32,640]{1,0:T(8,128)(2,1)S(1)} %multiply_convert_fusion), channel_id=1, replica_groups=mesh['z'=12,'yl'=4,'x'=4,'yh'=2,'c'=2] {'z'}, dimensions={0}, use_global_device_ids=true | all-gather | bytes 532480 | tf_op jit(solution)/shard_map/all_gather | solution.py:161
  134.8 3.1 %divide_subtract_fusion = (f32[9,40,640]{2,1,0:T(8,128)}, f32[9,40,640]{2,1,0:T(8,128)}, f32[9,40,640]{2,1,0:T(8,128)}) fusion(f32[9,40,640]{2,1,0:T(8,128)S(1)} %copy-done.2, bf16[9,40,640]{2,1,0:T(8,128)(2,1)S(1)} %bitcast.48, f32[9,40,640]{2,1,0:T(8,128)S(1)} %copy-done.5, f32[9,40,640]{2,1,0:T(8,128)} %param.12), kind=kLoop, calls=%fused_computation.11 | loop fusion | flops 2995200 | bytes 5990400 | tf_op jit(solution)/shard_map/sub | solution.py:166
  (32 shorter events, 3.7 us)
Async XLA Ops:
  1.9 5.2 %copy-start.1 = (bf16[9,40,640]{2,1,0:T(8,128)(2,1)}, bf16[9,40,640]{2,1,0:T(8,128)(2,1)S(1)}, u32[]{:S(2)}) copy-start(bf16[9,40,640]{2,1,0:T(8,128)(2,1)S(1)} %convert_element_type.42) | copy-start | bytes 1382404
  8.2 11.8 %collective-permute-start = (f32[8,40,1024]{2,1,0:T(8,128)}, f32[8,40,1024]{2,1,0:T(8,128)}, u32[]{:S(2)}, u32[]{:S(2)}) collective-permute-start(f32[8,40,1024]{2,1,0:T(8,128)} %dynamic-slice_bitcast_fusion), channel_id=1, source_target_pairs={{0,1},{1,0},{2,3},{3,2},{4,5},{5,4},{6,7},{7,6},{8,9},{9,8},{10,11... | collective-permute-start | bytes 3932168 | tf_op jit(solution)/shard_map/ppermute | solution.py:122
  12.3 24.0 %all-to-all-start = ((bf16[8,40,1024]{2,1,0:T(8,128)(2,1)}), bf16[8,40,1024]{2,1,0:T(8,128)(2,1)S(1)}, u32[]{:S(2)}, u32[]{:S(2)}) async-start(bf16[8,40,1024]{2,1,0:T(8,128)(2,1)} %get-tuple-element.11), calls=%async_computation | async-start | bytes 1310720 | tf_op jit(solution)/shard_map/all_to_all | solution.py:114
  36.3 4.0 %collective-permute-start.1 = (bf16[8,40,1024]{2,1,0:T(8,128)(2,1)S(1)}, bf16[8,40,1024]{2,1,0:T(8,128)(2,1)S(1)}, u32[]{:S(2)}, u32[]{:S(2)}) collective-permute-start(bf16[8,40,1024]{2,1,0:T(8,128)(2,1)S(1)} %all-to-all-done), channel_id=1, source_target_pairs={{0,1},{1,0},{2,3},{3,2},{4,5},{5,4},{6,7},{7,6},{8,9},{9,8},{10,11... | collective-permute-start | bytes 1966088 | tf_op jit(solution)/shard_map/ppermute | solution.py:125
  38.4 2.0 %copy-start.3 = (bf16[384,1024]{1,0:T(8,128)(2,1)S(1)}, bf16[384,1024]{1,0:T(8,128)(2,1)}, u32[]{:S(2)}) copy-start(bf16[384,1024]{1,0:T(8,128)(2,1)} %nine.1) | copy-start | bytes 2359300
  40.5 1.6 %copy-start = (bf16[640,1024]{1,0:T(8,128)(2,1)}, bf16[640,1024]{1,0:T(8,128)(2,1)S(1)}, u32[]{:S(2)}) copy-start(bf16[640,1024]{1,0:T(8,128)(2,1)S(1)} %bitcast_select_fusion.act_ref) | copy-start | bytes 3932164
  42.1 22.1 %copy-start.4 = (bf16[8,40,1024]{2,1,0:T(8,128)(2,1)S(1)}, bf16[8,40,1024]{2,1,0:T(8,128)(2,1)}, u32[]{:S(2)}) copy-start(bf16[8,40,1024]{2,1,0:T(8,128)(2,1)} %fusion) | copy-start | bytes 1966084
  42.1 44.9 %all-to-all-start.1 = ((bf16[12,32,640]{2,1,0:T(8,128)(2,1)}), bf16[12,32,640]{2,1,0:T(8,128)(2,1)S(1)}, u32[]{:S(2)}, u32[]{:S(2)}) async-start(bf16[12,32,640]{2,1,0:T(8,128)(2,1)} %bitcast.19), calls=%async_computation.1 | async-start | bytes 983040 | tf_op jit(solution)/shard_map/all_to_all | solution.py:134
  64.3 27.7 %collective-permute-start.2 = (bf16[2,40,1024]{2,1,0:T(8,128)(2,1)S(1)}, bf16[2,40,1024]{2,1,0:T(8,128)(2,1)S(1)}, u32[]{:S(2)}, u32[]{:S(2)}) collective-permute-start(bf16[2,40,1024]{2,1,0:T(8,128)(2,1)S(1)} %get-tuple-element.20), channel_id=1, source_target_pairs={{0,4},{4,8},{8,12},{12,0},{1,5},{5,9},{9,13},{13,1},{2,6},{6,10},{... | collective-permute-start | bytes 491528 | tf_op jit(solution)/shard_map/ppermute | solution.py:143
  66.2 25.8 %collective-permute-start.3 = (bf16[2,40,1024]{2,1,0:T(8,128)(2,1)S(1)}, bf16[2,40,1024]{2,1,0:T(8,128)(2,1)S(1)}, u32[]{:S(2)}, u32[]{:S(2)}) collective-permute-start(bf16[2,40,1024]{2,1,0:T(8,128)(2,1)S(1)} %get-tuple-element.22), channel_id=1, source_target_pairs={{0,8},{4,12},{8,0},{12,4},{1,9},{5,13},{9,1},{13,5},{2,10},{6,14},... | collective-permute-start | bytes 491528 | tf_op jit(solution)/shard_map/ppermute | solution.py:143
  70.4 21.6 %collective-permute-start.4 = (bf16[2,40,1024]{2,1,0:T(8,128)(2,1)S(1)}, bf16[2,40,1024]{2,1,0:T(8,128)(2,1)S(1)}, u32[]{:S(2)}, u32[]{:S(2)}) collective-permute-start(bf16[2,40,1024]{2,1,0:T(8,128)(2,1)S(1)} %get-tuple-element.21), channel_id=1, source_target_pairs={{0,12},{4,0},{8,4},{12,8},{1,13},{5,1},{9,5},{13,9},{2,14},{6,2},{... | collective-permute-start | bytes 491528 | tf_op jit(solution)/shard_map/ppermute | solution.py:143
  87.8 21.3 %all-to-all-start.2 = ((f32[4,32,640]{2,1,0:T(8,128)}), f32[4,32,640]{2,1,0:T(8,128)S(1)}, u32[]{:S(2)}, u32[]{:S(2)}) async-start(f32[4,32,640]{2,1,0:T(8,128)} %broadcast_in_dim.56), calls=%async_computation.2 | async-start | bytes 655360 | tf_op jit(solution)/shard_map/all_to_all | solution.py:157
  92.8 10.6 %collective-permute-start.5 = (bf16[40,1024]{1,0:T(8,128)(2,1)S(1)}, bf16[40,1024]{1,0:T(8,128)(2,1)S(1)}, u32[]{:S(2)}, u32[]{:S(2)}) collective-permute-start(bf16[40,1024]{1,0:T(8,128)(2,1)S(1)} %get-tuple-element.23), channel_id=1, source_target_pairs={{0,2},{2,0},{1,3},{3,1},{4,6},{6,4},{5,7},{7,5},{8,10},{10,8},{9,1... | collective-permute-start | bytes 245768 | tf_op jit(solution)/shard_map/ppermute | solution.py:148
  103.4 0.6 copy-start.6
  109.1 25.7 %copy-start.2 = (f32[9,40,640]{2,1,0:T(8,128)S(1)}, f32[9,40,640]{2,1,0:T(8,128)}, u32[]{:S(2)}) copy-start(f32[9,40,640]{2,1,0:T(8,128)} %param.10) | copy-start | bytes 2764804
  109.1 25.7 %copy-start.5 = (f32[9,40,640]{2,1,0:T(8,128)S(1)}, f32[9,40,640]{2,1,0:T(8,128)}, u32[]{:S(2)}) copy-start(f32[9,40,640]{2,1,0:T(8,128)} %param.11) | copy-start | bytes 2764804

commit v4 on v3

--- a/solution.py
+++ b/solution.py
@@ -112,16 +112,15 @@
     weight_nine = conv_weight.astype(bf16).reshape(9 * local_ch, all_ch)
 
     by_xy = lax.all_to_all(act, XY, 0, 0, tiled=True)
+    core = lax.axis_index("c")
     partial = lax.dot_general(
         weight_nine, grad_rows[: 9 * local_ch], (((0,), (0,)), ((), ())),
         preferred_element_type=f32,
     ).reshape(n_xy, 2, local_ch, width)
-    core = lax.axis_index("c")
-    keep = lax.dynamic_index_in_dim(partial, core, 1, keepdims=False)
     give = lax.dynamic_index_in_dim(partial, 1 - core, 1, keepdims=False)
-    taken = lax.ppermute(give, "c", swap)
-    partial = (keep + taken).astype(bf16)
-    by_xy, partial = lax.optimization_barrier((by_xy, partial))
+    by_xy, partial, give, weight_nine = lax.optimization_barrier(
+        (by_xy, partial, give, weight_nine)
+    )
     other = lax.ppermute(by_xy, "c", swap)
     mine = jnp.arange(2) == core
     gathered = jnp.where(mine[None, :, None, None], by_xy[:, None], other[:, None])
@@ -136,6 +135,9 @@
     block_out = pl.pallas_call(forward_kernel, out_shape=tile, name="forward")(
         weight_nine, gathered, inputs
     )
+    keep = lax.dynamic_index_in_dim(partial, core, 1, keepdims=False)
+    taken = lax.ppermute(give, "c", swap)
+    partial = (keep + taken).astype(bf16)
     at = lax.axis_index("x")
     by_chip = partial.reshape(n_x, 2, local_ch, width)
     pick = lambda k: lax.dynamic_index_in_dim(by_chip, lax.rem(at + k, n_x), 0, keepdims=False)
@@ -158,8 +160,10 @@
         jnp.broadcast_to(z_sum[None], (n_yl,) + z_sum.shape), "yl", 0, 0, tiled=True
     )
     total = (jnp.sum(by_yl, axis=0) / n_dp).astype(bf16)
-    total = lax.all_gather(total, "z", axis=0, tiled=True)
-    gradient = total[: 9 * local_ch].reshape(9, local_ch, all_ch).astype(f32)
+    total = lax.all_to_all(
+        jnp.broadcast_to(total[None], (n_z,) + total.shape), "z", 0, 0, tiled=True
+    )
+    gradient = total.reshape(pad_rows, all_ch)[: 9 * local_ch].reshape(9, local_ch, all_ch).astype(f32)
 
     first_new = BETA_ONE * moment_one + (1.0 - BETA_ONE) * gradient
     second_new = BETA_TWO * moment_two + (1.0 - BETA_TWO) * gradient * gradient

time: 139 us -> 130 us (0.935)
  the two profiles are of different devices: /device:TPU:16 before, /device:TPU:6 now
where the time goes in v4:
time: 130 us; the launch traced here: 128 us
  starting transfers between devices  49.1 us (38%)
  waiting for transfers between devices  41.1 us (32%)
  blocking collectives  13.7 us (11%)
  Pallas kernels  9.46 us (7%)
  local copies, waits for them, and re-layouts  5.61 us (4%)
  other arithmetic  4.89 us (4%)
  matrix products  3.72 us (3%)
    all_to_all x1, waiting for transfers between devices, step(): by_z = lax.all_to_all(taps, 'z', 0, 0, tiled=True)  20.9 us
    all_to_all x1, starting transfers between devices, step(): by_z = lax.all_to_all(taps, 'z', 0, 0, tiled=True)  15.2 us
    all_to_all x1, blocking collectives, step(): lax.all_to_all(jnp.broadcast_to(z_sum[None], (n_yl,) + z_sum.shape), 'yl'...  13.7 us
    all_to_all x1, starting transfers between devices, step(): by_xy = lax.all_to_all(act, XY, 0, 0, tiled=True)  13.6 us
    ppermute x3, starting transfers between devices, step(): lax.ppermute(pick(k), 'x', [(i, (i + k) % n_x) for i in range(n_x)])  8.77 us
    all_to_all x1, waiting for transfers between devices, step(): by_xy = lax.all_to_all(act, XY, 0, 0, tiled=True)  6.88 us
    ppermute x3, waiting for transfers between devices, step(): lax.ppermute(pick(k), 'x', [(i, (i + k) % n_x) for i in range(n_x)])  6.3 us
    all_to_all x1, starting transfers between devices, step(): lax.all_to_all(jnp.broadcast_to(total[None], (n_z,) + total.shape), 'z',...  5.66 us
  transfers between devices with their start and end apart: 9, of which 7 were waited for; matrix products, arithmetic and copies ran while one was open for 6% of the time, Pallas kernels for 6%

profile of v4, /device:TPU:6, one launch (start us, length us, event | category | flops | bytes accessed | tf_op | source)
XLA Modules:
  0.0 128.4 jit_solution(16048861974437798282)
XLA Ops:
  0.6 2.2 %norm.1 = (bf16[8,40,1024]{2,1,0:T(8,128)(2,1)}, f32[40,1024]{1,0:T(8,128)}, f32[40,1024]{1,0:T(8,128)}, f32[8,128]{1,0:T(8,128)}) custom-call(f32[40,1024]{1,0:T(8,128)} %x_ref.3, f32[1,40]{1,0:T(1,128)} %bitcast.51, f32[1,40]{1,0:T(1,128)} %bitcast.53), custom_call_target="tpu_custom_call" | custom-call | tf_op jit(solution)/shard_map/norm/pallas_call | solution.py:100
  2.8 13.6 %all-to-all-start = ((bf16[8,40,1024]{2,1,0:T(8,128)(2,1)}), bf16[8,40,1024]{2,1,0:T(8,128)(2,1)}, u32[]{:S(2)}, u32[]{:S(2)}) async-start(bf16[8,40,1024]{2,1,0:T(8,128)(2,1)} %get-tuple-element.13), calls=%async_computation | async-start | bytes 1310720 | tf_op jit(solution)/shard_map/all_to_all | solution.py:114
  17.5 2.0 %nine.1 = bf16[384,1024]{1,0:T(8,128)(2,1)} custom-call(f32[40,1024]{1,0:T(8,128)} %grad_ref.1), custom_call_target="tpu_custom_call" | custom-call | tf_op jit(solution)/shard_map/nine/pallas_call | solution.py:109
  19.5 2.1 %fusion.3 = f32[8,2,40,1024]{3,2,1,0:T(8,128)S(1)} fusion(bf16[8,2,40,360]{3,2,1,0:T(8,128)(2,1)} %bitcast.48, bf16[384,1024]{1,0:T(8,128)(2,1)} %nine.1), kind=kOutput, calls=%fused_computation.13 | convolution fusion | flops 471859200 | bytes 3850240 | tf_op jit(solution)/shard_map/dot_general | solution.py:116
  22.8 6.9 %all-to-all-done = bf16[8,40,1024]{2,1,0:T(8,128)(2,1)} async-done(((bf16[8,40,1024]{2,1,0:T(8,128)(2,1)}), bf16[8,40,1024]{2,1,0:T(8,128)(2,1)}, u32[]{:S(2)}, u32[]{:S(2)}) %all-to-all-start) | async-done | bytes 655392 | tf_op jit(solution)/shard_map/all_to_all | solution.py:114
  29.7 1.9 %collective-permute-start = (bf16[8,40,1024]{2,1,0:T(8,128)(2,1)}, bf16[8,40,1024]{2,1,0:T(8,128)(2,1)S(1)}, u32[]{:S(2)}, u32[]{:S(2)}) collective-permute-start(bf16[8,40,1024]{2,1,0:T(8,128)(2,1)} %all-to-all-done), channel_id=1, source_target_pairs={{0,1},{1,0},{2,3},{3,2},{4,5},{5,4},{6,7},{7,6},{8,9},{9,8},{10,11... | collective-permute-start | bytes 1966088 | tf_op jit(solution)/shard_map/ppermute | solution.py:124
  31.8 2.1 %collective-permute-done = bf16[8,40,1024]{2,1,0:T(8,128)(2,1)S(1)} collective-permute-done((bf16[8,40,1024]{2,1,0:T(8,128)(2,1)}, bf16[8,40,1024]{2,1,0:T(8,128)(2,1)S(1)}, u32[]{:S(2)}, u32[]{:S(2)}) %collective-permute-start) | collective-permute-done | bytes 655392 | tf_op jit(solution)/shard_map/ppermute | solution.py:124
  35.2 1.6 %convolution_convert_fusion = bf16[640,384]{0,1:T(8,128)(2,1)} fusion(bf16[640,1024]{1,0:T(8,128)(2,1)S(1)} %bitcast_select_fusion.act_ref, bf16[384,1024]{1,0:T(8,128)(2,1)S(1)} %copy-done.4), kind=kOutput, calls=%fused_computation.7 | convolution fusion | flops 503562240 | bytes 2588672 | tf_op jit(solution)/shard_map/dot_general | solution.py:129
  36.8 15.2 %all-to-all-start.1 = ((bf16[12,32,640]{2,1,0:T(8,128)(2,1)}), bf16[12,32,640]{2,1,0:T(8,128)(2,1)S(1)}, u32[]{:S(2)}, u32[]{:S(2)}) async-start(bf16[12,32,640]{2,1,0:T(8,128)(2,1)} %bitcast.50), calls=%async_computation.1 | async-start | bytes 983040 | tf_op jit(solution)/shard_map/all_to_all | solution.py:133
  52.0 1.9 %collective-permute-start.1 = (f32[8,40,1024]{2,1,0:T(8,128)}, f32[8,40,1024]{2,1,0:T(8,128)}, u32[]{:S(2)}, u32[]{:S(2)}) collective-permute-start(f32[8,40,1024]{2,1,0:T(8,128)} %dynamic-slice_bitcast_fusion), channel_id=1, source_target_pairs={{0,1},{1,0},{2,3},{3,2},{4,5},{5,4},{6,7},{7,6},{8,9},{9,8},{10,11... | collective-permute-start | bytes 3932168 | tf_op jit(solution)/shard_map/ppermute | solution.py:139
  53.9 20.9 %all-to-all-done.1 = bf16[12,32,640]{2,1,0:T(8,128)(2,1)S(1)} async-done(((bf16[12,32,640]{2,1,0:T(8,128)(2,1)}), bf16[12,32,640]{2,1,0:T(8,128)(2,1)S(1)}, u32[]{:S(2)}, u32[]{:S(2)}) %all-to-all-start.1) | async-done | bytes 491552 | tf_op jit(solution)/shard_map/all_to_all | solution.py:133
  74.9 13.7 %all_to_all.20 = f32[4,32,640]{2,1,0:T(8,128)S(1)} all-to-all(f32[4,32,640]{2,1,0:T(8,128)S(1)} %broadcast_in_dim.62), channel_id=1, replica_groups=mesh['z'=12,'yl'=4,'x'=4,'yh'=2,'c'=2] {'yl'}, dimensions={0} | all-to-all | bytes 655360 | tf_op jit(solution)/shard_map/all_to_all | solution.py:159
  89.4 5.7 %all-to-all-start.3 = ((bf16[12,32,640]{2,1,0:T(8,128)(2,1)}), bf16[12,32,640]{2,1,0:T(8,128)(2,1)}, u32[]{:S(2)}, u32[]{:S(2)}) async-start(bf16[12,32,640]{2,1,0:T(8,128)(2,1)} %broadcast_in_dim.63), calls=%async_computation.3 | async-start | bytes 983040 | tf_op jit(solution)/shard_map/all_to_all | solution.py:163
  95.1 1.5 %fusion = bf16[8,40,1024]{2,1,0:T(8,128)(2,1)S(1)} fusion(f32[8,40,1024]{2,1,0:T(8,128)} %collective-permute-done.1, f32[8,2,40,1024]{3,2,1,0:T(8,128)S(1)} %fusion.3, s32[]{:T(128)S(6)} %select_n.34), kind=kLoop, calls=%fused_computation.4 | loop fusion | flops 655360 | bytes 3276804 | tf_op jit(solution)/shard_map/convert_element_type | solution.py:140
  96.6 4.1 %collective-permute-start.2 = (bf16[2,40,1024]{2,1,0:T(8,128)(2,1)S(1)}, bf16[2,40,1024]{2,1,0:T(8,128)(2,1)S(1)}, u32[]{:S(2)}, u32[]{:S(2)}) collective-permute-start(bf16[2,40,1024]{2,1,0:T(8,128)(2,1)S(1)} %get-tuple-element.24), channel_id=1, source_target_pairs={{0,4},{4,8},{8,12},{12,0},{1,5},{5,9},{9,13},{13,1},{2,6},{6,10},{... | collective-permute-start | bytes 491528 | tf_op jit(solution)/shard_map/ppermute | solution.py:145
  100.7 2.2 %collective-permute-start.3 = (bf16[2,40,1024]{2,1,0:T(8,128)(2,1)S(1)}, bf16[2,40,1024]{2,1,0:T(8,128)(2,1)S(1)}, u32[]{:S(2)}, u32[]{:S(2)}) collective-permute-start(bf16[2,40,1024]{2,1,0:T(8,128)(2,1)S(1)} %get-tuple-element.26), channel_id=1, source_target_pairs={{0,8},{4,12},{8,0},{12,4},{1,9},{5,13},{9,1},{13,5},{2,10},{6,14},... | collective-permute-start | bytes 491528 | tf_op jit(solution)/shard_map/ppermute | solution.py:145
  102.9 2.5 %collective-permute-start.4 = (bf16[2,40,1024]{2,1,0:T(8,128)(2,1)S(1)}, bf16[2,40,1024]{2,1,0:T(8,128)(2,1)S(1)}, u32[]{:S(2)}, u32[]{:S(2)}) collective-permute-start(bf16[2,40,1024]{2,1,0:T(8,128)(2,1)S(1)} %get-tuple-element.25), channel_id=1, source_target_pairs={{0,12},{4,0},{8,4},{12,8},{1,13},{5,1},{9,5},{13,9},{2,14},{6,2},{... | collective-permute-start | bytes 491528 | tf_op jit(solution)/shard_map/ppermute | solution.py:145
  106.6 3.4 %collective-permute-done.3 = bf16[2,40,1024]{2,1,0:T(8,128)(2,1)S(1)} collective-permute-done((bf16[2,40,1024]{2,1,0:T(8,128)(2,1)S(1)}, bf16[2,40,1024]{2,1,0:T(8,128)(2,1)S(1)}, u32[]{:S(2)}, u32[]{:S(2)}) %collective-permute-start.3) | collective-permute-done | bytes 163872 | tf_op jit(solution)/shard_map/ppermute | solution.py:145
  110.0 1.7 %collective-permute-done.4 = bf16[2,40,1024]{2,1,0:T(8,128)(2,1)S(1)} collective-permute-done((bf16[2,40,1024]{2,1,0:T(8,128)(2,1)S(1)}, bf16[2,40,1024]{2,1,0:T(8,128)(2,1)S(1)}, u32[]{:S(2)}, u32[]{:S(2)}) %collective-permute-start.4) | collective-permute-done | bytes 163872 | tf_op jit(solution)/shard_map/ppermute | solution.py:145
  112.5 2.1 %collective-permute-start.5 = (bf16[40,1024]{1,0:T(8,128)(2,1)S(1)}, bf16[40,1024]{1,0:T(8,128)(2,1)S(1)}, u32[]{:S(2)}, u32[]{:S(2)}) collective-permute-start(bf16[40,1024]{1,0:T(8,128)(2,1)S(1)} %get-tuple-element.27), channel_id=1, source_target_pairs={{0,2},{2,0},{1,3},{3,1},{4,6},{6,4},{5,7},{7,5},{8,10},{10,8},{9,1... | collective-permute-start | bytes 245768 | tf_op jit(solution)/shard_map/ppermute | solution.py:150
  114.6 3.1 %forward.1 = f32[40,1024]{1,0:T(8,128)} custom-call(bf16[360,640]{1,0:T(8,128)(2,1)} %bitcast.45, bf16[640,1024]{1,0:T(8,128)(2,1)} %copy-done, f32[40,1024]{1,0:T(8,128)} %x_ref.3), custom_call_target="tpu_custom_call" | custom-call | tf_op jit(solution)/shard_map/forward/pallas_call | solution.py:135
  117.8 5.0 %collective-permute-done.5.taken_ref = bf16[40,1024]{1,0:T(8,128)(2,1)S(1)} collective-permute-done((bf16[40,1024]{1,0:T(8,128)(2,1)S(1)}, bf16[40,1024]{1,0:T(8,128)(2,1)S(1)}, u32[]{:S(2)}, u32[]{:S(2)}) %collective-permute-start.5) | collective-permute-done | bytes 81952 | tf_op jit(solution)/shard_map/ppermute | solution.py:150
  123.4 2.1 %back.1 = f32[40,1024]{1,0:T(8,128)} custom-call(bf16[40,1024]{1,0:T(8,128)(2,1)} %get-tuple-element.28.keep_ref, bf16[40,1024]{1,0:T(8,128)(2,1)} %copy-done.7, f32[40,1024]{1,0:T(8,128)} %get-tuple-element.18.normed_ref, f32[40,1024]{1,0:T(8,128)} %get-tuple-element.19.pre_ref, f32[8,128]{1,0:T(8,128)} %get-tuple-element.20.inv_ref, f32[1,40]{1,0:T(1,128)} %bitcast.52, ...), custom_call_target="tpu_custom_call" | custom-call | tf_op jit(solution)/shard_map/back/pallas_call | solution.py:154
  126.5 1.9 %divide_subtract_fusion = (f32[9,40,640]{2,1,0:T(8,128)}, f32[9,40,640]{2,1,0:T(8,128)}, f32[9,40,640]{2,1,0:T(8,128)}) fusion(f32[9,40,640]{2,1,0:T(8,128)S(1)} %copy-done.3, bf16[9,40,640]{2,1,0:T(8,128)(2,1)S(1)} %bitcast.49, f32[9,40,640]{2,1,0:T(8,128)S(1)} %copy-done.5, f32[9,40,640]{2,1,0:T(8,128)S(1)} %copy-done.6), kind=kLoop, calls=%fused_computation.11 | loop fusion | flops 2995200 | bytes 5990400 | tf_op jit(solution)/shard_map/sub | solution.py:170
  (35 shorter events, 8.3 us)
Async XLA Ops:
  0.6 15.8 %copy-start.2 = (f32[9,40,640]{2,1,0:T(8,128)S(1)}, f32[9,40,640]{2,1,0:T(8,128)}, u32[]{:S(2)}) copy-start(f32[9,40,640]{2,1,0:T(8,128)} %param.10) | copy-start | bytes 2764804
  2.8 26.9 %all-to-all-start = ((bf16[8,40,1024]{2,1,0:T(8,128)(2,1)}), bf16[8,40,1024]{2,1,0:T(8,128)(2,1)}, u32[]{:S(2)}, u32[]{:S(2)}) async-start(bf16[8,40,1024]{2,1,0:T(8,128)(2,1)} %get-tuple-element.13), calls=%async_computation | async-start | bytes 1310720 | tf_op jit(solution)/shard_map/all_to_all | solution.py:114
  16.5 5.2 %copy-start.1 = (bf16[9,40,640]{2,1,0:T(8,128)(2,1)}, bf16[9,40,640]{2,1,0:T(8,128)(2,1)S(1)}, u32[]{:S(2)}) copy-start(bf16[9,40,640]{2,1,0:T(8,128)(2,1)S(1)} %convert_element_type.46) | copy-start | bytes 1382404
  29.7 4.2 %collective-permute-start = (bf16[8,40,1024]{2,1,0:T(8,128)(2,1)}, bf16[8,40,1024]{2,1,0:T(8,128)(2,1)S(1)}, u32[]{:S(2)}, u32[]{:S(2)}) collective-permute-start(bf16[8,40,1024]{2,1,0:T(8,128)(2,1)} %all-to-all-done), channel_id=1, source_target_pairs={{0,1},{1,0},{2,3},{3,2},{4,5},{5,4},{6,7},{7,6},{8,9},{9,8},{10,11... | collective-permute-start | bytes 1966088 | tf_op jit(solution)/shard_map/ppermute | solution.py:124
  31.8 3.3 %copy-start.4 = (bf16[384,1024]{1,0:T(8,128)(2,1)S(1)}, bf16[384,1024]{1,0:T(8,128)(2,1)}, u32[]{:S(2)}) copy-start(bf16[384,1024]{1,0:T(8,128)(2,1)} %nine.1) | copy-start | bytes 2359300
  35.2 1.6 %copy-start = (bf16[640,1024]{1,0:T(8,128)(2,1)}, bf16[640,1024]{1,0:T(8,128)(2,1)S(1)}, u32[]{:S(2)}) copy-start(bf16[640,1024]{1,0:T(8,128)(2,1)S(1)} %bitcast_select_fusion.act_ref) | copy-start | bytes 3932164
  36.8 38.0 %all-to-all-start.1 = ((bf16[12,32,640]{2,1,0:T(8,128)(2,1)}), bf16[12,32,640]{2,1,0:T(8,128)(2,1)S(1)}, u32[]{:S(2)}, u32[]{:S(2)}) async-start(bf16[12,32,640]{2,1,0:T(8,128)(2,1)} %bitcast.50), calls=%async_computation.1 | async-start | bytes 983040 | tf_op jit(solution)/shard_map/all_to_all | solution.py:133
  52.0 43.1 %collective-permute-start.1 = (f32[8,40,1024]{2,1,0:T(8,128)}, f32[8,40,1024]{2,1,0:T(8,128)}, u32[]{:S(2)}, u32[]{:S(2)}) collective-permute-start(f32[8,40,1024]{2,1,0:T(8,128)} %dynamic-slice_bitcast_fusion), channel_id=1, source_target_pairs={{0,1},{1,0},{2,3},{3,2},{4,5},{5,4},{6,7},{7,6},{8,9},{9,8},{10,11... | collective-permute-start | bytes 3932168 | tf_op jit(solution)/shard_map/ppermute | solution.py:139
  89.4 36.0 %all-to-all-start.3 = ((bf16[12,32,640]{2,1,0:T(8,128)(2,1)}), bf16[12,32,640]{2,1,0:T(8,128)(2,1)}, u32[]{:S(2)}, u32[]{:S(2)}) async-start(bf16[12,32,640]{2,1,0:T(8,128)(2,1)} %broadcast_in_dim.63), calls=%async_computation.3 | async-start | bytes 983040 | tf_op jit(solution)/shard_map/all_to_all | solution.py:163
  96.6 10.0 %collective-permute-start.2 = (bf16[2,40,1024]{2,1,0:T(8,128)(2,1)S(1)}, bf16[2,40,1024]{2,1,0:T(8,128)(2,1)S(1)}, u32[]{:S(2)}, u32[]{:S(2)}) collective-permute-start(bf16[2,40,1024]{2,1,0:T(8,128)(2,1)S(1)} %get-tuple-element.24), channel_id=1, source_target_pairs={{0,4},{4,8},{8,12},{12,0},{1,5},{5,9},{9,13},{13,1},{2,6},{6,10},{... | collective-permute-start | bytes 491528 | tf_op jit(solution)/shard_map/ppermute | solution.py:145
  100.7 9.3 %collective-permute-start.3 = (bf16[2,40,1024]{2,1,0:T(8,128)(2,1)S(1)}, bf16[2,40,1024]{2,1,0:T(8,128)(2,1)S(1)}, u32[]{:S(2)}, u32[]{:S(2)}) collective-permute-start(bf16[2,40,1024]{2,1,0:T(8,128)(2,1)S(1)} %get-tuple-element.26), channel_id=1, source_target_pairs={{0,8},{4,12},{8,0},{12,4},{1,9},{5,13},{9,1},{13,5},{2,10},{6,14},... | collective-permute-start | bytes 491528 | tf_op jit(solution)/shard_map/ppermute | solution.py:145
  102.9 8.9 %collective-permute-start.4 = (bf16[2,40,1024]{2,1,0:T(8,128)(2,1)S(1)}, bf16[2,40,1024]{2,1,0:T(8,128)(2,1)S(1)}, u32[]{:S(2)}, u32[]{:S(2)}) collective-permute-start(bf16[2,40,1024]{2,1,0:T(8,128)(2,1)S(1)} %get-tuple-element.25), channel_id=1, source_target_pairs={{0,12},{4,0},{8,4},{12,8},{1,13},{5,1},{9,5},{13,9},{2,14},{6,2},{... | collective-permute-start | bytes 491528 | tf_op jit(solution)/shard_map/ppermute | solution.py:145
  112.5 10.2 %collective-permute-start.5 = (bf16[40,1024]{1,0:T(8,128)(2,1)S(1)}, bf16[40,1024]{1,0:T(8,128)(2,1)S(1)}, u32[]{:S(2)}, u32[]{:S(2)}) collective-permute-start(bf16[40,1024]{1,0:T(8,128)(2,1)S(1)} %get-tuple-element.27), channel_id=1, source_target_pairs={{0,2},{2,0},{1,3},{3,1},{4,6},{6,4},{5,7},{7,5},{8,10},{10,8},{9,1... | collective-permute-start | bytes 245768 | tf_op jit(solution)/shard_map/ppermute | solution.py:150
  114.6 11.9 %copy-start.5 = (f32[9,40,640]{2,1,0:T(8,128)S(1)}, f32[9,40,640]{2,1,0:T(8,128)}, u32[]{:S(2)}) copy-start(f32[9,40,640]{2,1,0:T(8,128)} %param.11) | copy-start | bytes 2764804
  114.6 11.9 %copy-start.6 = (f32[9,40,640]{2,1,0:T(8,128)S(1)}, f32[9,40,640]{2,1,0:T(8,128)}, u32[]{:S(2)}) copy-start(f32[9,40,640]{2,1,0:T(8,128)} %param.12) | copy-start | bytes 2764804
  117.8 8.8 %copy-start.3 = (f32[9,40,640]{2,1,0:T(8,128)S(1)}, f32[9,40,640]{2,1,0:T(8,128)}, u32[]{:S(2)}) copy-start(f32[9,40,640]{2,1,0:T(8,128)} %param.10) | copy-start | bytes 2764804
  122.7 0.6 copy-start.7

commit v5 on v4

--- a/solution.py
+++ b/solution.py
@@ -1,3 +1,5 @@
+import functools
+
 import jax
 import jax.numpy as jnp
 from jax import lax
@@ -16,6 +18,7 @@
 EPS_ADAM = 1e-08
 OFFSETS = ((-1, -1), (-1, 0), (-1, 1), (0, -1), (0, 0), (0, 1), (1, -1), (1, 0), (1, 1))
 
+SMALL = pltpu.CompilerParams(vmem_limit_bytes=16 * 2**20)
 DP = ("z", "yl")
 FSDP = ("x", "yh", "c")
 XY = ("x", "yh")
@@ -73,6 +76,12 @@
     out_ref[...] = total
 
 
+def sum_copies_kernel(parts_ref, out_ref, *, scale):
+    total = (jnp.sum(parts_ref[...].astype(jnp.float32), axis=0) * scale).astype(out_ref.dtype)
+    for copy in range(out_ref.shape[0]):
+        out_ref[copy] = total
+
+
 def back_kernel(keep_ref, taken_ref, normed_ref, pre_ref, inv_ref, gain_ref, grad_ref, out_ref):
     grad_act = keep_ref[...].astype(jnp.float32) + taken_ref[...].astype(jnp.float32)
     pre, normed = pre_ref[...], normed_ref[...]
@@ -107,7 +116,7 @@
     )(inputs, gain_row, bias_row)
 
     grad_rows = pl.pallas_call(
-        nine_kernel, out_shape=jax.ShapeDtypeStruct((pad_rows, width), bf16), name="nine"
+        nine_kernel, out_shape=jax.ShapeDtypeStruct((pad_rows, width), bf16), name="nine", compiler_params=SMALL
     )(out_grad)
     weight_nine = conv_weight.astype(bf16).reshape(9 * local_ch, all_ch)
 
@@ -132,7 +141,7 @@
     taps = taps.astype(bf16).reshape(n_z, chunk_rows, all_ch)
     by_z = lax.all_to_all(taps, "z", 0, 0, tiled=True)
 
-    block_out = pl.pallas_call(forward_kernel, out_shape=tile, name="forward")(
+    block_out = pl.pallas_call(forward_kernel, out_shape=tile, name="forward", compiler_params=SMALL)(
         weight_nine, gathered, inputs
     )
     keep = lax.dynamic_index_in_dim(partial, core, 1, keepdims=False)
@@ -151,18 +160,22 @@
         lax.dynamic_index_in_dim(pair, 1 - row, 0, keepdims=False), "yh", swap
     )
     keep = lax.dynamic_index_in_dim(pair, row, 0, keepdims=False)
-    input_grad = pl.pallas_call(back_kernel, out_shape=tile, name="back")(
+    input_grad = pl.pallas_call(back_kernel, out_shape=tile, name="back", compiler_params=SMALL)(
         keep, taken, normed, pre_act, inv, gain_row, out_grad
     )
 
-    z_sum = jnp.sum(by_z.astype(f32), axis=0)
-    by_yl = lax.all_to_all(
-        jnp.broadcast_to(z_sum[None], (n_yl,) + z_sum.shape), "yl", 0, 0, tiled=True
-    )
-    total = (jnp.sum(by_yl, axis=0) / n_dp).astype(bf16)
-    total = lax.all_to_all(
-        jnp.broadcast_to(total[None], (n_z,) + total.shape), "z", 0, 0, tiled=True
-    )
+    z_sum = pl.pallas_call(
+        functools.partial(sum_copies_kernel, scale=1.0),
+        out_shape=jax.ShapeDtypeStruct((n_yl, chunk_rows, all_ch), f32),
+        name="sum_z", compiler_params=SMALL,
+    )(by_z)
+    by_yl = lax.all_to_all(z_sum, "yl", 0, 0, tiled=True)
+    total = pl.pallas_call(
+        functools.partial(sum_copies_kernel, scale=1.0 / n_dp),
+        out_shape=jax.ShapeDtypeStruct((n_z, chunk_rows, all_ch), bf16),
+        name="sum_yl", compiler_params=SMALL,
+    )(by_yl)
+    total = lax.all_to_all(total, "z", 0, 0, tiled=True)
     gradient = total.reshape(pad_rows, all_ch)[: 9 * local_ch].reshape(9, local_ch, all_ch).astype(f32)
 
     first_new = BETA_ONE * moment_one + (1.0 - BETA_ONE) * gradient

time: 130 us -> 130 us (level)
  waiting for transfers between devices: 41.1 us -> 45 us
  Pallas kernels: 9.46 us -> 5.82 us
  other arithmetic: 4.89 us -> 7.74 us
    all_to_all x1, waiting for transfers between devices: 6.88 us -> 9.15 us  [step(): by_xy = lax.all_to_all(act, XY, 0, 0, tiled=True)]
    pallas_call x2 -> x4, Pallas kernels: 5.21 us -> 3.38 us  [the longest x1 1.58 us: step(): pl.pallas_call(forward_kernel, out_shape=tile, name='forward', compiler_p...]
    pallas_call x1, Pallas kernels: 2.04 us -> 0.24 us  [step(): pl.pallas_call(nine_kernel, out_shape=jax.ShapeDtypeStruct((pad_rows, wid...]
    ppermute x1, waiting for transfers between devices: 4.97 us -> 6.56 us  [step(): lax.ppermute(lax.dynamic_index_in_dim(pair, 1 - row, 0, keepdims=False),...]
    unnamed x16 -> x18, local copies, waits for them, and re-layouts: 0.67 us -> 2.13 us
    sub x1, other arithmetic: 1.91 us -> 3.35 us  [step(): conv_weight - LEARN_RATE * (first_new / CORRECT_ONE) / (jnp.sqrt(second_n...]
  transfers between devices with their start and end apart: 9 -> 9, of which waited for: 7 -> 7; matrix products, arithmetic and copies ran while one was open for 6% -> 5% of each run, Pallas kernels for 6% -> 3%
where the time goes in v5:
time: 130 us; the launch traced here: 129 us
  starting transfers between devices  48.5 us (37%)
  waiting for transfers between devices  45 us (35%)
  blocking collectives  13.7 us (11%)
  other arithmetic  7.74 us (6%)
  Pallas kernels  5.82 us (4%)
  local copies, waits for them, and re-layouts  4.55 us (4%)
  matrix products  2.46 us (2%)
    all_to_all x1, waiting for transfers between devices, step(): by_z = lax.all_to_all(taps, 'z', 0, 0, tiled=True)  20.9 us
    all_to_all x1, starting transfers between devices, step(): by_z = lax.all_to_all(taps, 'z', 0, 0, tiled=True)  15.2 us
    all_to_all x1, blocking collectives, step(): by_yl = lax.all_to_all(z_sum, 'yl', 0, 0, tiled=True)  13.7 us
    all_to_all x1, starting transfers between devices, step(): by_xy = lax.all_to_all(act, XY, 0, 0, tiled=True)  12.9 us
    all_to_all x1, waiting for transfers between devices, step(): by_xy = lax.all_to_all(act, XY, 0, 0, tiled=True)  9.15 us
    ppermute x3, starting transfers between devices, step(): lax.ppermute(pick(k), 'x', [(i, (i + k) % n_x) for i in range(n_x)])  8.76 us
    ppermute x1, waiting for transfers between devices, step(): lax.ppermute(lax.dynamic_index_in_dim(pair, 1 - row, 0, keepdims=False),...  6.56 us
    ppermute x3, waiting for transfers between devices, step(): lax.ppermute(pick(k), 'x', [(i, (i + k) % n_x) for i in range(n_x)])  6.42 us
  transfers between devices with their start and end apart: 9, of which 7 were waited for; matrix products, arithmetic and copies ran while one was open for 5% of the time, Pallas kernels for 3%

profile of v5, /device:TPU:6, one launch (start us, length us, event | category | flops | bytes accessed | tf_op | source)
XLA Modules:
  0.0 128.7 jit_solution(11901350974285154610)
XLA Ops:
  0.6 2.2 %norm.1 = (bf16[8,40,1024]{2,1,0:T(8,128)(2,1)}, f32[40,1024]{1,0:T(8,128)}, f32[40,1024]{1,0:T(8,128)}, f32[8,128]{1,0:T(8,128)}) custom-call(f32[40,1024]{1,0:T(8,128)} %x_ref.3, f32[1,40]{1,0:T(1,128)} %bitcast.46, f32[1,40]{1,0:T(1,128)} %bitcast.53), custom_call_target="tpu_custom_call" | custom-call | tf_op jit(solution)/shard_map/norm/pallas_call | solution.py:109
  2.8 12.9 %all-to-all-start = ((bf16[8,40,1024]{2,1,0:T(8,128)(2,1)}), bf16[8,40,1024]{2,1,0:T(8,128)(2,1)S(1)}, u32[]{:S(2)}, u32[]{:S(2)}) async-start(bf16[8,40,1024]{2,1,0:T(8,128)(2,1)} %get-tuple-element.13), calls=%async_computation | async-start | bytes 1310720 | tf_op jit(solution)/shard_map/all_to_all | solution.py:123
  17.8 1.5 %copy-done.6 = f32[8,2,40,1024]{3,2,1,0:T(8,128)} copy-done((f32[8,2,40,1024]{3,2,1,0:T(8,128)}, f32[8,2,40,1024]{3,2,1,0:T(8,128)S(1)}, u32[]{:S(2)}) %copy-start.6) | copy-done | bytes 2621464
  20.5 9.1 %all-to-all-done = bf16[8,40,1024]{2,1,0:T(8,128)(2,1)S(1)} async-done(((bf16[8,40,1024]{2,1,0:T(8,128)(2,1)}), bf16[8,40,1024]{2,1,0:T(8,128)(2,1)S(1)}, u32[]{:S(2)}, u32[]{:S(2)}) %all-to-all-start) | async-done | bytes 655392 | tf_op jit(solution)/shard_map/all_to_all | solution.py:123
  29.6 1.9 %collective-permute-start = (bf16[8,40,1024]{2,1,0:T(8,128)(2,1)S(1)}, bf16[8,40,1024]{2,1,0:T(8,128)(2,1)}, u32[]{:S(2)}, u32[]{:S(2)}) collective-permute-start(bf16[8,40,1024]{2,1,0:T(8,128)(2,1)S(1)} %all-to-all-done), channel_id=1, source_target_pairs={{0,1},{1,0},{2,3},{3,2},{4,5},{5,4},{6,7},{7,6},{8,9},{9,8},{10,11... | collective-permute-start | bytes 1966088 | tf_op jit(solution)/shard_map/ppermute | solution.py:133
  31.7 2.0 %collective-permute-done = bf16[8,40,1024]{2,1,0:T(8,128)(2,1)} collective-permute-done((bf16[8,40,1024]{2,1,0:T(8,128)(2,1)S(1)}, bf16[8,40,1024]{2,1,0:T(8,128)(2,1)}, u32[]{:S(2)}, u32[]{:S(2)}) %collective-permute-start) | collective-permute-done | bytes 655392 | tf_op jit(solution)/shard_map/ppermute | solution.py:133
  33.7 1.3 bitcast_select_fusion.act_ref
  35.0 1.6 %convolution_convert_fusion = bf16[640,384]{0,1:T(8,128)(2,1)} fusion(bf16[640,1024]{1,0:T(8,128)(2,1)S(1)} %bitcast_select_fusion.act_ref, bf16[384,1024]{1,0:T(8,128)(2,1)S(1)} %nine.1), kind=kOutput, calls=%fused_computation.7 | convolution fusion | flops 503562240 | bytes 2588672 | tf_op jit(solution)/shard_map/dot_general | solution.py:138
  36.6 15.2 %all-to-all-start.1 = ((bf16[12,32,640]{2,1,0:T(8,128)(2,1)}), bf16[12,32,640]{2,1,0:T(8,128)(2,1)S(1)}, u32[]{:S(2)}, u32[]{:S(2)}) async-start(bf16[12,32,640]{2,1,0:T(8,128)(2,1)} %bitcast.19), calls=%async_computation.1 | async-start | bytes 983040 | tf_op jit(solution)/shard_map/all_to_all | solution.py:142
  51.8 1.9 %collective-permute-start.1 = (f32[8,40,1024]{2,1,0:T(8,128)}, f32[8,40,1024]{2,1,0:T(8,128)}, u32[]{:S(2)}, u32[]{:S(2)}) collective-permute-start(f32[8,40,1024]{2,1,0:T(8,128)} %dynamic-slice_bitcast_fusion), channel_id=1, source_target_pairs={{0,1},{1,0},{2,3},{3,2},{4,5},{5,4},{6,7},{7,6},{8,9},{9,8},{10,11... | collective-permute-start | bytes 3932168 | tf_op jit(solution)/shard_map/ppermute | solution.py:148
  53.7 20.9 %all-to-all-done.1.parts_ref = bf16[12,32,640]{2,1,0:T(8,128)(2,1)S(1)} async-done(((bf16[12,32,640]{2,1,0:T(8,128)(2,1)}), bf16[12,32,640]{2,1,0:T(8,128)(2,1)S(1)}, u32[]{:S(2)}, u32[]{:S(2)}) %all-to-all-start.1) | async-done | bytes 491552 | tf_op jit(solution)/shard_map/all_to_all | solution.py:142
  74.6 13.7 %all_to_all.20.parts_ref = f32[4,32,640]{2,1,0:T(8,128)S(1)} all-to-all(f32[4,32,640]{2,1,0:T(8,128)S(1)} %sum_z.1), channel_id=1, replica_groups=mesh['z'=12,'yl'=4,'x'=4,'yh'=2,'c'=2] {'yl'}, dimensions={0} | all-to-all | bytes 655360 | tf_op jit(solution)/shard_map/all_to_all | solution.py:172
  89.2 5.6 %all-to-all-start.3 = ((bf16[12,32,640]{2,1,0:T(8,128)(2,1)}), bf16[12,32,640]{2,1,0:T(8,128)(2,1)S(1)}, u32[]{:S(2)}, u32[]{:S(2)}) async-start(bf16[12,32,640]{2,1,0:T(8,128)(2,1)} %sum_yl.1), calls=%async_computation.3 | async-start | bytes 983040 | tf_op jit(solution)/shard_map/all_to_all | solution.py:178
  94.8 1.9 %fusion = bf16[8,40,1024]{2,1,0:T(8,128)(2,1)S(1)} fusion(f32[8,40,1024]{2,1,0:T(8,128)} %collective-permute-done.1, f32[8,2,40,1024]{3,2,1,0:T(8,128)} %copy-done.6, s32[]{:T(128)S(6)} %select_n.34), kind=kLoop, calls=%fused_computation.4 | loop fusion | flops 655360 | bytes 3276804 | tf_op jit(solution)/shard_map/convert_element_type | solution.py:149
  97.5 4.1 %collective-permute-start.2 = (bf16[2,40,1024]{2,1,0:T(8,128)(2,1)}, bf16[2,40,1024]{2,1,0:T(8,128)(2,1)}, u32[]{:S(2)}, u32[]{:S(2)}) collective-permute-start(bf16[2,40,1024]{2,1,0:T(8,128)(2,1)} %get-tuple-element.24), channel_id=1, source_target_pairs={{0,4},{4,8},{8,12},{12,0},{1,5},{5,9},{9,13},{13,1},{2,6},{6,10},{... | collective-permute-start | bytes 491528 | tf_op jit(solution)/shard_map/ppermute | solution.py:154
  101.6 2.2 %collective-permute-start.3 = (bf16[2,40,1024]{2,1,0:T(8,128)(2,1)}, bf16[2,40,1024]{2,1,0:T(8,128)(2,1)}, u32[]{:S(2)}, u32[]{:S(2)}) collective-permute-start(bf16[2,40,1024]{2,1,0:T(8,128)(2,1)} %get-tuple-element.26), channel_id=1, source_target_pairs={{0,8},{4,12},{8,0},{12,4},{1,9},{5,13},{9,1},{13,5},{2,10},{6,14},... | collective-permute-start | bytes 491528 | tf_op jit(solution)/shard_map/ppermute | solution.py:154
  103.8 2.5 %collective-permute-start.4 = (bf16[2,40,1024]{2,1,0:T(8,128)(2,1)S(1)}, bf16[2,40,1024]{2,1,0:T(8,128)(2,1)}, u32[]{:S(2)}, u32[]{:S(2)}) collective-permute-start(bf16[2,40,1024]{2,1,0:T(8,128)(2,1)S(1)} %get-tuple-element.25), channel_id=1, source_target_pairs={{0,12},{4,0},{8,4},{12,8},{1,13},{5,1},{9,5},{13,9},{2,14},{6,2},{... | collective-permute-start | bytes 491528 | tf_op jit(solution)/shard_map/ppermute | solution.py:154
  106.3 1.5 %collective-permute-done.2 = bf16[2,40,1024]{2,1,0:T(8,128)(2,1)} collective-permute-done((bf16[2,40,1024]{2,1,0:T(8,128)(2,1)}, bf16[2,40,1024]{2,1,0:T(8,128)(2,1)}, u32[]{:S(2)}, u32[]{:S(2)}) %collective-permute-start.2) | collective-permute-done | bytes 163872 | tf_op jit(solution)/shard_map/ppermute | solution.py:154
  107.8 3.2 %collective-permute-done.3 = bf16[2,40,1024]{2,1,0:T(8,128)(2,1)} collective-permute-done((bf16[2,40,1024]{2,1,0:T(8,128)(2,1)}, bf16[2,40,1024]{2,1,0:T(8,128)(2,1)}, u32[]{:S(2)}, u32[]{:S(2)}) %collective-permute-start.3) | collective-permute-done | bytes 163872 | tf_op jit(solution)/shard_map/ppermute | solution.py:154
  111.0 1.7 %collective-permute-done.4 = bf16[2,40,1024]{2,1,0:T(8,128)(2,1)} collective-permute-done((bf16[2,40,1024]{2,1,0:T(8,128)(2,1)S(1)}, bf16[2,40,1024]{2,1,0:T(8,128)(2,1)}, u32[]{:S(2)}, u32[]{:S(2)}) %collective-permute-start.4) | collective-permute-done | bytes 163872 | tf_op jit(solution)/shard_map/ppermute | solution.py:154
  114.0 2.2 %collective-permute-start.5 = (bf16[40,1024]{1,0:T(8,128)(2,1)S(1)}, bf16[40,1024]{1,0:T(8,128)(2,1)S(1)}, u32[]{:S(2)}, u32[]{:S(2)}) collective-permute-start(bf16[40,1024]{1,0:T(8,128)(2,1)S(1)} %get-tuple-element.27), channel_id=1, source_target_pairs={{0,2},{2,0},{1,3},{3,1},{4,6},{6,4},{5,7},{7,5},{8,10},{10,8},{9,1... | collective-permute-start | bytes 245768 | tf_op jit(solution)/shard_map/ppermute | solution.py:159
  116.2 1.6 %forward.1 = f32[40,1024]{1,0:T(8,128)} custom-call(bf16[360,640]{1,0:T(8,128)(2,1)S(1)} %bitcast.45, bf16[640,1024]{1,0:T(8,128)(2,1)S(1)} %bitcast_select_fusion.act_ref, f32[40,1024]{1,0:T(8,128)S(1)} %copy-done), custom_call_target="tpu_custom_call" | custom-call | tf_op jit(solution)/shard_map/forward/pallas_call | solution.py:144
  117.8 6.6 %collective-permute-done.5.taken_ref = bf16[40,1024]{1,0:T(8,128)(2,1)S(1)} collective-permute-done((bf16[40,1024]{1,0:T(8,128)(2,1)S(1)}, bf16[40,1024]{1,0:T(8,128)(2,1)S(1)}, u32[]{:S(2)}, u32[]{:S(2)}) %collective-permute-start.5) | collective-permute-done | bytes 81952 | tf_op jit(solution)/shard_map/ppermute | solution.py:159
  125.4 3.3 %divide_subtract_fusion = (f32[9,40,640]{2,1,0:T(8,128)}, f32[9,40,640]{2,1,0:T(8,128)}, f32[9,40,640]{2,1,0:T(8,128)}) fusion(f32[9,40,640]{2,1,0:T(8,128)S(1)} %copy-done.8, bf16[9,40,640]{2,1,0:T(8,128)(2,1)S(1)} %bitcast.52, f32[9,40,640]{2,1,0:T(8,128)} %param.11, f32[9,40,640]{2,1,0:T(8,128)} %param.12), kind=kLoop, calls=%fused_computation.10 | loop fusion | flops 2995200 | bytes 5990400 | tf_op jit(solution)/shard_map/sub | solution.py:183
  (34 shorter events, 7.2 us)
Async XLA Ops:
  0.6 15.2 %copy-start.7 = (f32[9,40,640]{2,1,0:T(8,128)S(1)}, f32[9,40,640]{2,1,0:T(8,128)}, u32[]{:S(2)}) copy-start(f32[9,40,640]{2,1,0:T(8,128)} %param.10) | copy-start | bytes 2764804
  2.8 26.8 %all-to-all-start = ((bf16[8,40,1024]{2,1,0:T(8,128)(2,1)}), bf16[8,40,1024]{2,1,0:T(8,128)(2,1)S(1)}, u32[]{:S(2)}, u32[]{:S(2)}) async-start(bf16[8,40,1024]{2,1,0:T(8,128)(2,1)} %get-tuple-element.13), calls=%async_computation | async-start | bytes 1310720 | tf_op jit(solution)/shard_map/all_to_all | solution.py:123
  15.8 0.9 copy-start.1
  17.8 1.5 %copy-start.6 = (f32[8,2,40,1024]{3,2,1,0:T(8,128)}, f32[8,2,40,1024]{3,2,1,0:T(8,128)S(1)}, u32[]{:S(2)}) copy-start(f32[8,2,40,1024]{3,2,1,0:T(8,128)S(1)} %fusion.3) | copy-start | bytes 7864324
  29.6 4.1 %collective-permute-start = (bf16[8,40,1024]{2,1,0:T(8,128)(2,1)S(1)}, bf16[8,40,1024]{2,1,0:T(8,128)(2,1)}, u32[]{:S(2)}, u32[]{:S(2)}) collective-permute-start(bf16[8,40,1024]{2,1,0:T(8,128)(2,1)S(1)} %all-to-all-done), channel_id=1, source_target_pairs={{0,1},{1,0},{2,3},{3,2},{4,5},{5,4},{6,7},{7,6},{8,9},{9,8},{10,11... | collective-permute-start | bytes 1966088 | tf_op jit(solution)/shard_map/ppermute | solution.py:133
  36.6 38.0 %all-to-all-start.1 = ((bf16[12,32,640]{2,1,0:T(8,128)(2,1)}), bf16[12,32,640]{2,1,0:T(8,128)(2,1)S(1)}, u32[]{:S(2)}, u32[]{:S(2)}) async-start(bf16[12,32,640]{2,1,0:T(8,128)(2,1)} %bitcast.19), calls=%async_computation.1 | async-start | bytes 983040 | tf_op jit(solution)/shard_map/all_to_all | solution.py:142
  51.8 43.1 %collective-permute-start.1 = (f32[8,40,1024]{2,1,0:T(8,128)}, f32[8,40,1024]{2,1,0:T(8,128)}, u32[]{:S(2)}, u32[]{:S(2)}) collective-permute-start(f32[8,40,1024]{2,1,0:T(8,128)} %dynamic-slice_bitcast_fusion), channel_id=1, source_target_pairs={{0,1},{1,0},{2,3},{3,2},{4,5},{5,4},{6,7},{7,6},{8,9},{9,8},{10,11... | collective-permute-start | bytes 3932168 | tf_op jit(solution)/shard_map/ppermute | solution.py:148
  89.2 36.1 %all-to-all-start.3 = ((bf16[12,32,640]{2,1,0:T(8,128)(2,1)}), bf16[12,32,640]{2,1,0:T(8,128)(2,1)S(1)}, u32[]{:S(2)}, u32[]{:S(2)}) async-start(bf16[12,32,640]{2,1,0:T(8,128)(2,1)} %sum_yl.1), calls=%async_computation.3 | async-start | bytes 983040 | tf_op jit(solution)/shard_map/all_to_all | solution.py:178
  96.7 19.5 %copy-start = (f32[40,1024]{1,0:T(8,128)S(1)}, f32[40,1024]{1,0:T(8,128)}, u32[]{:S(2)}) copy-start(f32[40,1024]{1,0:T(8,128)} %x_ref.3) | copy-start | bytes 491524
  97.5 10.3 %collective-permute-start.2 = (bf16[2,40,1024]{2,1,0:T(8,128)(2,1)}, bf16[2,40,1024]{2,1,0:T(8,128)(2,1)}, u32[]{:S(2)}, u32[]{:S(2)}) collective-permute-start(bf16[2,40,1024]{2,1,0:T(8,128)(2,1)} %get-tuple-element.24), channel_id=1, source_target_pairs={{0,4},{4,8},{8,12},{12,0},{1,5},{5,9},{9,13},{13,1},{2,6},{6,10},{... | collective-permute-start | bytes 491528 | tf_op jit(solution)/shard_map/ppermute | solution.py:154
  101.6 9.4 %collective-permute-start.3 = (bf16[2,40,1024]{2,1,0:T(8,128)(2,1)}, bf16[2,40,1024]{2,1,0:T(8,128)(2,1)}, u32[]{:S(2)}, u32[]{:S(2)}) collective-permute-start(bf16[2,40,1024]{2,1,0:T(8,128)(2,1)} %get-tuple-element.26), channel_id=1, source_target_pairs={{0,8},{4,12},{8,0},{12,4},{1,9},{5,13},{9,1},{13,5},{2,10},{6,14},... | collective-permute-start | bytes 491528 | tf_op jit(solution)/shard_map/ppermute | solution.py:154
  103.8 9.0 %collective-permute-start.4 = (bf16[2,40,1024]{2,1,0:T(8,128)(2,1)S(1)}, bf16[2,40,1024]{2,1,0:T(8,128)(2,1)}, u32[]{:S(2)}, u32[]{:S(2)}) collective-permute-start(bf16[2,40,1024]{2,1,0:T(8,128)(2,1)S(1)} %get-tuple-element.25), channel_id=1, source_target_pairs={{0,12},{4,0},{8,4},{12,8},{1,13},{5,1},{9,5},{13,9},{2,14},{6,2},{... | collective-permute-start | bytes 491528 | tf_op jit(solution)/shard_map/ppermute | solution.py:154
  113.9 10.5 %copy-start.2 = (f32[40,1024]{1,0:T(8,128)S(1)}, f32[40,1024]{1,0:T(8,128)}, u32[]{:S(2)}) copy-start(f32[40,1024]{1,0:T(8,128)} %get-tuple-element.18.normed_ref) | copy-start | bytes 491524
  113.9 10.4 %copy-start.3 = (f32[40,1024]{1,0:T(8,128)S(1)}, f32[40,1024]{1,0:T(8,128)}, u32[]{:S(2)}) copy-start(f32[40,1024]{1,0:T(8,128)} %get-tuple-element.19.pre_ref) | copy-start | bytes 491524
  113.9 10.4 %copy-start.4 = (f32[8,128]{1,0:T(8,128)S(1)}, f32[8,128]{1,0:T(8,128)}, u32[]{:S(2)}) copy-start(f32[8,128]{1,0:T(8,128)} %get-tuple-element.20.inv_ref) | copy-start | bytes 12292
  114.0 10.4 %copy-start.5 = (f32[40]{0:T(128)S(1)}, f32[40]{0:T(128)}, u32[]{:S(2)}) copy-start(f32[40]{0:T(128)} %param.8) | copy-start | bytes 484
  114.0 10.4 %collective-permute-start.5 = (bf16[40,1024]{1,0:T(8,128)(2,1)S(1)}, bf16[40,1024]{1,0:T(8,128)(2,1)S(1)}, u32[]{:S(2)}, u32[]{:S(2)}) collective-permute-start(bf16[40,1024]{1,0:T(8,128)(2,1)S(1)} %get-tuple-element.27), channel_id=1, source_target_pairs={{0,2},{2,0},{1,3},{3,1},{4,6},{6,4},{5,7},{7,5},{8,10},{10,8},{9,1... | collective-permute-start | bytes 245768 | tf_op jit(solution)/shard_map/ppermute | solution.py:159
  117.8 7.5 %copy-start.8 = (f32[9,40,640]{2,1,0:T(8,128)S(1)}, f32[9,40,640]{2,1,0:T(8,128)}, u32[]{:S(2)}) copy-start(f32[9,40,640]{2,1,0:T(8,128)} %param.10) | copy-start | bytes 2764804

commit v6 on v5

--- a/solution.py
+++ b/solution.py
@@ -1,5 +1,3 @@
-import functools
-
 import jax
 import jax.numpy as jnp
 from jax import lax
@@ -76,8 +74,8 @@
     out_ref[...] = total
 
 
-def sum_copies_kernel(parts_ref, out_ref, *, scale):
-    total = (jnp.sum(parts_ref[...].astype(jnp.float32), axis=0) * scale).astype(out_ref.dtype)
+def sum_copies_kernel(parts_ref, out_ref):
+    total = jnp.sum(parts_ref[...].astype(jnp.float32), axis=0).astype(out_ref.dtype)
     for copy in range(out_ref.shape[0]):
         out_ref[copy] = total
 
@@ -127,9 +125,10 @@
         preferred_element_type=f32,
     ).reshape(n_xy, 2, local_ch, width)
     give = lax.dynamic_index_in_dim(partial, 1 - core, 1, keepdims=False)
-    by_xy, partial, give, weight_nine = lax.optimization_barrier(
-        (by_xy, partial, give, weight_nine)
-    )
+    taken = lax.ppermute(give, "c", swap)
+    keep = lax.dynamic_index_in_dim(partial, core, 1, keepdims=False)
+    partial = (keep + taken).astype(bf16)
+    by_xy, partial, weight_nine = lax.optimization_barrier((by_xy, partial, weight_nine))
     other = lax.ppermute(by_xy, "c", swap)
     mine = jnp.arange(2) == core
     gathered = jnp.where(mine[None, :, None, None], by_xy[:, None], other[:, None])
@@ -144,9 +143,6 @@
     block_out = pl.pallas_call(forward_kernel, out_shape=tile, name="forward", compiler_params=SMALL)(
         weight_nine, gathered, inputs
     )
-    keep = lax.dynamic_index_in_dim(partial, core, 1, keepdims=False)
-    taken = lax.ppermute(give, "c", swap)
-    partial = (keep + taken).astype(bf16)
     at = lax.axis_index("x")
     by_chip = partial.reshape(n_x, 2, local_ch, width)
     pick = lambda k: lax.dynamic_index_in_dim(by_chip, lax.rem(at + k, n_x), 0, keepdims=False)
@@ -165,21 +161,19 @@
     )
 
     z_sum = pl.pallas_call(
-        functools.partial(sum_copies_kernel, scale=1.0),
+        sum_copies_kernel,
         out_shape=jax.ShapeDtypeStruct((n_yl, chunk_rows, all_ch), f32),
         name="sum_z", compiler_params=SMALL,
     )(by_z)
     by_yl = lax.all_to_all(z_sum, "yl", 0, 0, tiled=True)
-    total = pl.pallas_call(
-        functools.partial(sum_copies_kernel, scale=1.0 / n_dp),
-        out_shape=jax.ShapeDtypeStruct((n_z, chunk_rows, all_ch), bf16),
-        name="sum_yl", compiler_params=SMALL,
-    )(by_yl)
-    total = lax.all_to_all(total, "z", 0, 0, tiled=True)
-    gradient = total.reshape(pad_rows, all_ch)[: 9 * local_ch].reshape(9, local_ch, all_ch).astype(f32)
+    first_old, second_old = BETA_ONE * moment_one, BETA_TWO * moment_two
+    by_yl, first_old, second_old = lax.optimization_barrier((by_yl, first_old, second_old))
+    total = (jnp.sum(by_yl, axis=0) / n_dp).astype(bf16)
+    total = lax.all_gather(total, "z", axis=0, tiled=True)
+    gradient = total[: 9 * local_ch].reshape(9, local_ch, all_ch).astype(f32)
 
-    first_new = BETA_ONE * moment_one + (1.0 - BETA_ONE) * gradient
-    second_new = BETA_TWO * moment_two + (1.0 - BETA_TWO) * gradient * gradient
+    first_new = first_old + (1.0 - BETA_ONE) * gradient
+    second_new = second_old + (1.0 - BETA_TWO) * gradient * gradient
     weight_new = conv_weight - LEARN_RATE * (first_new / CORRECT_ONE) / (
         jnp.sqrt(second_new / CORRECT_TWO) + EPS_ADAM
     )

time: 130 us -> 135 us (1.038)
  the two profiles are of different devices: /device:TPU:6 before, /device:TPU:8 now
where the time goes in v6:
time: 135 us
  waiting for transfers between devices  42.6 us (32%)
  starting transfers between devices  41.3 us (31%)
  blocking collectives  25.8 us (19%)
  other arithmetic  10.4 us (8%)
  Pallas kernels  5.64 us (4%)
  matrix products  3.97 us (3%)
  local copies, waits for them, and re-layouts  3.87 us (3%)
    all_gather x1, blocking collectives, step(): total = lax.all_gather(total, 'z', axis=0, tiled=True)  25.8 us
    all_to_all x1, waiting for transfers between devices, step(): by_xy = lax.all_to_all(act, XY, 0, 0, tiled=True)  20.6 us
    all_to_all x1, starting transfers between devices, step(): by_z = lax.all_to_all(taps, 'z', 0, 0, tiled=True)  15.3 us
    all_to_all x1, waiting for transfers between devices, step(): by_z = lax.all_to_all(taps, 'z', 0, 0, tiled=True)  13.9 us
    all_to_all x1, starting transfers between devices, step(): by_xy = lax.all_to_all(act, XY, 0, 0, tiled=True)  8.67 us
    ppermute x3, starting transfers between devices, step(): lax.ppermute(pick(k), 'x', [(i, (i + k) % n_x) for i in range(n_x)])  7.99 us
    ppermute x1, waiting for transfers between devices, step(): lax.ppermute(lax.dynamic_index_in_dim(pair, 1 - row, 0, keepdims=False),...  6.04 us
    all_to_all x1, starting transfers between devices, step(): by_yl = lax.all_to_all(z_sum, 'yl', 0, 0, tiled=True)  3.44 us
  transfers between devices with their start and end apart: 9, of which 4 were waited for; matrix products, arithmetic and copies ran while one was open for 5% of the time, Pallas kernels for 4%

profile of v6, /device:TPU:8, one launch (start us, length us, event | category | flops | bytes accessed | tf_op | source)
XLA Modules:
  0.0 134.5 jit_solution(6341926927635041041)
XLA Ops:
  0.6 1.3 convert_element_type.39
  2.5 2.4 %fusion.3 = f32[8,2,40,1024]{3,2,1,0:T(8,128)} fusion(bf16[8,2,40,360]{3,2,1,0:T(8,128)(2,1)S(1)} %bitcast.49, bf16[384,1024]{1,0:T(8,128)(2,1)S(1)} %nine.1), kind=kOutput, calls=%fused_computation.12 | convolution fusion | flops 471859200 | bytes 3850240 | tf_op jit(solution)/shard_map/dot_general | solution.py:123
  4.8 2.5 %dynamic-slice_bitcast_fusion = f32[8,40,1024]{2,1,0:T(8,128)} fusion(f32[8,2,40,1024]{3,2,1,0:T(8,128)} %fusion.3, s32[]{:T(128)S(6)} %select_n.33), kind=kLoop, calls=%fused_computation.6 | loop fusion | bytes 2621444 | tf_op jit(solution)/shard_map/jit(dynamic_index_in_dim)/squeeze | solution.py:127
  7.3 1.9 %collective-permute-start = (f32[8,40,1024]{2,1,0:T(8,128)}, f32[8,40,1024]{2,1,0:T(8,128)S(1)}, u32[]{:S(2)}, u32[]{:S(2)}) collective-permute-start(f32[8,40,1024]{2,1,0:T(8,128)} %dynamic-slice_bitcast_fusion), channel_id=1, source_target_pairs={{0,1},{1,0},{2,3},{3,2},{4,5},{5,4},{6,7},{7,6},{8,9},{9,8},{10,11... | collective-permute-start | bytes 3932168 | tf_op jit(solution)/shard_map/ppermute | solution.py:128
  9.3 2.1 %norm.1 = (bf16[8,40,1024]{2,1,0:T(8,128)(2,1)}, f32[40,1024]{1,0:T(8,128)}, f32[40,1024]{1,0:T(8,128)}, f32[8,128]{1,0:T(8,128)}) custom-call(f32[40,1024]{1,0:T(8,128)} %x_ref.3, f32[1,40]{1,0:T(1,128)} %bitcast.45, f32[1,40]{1,0:T(1,128)} %bitcast.52), custom_call_target="tpu_custom_call" | custom-call | tf_op jit(solution)/shard_map/norm/pallas_call | solution.py:107
  11.4 8.7 %all-to-all-start = ((bf16[8,40,1024]{2,1,0:T(8,128)(2,1)}), bf16[8,40,1024]{2,1,0:T(8,128)(2,1)S(1)}, u32[]{:S(2)}, u32[]{:S(2)}) async-start(bf16[8,40,1024]{2,1,0:T(8,128)(2,1)} %get-tuple-element.15), calls=%async_computation | async-start | bytes 1310720 | tf_op jit(solution)/shard_map/all_to_all | solution.py:121
  20.1 2.4 %fusion = bf16[8,40,1024]{2,1,0:T(8,128)(2,1)} fusion(f32[8,40,1024]{2,1,0:T(8,128)S(1)} %collective-permute-done, f32[8,2,40,1024]{3,2,1,0:T(8,128)} %fusion.3, s32[]{:T(128)S(6)} %select_n.32), kind=kLoop, calls=%fused_computation.5 | loop fusion | flops 655360 | bytes 3276804 | tf_op jit(solution)/shard_map/convert_element_type | solution.py:130
  22.5 20.6 %all-to-all-done = bf16[8,40,1024]{2,1,0:T(8,128)(2,1)S(1)} async-done(((bf16[8,40,1024]{2,1,0:T(8,128)(2,1)}), bf16[8,40,1024]{2,1,0:T(8,128)(2,1)S(1)}, u32[]{:S(2)}, u32[]{:S(2)}) %all-to-all-start) | async-done | bytes 655392 | tf_op jit(solution)/shard_map/all_to_all | solution.py:121
  43.1 1.9 %collective-permute-start.1 = (bf16[8,40,1024]{2,1,0:T(8,128)(2,1)S(1)}, bf16[8,40,1024]{2,1,0:T(8,128)(2,1)}, u32[]{:S(2)}, u32[]{:S(2)}) collective-permute-start(bf16[8,40,1024]{2,1,0:T(8,128)(2,1)S(1)} %all-to-all-done), channel_id=1, source_target_pairs={{0,1},{1,0},{2,3},{3,2},{4,5},{5,4},{6,7},{7,6},{8,9},{9,8},{10,11... | collective-permute-start | bytes 1966088 | tf_op jit(solution)/shard_map/ppermute | solution.py:132
  45.2 2.0 %collective-permute-done.1 = bf16[8,40,1024]{2,1,0:T(8,128)(2,1)} collective-permute-done((bf16[8,40,1024]{2,1,0:T(8,128)(2,1)S(1)}, bf16[8,40,1024]{2,1,0:T(8,128)(2,1)}, u32[]{:S(2)}, u32[]{:S(2)}) %collective-permute-start.1) | collective-permute-done | bytes 655392 | tf_op jit(solution)/shard_map/ppermute | solution.py:132
  47.3 1.3 bitcast_select_fusion.act_ref
  48.5 1.6 %convolution_convert_fusion = bf16[640,384]{0,1:T(8,128)(2,1)} fusion(bf16[640,1024]{1,0:T(8,128)(2,1)S(1)} %bitcast_select_fusion.act_ref, bf16[384,1024]{1,0:T(8,128)(2,1)S(1)} %nine.1), kind=kOutput, calls=%fused_computation.7 | convolution fusion | flops 503562240 | bytes 2588672 | tf_op jit(solution)/shard_map/dot_general | solution.py:137
  50.1 15.3 %all-to-all-start.1 = ((bf16[12,32,640]{2,1,0:T(8,128)(2,1)}), bf16[12,32,640]{2,1,0:T(8,128)(2,1)S(1)}, u32[]{:S(2)}, u32[]{:S(2)}) async-start(bf16[12,32,640]{2,1,0:T(8,128)(2,1)} %bitcast.51), calls=%async_computation.1 | async-start | bytes 983040 | tf_op jit(solution)/shard_map/all_to_all | solution.py:141
  66.2 3.1 %collective-permute-start.4 = (bf16[2,40,1024]{2,1,0:T(8,128)(2,1)}, bf16[2,40,1024]{2,1,0:T(8,128)(2,1)}, u32[]{:S(2)}, u32[]{:S(2)}) collective-permute-start(bf16[2,40,1024]{2,1,0:T(8,128)(2,1)} %get-tuple-element.29), channel_id=1, source_target_pairs={{0,12},{4,0},{8,4},{12,8},{1,13},{5,1},{9,5},{13,9},{2,14},{6,2},{... | collective-permute-start | bytes 491528 | tf_op jit(solution)/shard_map/ppermute | solution.py:150
  69.3 2.5 %collective-permute-start.3 = (bf16[2,40,1024]{2,1,0:T(8,128)(2,1)}, bf16[2,40,1024]{2,1,0:T(8,128)(2,1)}, u32[]{:S(2)}, u32[]{:S(2)}) collective-permute-start(bf16[2,40,1024]{2,1,0:T(8,128)(2,1)} %get-tuple-element.30), channel_id=1, source_target_pairs={{0,8},{4,12},{8,0},{12,4},{1,9},{5,13},{9,1},{13,5},{2,10},{6,14},... | collective-permute-start | bytes 491528 | tf_op jit(solution)/shard_map/ppermute | solution.py:150
  71.9 2.4 %collective-permute-start.2 = (bf16[2,40,1024]{2,1,0:T(8,128)(2,1)}, bf16[2,40,1024]{2,1,0:T(8,128)(2,1)}, u32[]{:S(2)}, u32[]{:S(2)}) collective-permute-start(bf16[2,40,1024]{2,1,0:T(8,128)(2,1)} %get-tuple-element.28), channel_id=1, source_target_pairs={{0,4},{4,8},{8,12},{12,0},{1,5},{5,9},{9,13},{13,1},{2,6},{6,10},{... | collective-permute-start | bytes 491528 | tf_op jit(solution)/shard_map/ppermute | solution.py:150
  74.3 13.9 %all-to-all-done.1.parts_ref = bf16[12,32,640]{2,1,0:T(8,128)(2,1)S(1)} async-done(((bf16[12,32,640]{2,1,0:T(8,128)(2,1)}), bf16[12,32,640]{2,1,0:T(8,128)(2,1)S(1)}, u32[]{:S(2)}, u32[]{:S(2)}) %all-to-all-start.1) | async-done | bytes 491552 | tf_op jit(solution)/shard_map/all_to_all | solution.py:141
  89.0 3.4 %all-to-all-start.2 = ((f32[4,32,640]{2,1,0:T(8,128)}), f32[4,32,640]{2,1,0:T(8,128)S(1)}, u32[]{:S(2)}, u32[]{:S(2)}) async-start(f32[4,32,640]{2,1,0:T(8,128)} %sum_z.1), calls=%async_computation.2 | async-start | bytes 655360 | tf_op jit(solution)/shard_map/all_to_all | solution.py:168
  93.8 2.1 %collective-permute-start.5 = (bf16[40,1024]{1,0:T(8,128)(2,1)S(1)}, bf16[40,1024]{1,0:T(8,128)(2,1)S(1)}, u32[]{:S(2)}, u32[]{:S(2)}) collective-permute-start(bf16[40,1024]{1,0:T(8,128)(2,1)S(1)} %get-tuple-element.31), channel_id=1, source_target_pairs={{0,2},{2,0},{1,3},{3,1},{4,6},{6,4},{5,7},{7,5},{8,10},{10,8},{9,1... | collective-permute-start | bytes 245768 | tf_op jit(solution)/shard_map/ppermute | solution.py:155
  95.9 2.3 %broadcast_multiply_fusion = (f32[9,40,640]{2,1,0:T(8,128)S(1)}, f32[9,40,640]{2,1,0:T(8,128)}) fusion(f32[9,40,640]{2,1,0:T(8,128)S(1)} %copy-done.9, f32[9,40,640]{2,1,0:T(8,128)} %param.11), kind=kLoop, calls=%fused_computation.13 | loop fusion | flops 460800 | bytes 3686400 | tf_op jit(solution)/shard_map/mul | solution.py:169
  98.2 6.0 %collective-permute-done.5.taken_ref = bf16[40,1024]{1,0:T(8,128)(2,1)S(1)} collective-permute-done((bf16[40,1024]{1,0:T(8,128)(2,1)S(1)}, bf16[40,1024]{1,0:T(8,128)(2,1)S(1)}, u32[]{:S(2)}, u32[]{:S(2)}) %collective-permute-start.5) | collective-permute-done | bytes 81952 | tf_op jit(solution)/shard_map/ppermute | solution.py:155
  105.1 1.6 %forward.1 = f32[40,1024]{1,0:T(8,128)} custom-call(bf16[360,640]{1,0:T(8,128)(2,1)S(1)} %bitcast.44, bf16[640,1024]{1,0:T(8,128)(2,1)S(1)} %bitcast_select_fusion.act_ref, f32[40,1024]{1,0:T(8,128)S(1)} %copy-done), custom_call_target="tpu_custom_call" | custom-call | tf_op jit(solution)/shard_map/forward/pallas_call | solution.py:143
  106.8 25.8 %all_gather.3 = bf16[384,640]{1,0:T(8,128)(2,1)S(1)} all-gather(bf16[32,640]{1,0:T(8,128)(2,1)S(1)} %multiply_convert_fusion), channel_id=1, replica_groups=mesh['z'=12,'yl'=4,'x'=4,'yh'=2,'c'=2] {'z'}, dimensions={0}, use_global_device_ids=true | all-gather | bytes 532480 | tf_op jit(solution)/shard_map/all_gather | solution.py:172
  132.7 1.9 %divide_subtract_fusion = (f32[9,40,640]{2,1,0:T(8,128)}, f32[9,40,640]{2,1,0:T(8,128)}, f32[9,40,640]{2,1,0:T(8,128)}) fusion(f32[9,40,640]{2,1,0:T(8,128)S(1)} %copy-done.7, f32[9,40,640]{2,1,0:T(8,128)S(1)} %copy-done.6, bf16[9,40,640]{2,1,0:T(8,128)(2,1)S(1)} %bitcast.50, f32[9,40,640]{2,1,0:T(8,128)S(1)} %get-tuple-element.24), kind=kLoop, calls=%fused_computation.10 | loop fusion | flops 2534400 | bytes 5990400 | tf_op jit(solution)/shard_map/sub | solution.py:177
  (38 shorter events, 4.6 us)
Async XLA Ops:
  0.6 1.6 %copy-start.1 = (f32[40,1024]{1,0:T(8,128)S(1)}, f32[40,1024]{1,0:T(8,128)}, u32[]{:S(2)}) copy-start(f32[40,1024]{1,0:T(8,128)} %grad_ref.1) | copy-start | bytes 491524
  7.3 12.7 %collective-permute-start = (f32[8,40,1024]{2,1,0:T(8,128)}, f32[8,40,1024]{2,1,0:T(8,128)S(1)}, u32[]{:S(2)}, u32[]{:S(2)}) collective-permute-start(f32[8,40,1024]{2,1,0:T(8,128)} %dynamic-slice_bitcast_fusion), channel_id=1, source_target_pairs={{0,1},{1,0},{2,3},{3,2},{4,5},{5,4},{6,7},{7,6},{8,9},{9,8},{10,11... | collective-permute-start | bytes 3932168 | tf_op jit(solution)/shard_map/ppermute | solution.py:128
  11.4 31.7 %all-to-all-start = ((bf16[8,40,1024]{2,1,0:T(8,128)(2,1)}), bf16[8,40,1024]{2,1,0:T(8,128)(2,1)S(1)}, u32[]{:S(2)}, u32[]{:S(2)}) async-start(bf16[8,40,1024]{2,1,0:T(8,128)(2,1)} %get-tuple-element.15), calls=%async_computation | async-start | bytes 1310720 | tf_op jit(solution)/shard_map/all_to_all | solution.py:121
  43.1 4.1 %collective-permute-start.1 = (bf16[8,40,1024]{2,1,0:T(8,128)(2,1)S(1)}, bf16[8,40,1024]{2,1,0:T(8,128)(2,1)}, u32[]{:S(2)}, u32[]{:S(2)}) collective-permute-start(bf16[8,40,1024]{2,1,0:T(8,128)(2,1)S(1)} %all-to-all-done), channel_id=1, source_target_pairs={{0,1},{1,0},{2,3},{3,2},{4,5},{5,4},{6,7},{7,6},{8,9},{9,8},{10,11... | collective-permute-start | bytes 1966088 | tf_op jit(solution)/shard_map/ppermute | solution.py:132
  50.1 15.3 %copy-start.8 = (bf16[8,40,1024]{2,1,0:T(8,128)(2,1)S(1)}, bf16[8,40,1024]{2,1,0:T(8,128)(2,1)}, u32[]{:S(2)}) copy-start(bf16[8,40,1024]{2,1,0:T(8,128)(2,1)} %fusion) | copy-start | bytes 1966084
  50.1 38.1 %all-to-all-start.1 = ((bf16[12,32,640]{2,1,0:T(8,128)(2,1)}), bf16[12,32,640]{2,1,0:T(8,128)(2,1)S(1)}, u32[]{:S(2)}, u32[]{:S(2)}) async-start(bf16[12,32,640]{2,1,0:T(8,128)(2,1)} %bitcast.51), calls=%async_computation.1 | async-start | bytes 983040 | tf_op jit(solution)/shard_map/all_to_all | solution.py:141
  66.2 26.2 %collective-permute-start.4 = (bf16[2,40,1024]{2,1,0:T(8,128)(2,1)}, bf16[2,40,1024]{2,1,0:T(8,128)(2,1)}, u32[]{:S(2)}, u32[]{:S(2)}) collective-permute-start(bf16[2,40,1024]{2,1,0:T(8,128)(2,1)} %get-tuple-element.29), channel_id=1, source_target_pairs={{0,12},{4,0},{8,4},{12,8},{1,13},{5,1},{9,5},{13,9},{2,14},{6,2},{... | collective-permute-start | bytes 491528 | tf_op jit(solution)/shard_map/ppermute | solution.py:150
  69.3 23.2 %collective-permute-start.3 = (bf16[2,40,1024]{2,1,0:T(8,128)(2,1)}, bf16[2,40,1024]{2,1,0:T(8,128)(2,1)}, u32[]{:S(2)}, u32[]{:S(2)}) collective-permute-start(bf16[2,40,1024]{2,1,0:T(8,128)(2,1)} %get-tuple-element.30), channel_id=1, source_target_pairs={{0,8},{4,12},{8,0},{12,4},{1,9},{5,13},{9,1},{13,5},{2,10},{6,14},... | collective-permute-start | bytes 491528 | tf_op jit(solution)/shard_map/ppermute | solution.py:150
  71.9 20.6 %collective-permute-start.2 = (bf16[2,40,1024]{2,1,0:T(8,128)(2,1)}, bf16[2,40,1024]{2,1,0:T(8,128)(2,1)}, u32[]{:S(2)}, u32[]{:S(2)}) collective-permute-start(bf16[2,40,1024]{2,1,0:T(8,128)(2,1)} %get-tuple-element.28), channel_id=1, source_target_pairs={{0,4},{4,8},{8,12},{12,0},{1,5},{5,9},{9,13},{13,1},{2,6},{6,10},{... | collective-permute-start | bytes 491528 | tf_op jit(solution)/shard_map/ppermute | solution.py:150
  89.0 17.7 %all-to-all-start.2 = ((f32[4,32,640]{2,1,0:T(8,128)}), f32[4,32,640]{2,1,0:T(8,128)S(1)}, u32[]{:S(2)}, u32[]{:S(2)}) async-start(f32[4,32,640]{2,1,0:T(8,128)} %sum_z.1), calls=%async_computation.2 | async-start | bytes 655360 | tf_op jit(solution)/shard_map/all_to_all | solution.py:168
  92.5 3.5 %copy-start.9 = (f32[9,40,640]{2,1,0:T(8,128)S(1)}, f32[9,40,640]{2,1,0:T(8,128)}, u32[]{:S(2)}) copy-start(f32[9,40,640]{2,1,0:T(8,128)} %param.12) | copy-start | bytes 2764804
  93.8 10.4 %copy-start.2 = (f32[40,1024]{1,0:T(8,128)S(1)}, f32[40,1024]{1,0:T(8,128)}, u32[]{:S(2)}) copy-start(f32[40,1024]{1,0:T(8,128)} %get-tuple-element.19.normed_ref) | copy-start | bytes 491524
  93.8 10.4 %copy-start.3 = (f32[40,1024]{1,0:T(8,128)S(1)}, f32[40,1024]{1,0:T(8,128)}, u32[]{:S(2)}) copy-start(f32[40,1024]{1,0:T(8,128)} %get-tuple-element.20.pre_ref) | copy-start | bytes 491524
  93.8 10.4 %copy-start.4 = (f32[8,128]{1,0:T(8,128)S(1)}, f32[8,128]{1,0:T(8,128)}, u32[]{:S(2)}) copy-start(f32[8,128]{1,0:T(8,128)} %get-tuple-element.21.inv_ref) | copy-start | bytes 12292
  93.8 10.4 %copy-start.5 = (f32[40]{0:T(128)S(1)}, f32[40]{0:T(128)}, u32[]{:S(2)}) copy-start(f32[40]{0:T(128)} %param.8) | copy-start | bytes 484
  93.8 11.3 %copy-start = (f32[40,1024]{1,0:T(8,128)S(1)}, f32[40,1024]{1,0:T(8,128)}, u32[]{:S(2)}) copy-start(f32[40,1024]{1,0:T(8,128)} %x_ref.3) | copy-start | bytes 491524
  93.8 10.4 %collective-permute-start.5 = (bf16[40,1024]{1,0:T(8,128)(2,1)S(1)}, bf16[40,1024]{1,0:T(8,128)(2,1)S(1)}, u32[]{:S(2)}, u32[]{:S(2)}) collective-permute-start(bf16[40,1024]{1,0:T(8,128)(2,1)S(1)} %get-tuple-element.31), channel_id=1, source_target_pairs={{0,2},{2,0},{1,3},{3,1},{4,6},{6,4},{5,7},{7,5},{8,10},{10,8},{9,1... | collective-permute-start | bytes 245768 | tf_op jit(solution)/shard_map/ppermute | solution.py:155
  106.7 25.9 %copy-start.6 = (f32[9,40,640]{2,1,0:T(8,128)S(1)}, f32[9,40,640]{2,1,0:T(8,128)}, u32[]{:S(2)}) copy-start(f32[9,40,640]{2,1,0:T(8,128)} %get-tuple-element.22) | copy-start | bytes 2764804
  106.7 25.9 %copy-start.7 = (f32[9,40,640]{2,1,0:T(8,128)S(1)}, f32[9,40,640]{2,1,0:T(8,128)}, u32[]{:S(2)}) copy-start(f32[9,40,640]{2,1,0:T(8,128)} %param.10) | copy-start | bytes 2764804

commit v7 on v6

--- a/solution.py
+++ b/solution.py
@@ -140,7 +140,7 @@
     taps = taps.astype(bf16).reshape(n_z, chunk_rows, all_ch)
     by_z = lax.all_to_all(taps, "z", 0, 0, tiled=True)
 
-    block_out = pl.pallas_call(forward_kernel, out_shape=tile, name="forward", compiler_params=SMALL)(
+    block_out = pl.pallas_call(forward_kernel, out_shape=tile, name="forward")(
         weight_nine, gathered, inputs
     )
     at = lax.axis_index("x")
@@ -156,7 +156,7 @@
         lax.dynamic_index_in_dim(pair, 1 - row, 0, keepdims=False), "yh", swap
     )
     keep = lax.dynamic_index_in_dim(pair, row, 0, keepdims=False)
-    input_grad = pl.pallas_call(back_kernel, out_shape=tile, name="back", compiler_params=SMALL)(
+    input_grad = pl.pallas_call(back_kernel, out_shape=tile, name="back")(
         keep, taken, normed, pre_act, inv, gain_row, out_grad
     )
 
@@ -166,14 +166,12 @@
         name="sum_z", compiler_params=SMALL,
     )(by_z)
     by_yl = lax.all_to_all(z_sum, "yl", 0, 0, tiled=True)
-    first_old, second_old = BETA_ONE * moment_one, BETA_TWO * moment_two
-    by_yl, first_old, second_old = lax.optimization_barrier((by_yl, first_old, second_old))
     total = (jnp.sum(by_yl, axis=0) / n_dp).astype(bf16)
     total = lax.all_gather(total, "z", axis=0, tiled=True)
     gradient = total[: 9 * local_ch].reshape(9, local_ch, all_ch).astype(f32)
 
-    first_new = first_old + (1.0 - BETA_ONE) * gradient
-    second_new = second_old + (1.0 - BETA_TWO) * gradient * gradient
+    first_new = BETA_ONE * moment_one + (1.0 - BETA_ONE) * gradient
+    second_new = BETA_TWO * moment_two + (1.0 - BETA_TWO) * gradient * gradient
     weight_new = conv_weight - LEARN_RATE * (first_new / CORRECT_ONE) / (
         jnp.sqrt(second_new / CORRECT_TWO) + EPS_ADAM
     )

time: 135 us -> 138 us (1.022)
  the two profiles are of different devices: /device:TPU:8 before, /device:TPU:16 now
where the time goes in v7:
time: 138 us; the launch traced here: 137 us
  starting transfers between devices  49.1 us (36%)
  waiting for transfers between devices  38.2 us (28%)
  blocking collectives  25.6 us (19%)
  Pallas kernels  8.32 us (6%)
  other arithmetic  6.89 us (5%)
  local copies, waits for them, and re-layouts  4.49 us (3%)
  matrix products  3.48 us (3%)
    all_gather x1, blocking collectives, step(): total = lax.all_gather(total, 'z', axis=0, tiled=True)  25.6 us
    all_to_all x1, starting transfers between devices, step(): by_z = lax.all_to_all(taps, 'z', 0, 0, tiled=True)  22.2 us
    all_to_all x1, waiting for transfers between devices, step(): by_xy = lax.all_to_all(act, XY, 0, 0, tiled=True)  14 us
    all_to_all x1, waiting for transfers between devices, step(): by_z = lax.all_to_all(taps, 'z', 0, 0, tiled=True)  13.5 us
    ppermute x3, starting transfers between devices, step(): lax.ppermute(pick(k), 'x', [(i, (i + k) % n_x) for i in range(n_x)])  9.21 us
    ppermute x1, waiting for transfers between devices, step(): lax.ppermute(lax.dynamic_index_in_dim(pair, 1 - row, 0, keepdims=False),...  8.68 us
    all_to_all x1, starting transfers between devices, step(): by_xy = lax.all_to_all(act, XY, 0, 0, tiled=True)  7.77 us
    all_to_all x1, starting transfers between devices, step(): by_yl = lax.all_to_all(z_sum, 'yl', 0, 0, tiled=True)  4.19 us
  transfers between devices with their start and end apart: 9, of which 4 were waited for; matrix products, arithmetic and copies ran while one was open for 2% of the time, Pallas kernels for 6%

profile of v7, /device:TPU:16, one launch (start us, length us, event | category | flops | bytes accessed | tf_op | source)
XLA Modules:
  0.0 136.9 jit_solution(4958830884951524291)
XLA Ops:
  0.6 1.3 convert_element_type.39
  3.9 1.9 %fusion.3 = f32[8,2,40,1024]{3,2,1,0:T(8,128)S(1)} fusion(bf16[8,2,40,360]{3,2,1,0:T(8,128)(2,1)} %bitcast.47, bf16[384,1024]{1,0:T(8,128)(2,1)S(1)} %nine.1), kind=kOutput, calls=%fused_computation.12 | convolution fusion | flops 471859200 | bytes 3819520 | tf_op jit(solution)/shard_map/dot_general | solution.py:123
  5.8 1.2 dynamic-slice_bitcast_fusion
  7.0 1.9 %collective-permute-start = (f32[8,40,1024]{2,1,0:T(8,128)}, f32[8,40,1024]{2,1,0:T(8,128)}, u32[]{:S(2)}, u32[]{:S(2)}) collective-permute-start(f32[8,40,1024]{2,1,0:T(8,128)} %dynamic-slice_bitcast_fusion), channel_id=1, source_target_pairs={{0,1},{1,0},{2,3},{3,2},{4,5},{5,4},{6,7},{7,6},{8,9},{9,8},{10,11... | collective-permute-start | bytes 3932168 | tf_op jit(solution)/shard_map/ppermute | solution.py:128
  8.9 2.1 %norm.1 = (bf16[8,40,1024]{2,1,0:T(8,128)(2,1)}, f32[40,1024]{1,0:T(8,128)}, f32[40,1024]{1,0:T(8,128)}, f32[8,128]{1,0:T(8,128)}) custom-call(f32[40,1024]{1,0:T(8,128)} %x_ref.3, f32[1,40]{1,0:T(1,128)} %bitcast.49, f32[1,40]{1,0:T(1,128)} %bitcast.51), custom_call_target="tpu_custom_call" | custom-call | tf_op jit(solution)/shard_map/norm/pallas_call | solution.py:107
  11.0 7.8 %all-to-all-start = ((bf16[8,40,1024]{2,1,0:T(8,128)(2,1)}), bf16[8,40,1024]{2,1,0:T(8,128)(2,1)}, u32[]{:S(2)}, u32[]{:S(2)}) async-start(bf16[8,40,1024]{2,1,0:T(8,128)(2,1)} %get-tuple-element.12), calls=%async_computation | async-start | bytes 1310720 | tf_op jit(solution)/shard_map/all_to_all | solution.py:121
  18.8 2.3 %fusion = bf16[8,40,1024]{2,1,0:T(8,128)(2,1)} fusion(f32[8,40,1024]{2,1,0:T(8,128)} %collective-permute-done, f32[8,2,40,1024]{3,2,1,0:T(8,128)S(1)} %fusion.3, s32[]{:T(128)S(6)} %select_n.32), kind=kLoop, calls=%fused_computation.5 | loop fusion | flops 655360 | bytes 3276804 | tf_op jit(solution)/shard_map/convert_element_type | solution.py:130
  21.1 14.0 %all-to-all-done = bf16[8,40,1024]{2,1,0:T(8,128)(2,1)} async-done(((bf16[8,40,1024]{2,1,0:T(8,128)(2,1)}), bf16[8,40,1024]{2,1,0:T(8,128)(2,1)}, u32[]{:S(2)}, u32[]{:S(2)}) %all-to-all-start) | async-done | bytes 655392 | tf_op jit(solution)/shard_map/all_to_all | solution.py:121
  35.1 1.9 %collective-permute-start.1 = (bf16[8,40,1024]{2,1,0:T(8,128)(2,1)}, bf16[8,40,1024]{2,1,0:T(8,128)(2,1)S(1)}, u32[]{:S(2)}, u32[]{:S(2)}) collective-permute-start(bf16[8,40,1024]{2,1,0:T(8,128)(2,1)} %all-to-all-done), channel_id=1, source_target_pairs={{0,1},{1,0},{2,3},{3,2},{4,5},{5,4},{6,7},{7,6},{8,9},{9,8},{10,11... | collective-permute-start | bytes 1966088 | tf_op jit(solution)/shard_map/ppermute | solution.py:132
  37.2 2.1 %collective-permute-done.1 = bf16[8,40,1024]{2,1,0:T(8,128)(2,1)S(1)} collective-permute-done((bf16[8,40,1024]{2,1,0:T(8,128)(2,1)}, bf16[8,40,1024]{2,1,0:T(8,128)(2,1)S(1)}, u32[]{:S(2)}, u32[]{:S(2)}) %collective-permute-start.1) | collective-permute-done | bytes 655392 | tf_op jit(solution)/shard_map/ppermute | solution.py:132
  39.3 1.2 bitcast_select_fusion.act_ref
  40.6 1.6 %convolution_convert_fusion = bf16[640,384]{0,1:T(8,128)(2,1)} fusion(bf16[640,1024]{1,0:T(8,128)(2,1)S(1)} %bitcast_select_fusion.act_ref, bf16[384,1024]{1,0:T(8,128)(2,1)S(1)} %nine.1), kind=kOutput, calls=%fused_computation.7 | convolution fusion | flops 503562240 | bytes 2588672 | tf_op jit(solution)/shard_map/dot_general | solution.py:137
  42.2 22.2 %all-to-all-start.1 = ((bf16[12,32,640]{2,1,0:T(8,128)(2,1)}), bf16[12,32,640]{2,1,0:T(8,128)(2,1)S(1)}, u32[]{:S(2)}, u32[]{:S(2)}) async-start(bf16[12,32,640]{2,1,0:T(8,128)(2,1)} %bitcast.19), calls=%async_computation.1 | async-start | bytes 983040 | tf_op jit(solution)/shard_map/all_to_all | solution.py:141
  64.4 1.9 %collective-permute-start.2 = (bf16[2,40,1024]{2,1,0:T(8,128)(2,1)S(1)}, bf16[2,40,1024]{2,1,0:T(8,128)(2,1)S(1)}, u32[]{:S(2)}, u32[]{:S(2)}) collective-permute-start(bf16[2,40,1024]{2,1,0:T(8,128)(2,1)S(1)} %get-tuple-element.22), channel_id=1, source_target_pairs={{0,4},{4,8},{8,12},{12,0},{1,5},{5,9},{9,13},{13,1},{2,6},{6,10},{... | collective-permute-start | bytes 491528 | tf_op jit(solution)/shard_map/ppermute | solution.py:150
  66.4 4.2 %collective-permute-start.3 = (bf16[2,40,1024]{2,1,0:T(8,128)(2,1)S(1)}, bf16[2,40,1024]{2,1,0:T(8,128)(2,1)S(1)}, u32[]{:S(2)}, u32[]{:S(2)}) collective-permute-start(bf16[2,40,1024]{2,1,0:T(8,128)(2,1)S(1)} %get-tuple-element.24), channel_id=1, source_target_pairs={{0,8},{4,12},{8,0},{12,4},{1,9},{5,13},{9,1},{13,5},{2,10},{6,14},... | collective-permute-start | bytes 491528 | tf_op jit(solution)/shard_map/ppermute | solution.py:150
  70.6 3.1 %collective-permute-start.4 = (bf16[2,40,1024]{2,1,0:T(8,128)(2,1)S(1)}, bf16[2,40,1024]{2,1,0:T(8,128)(2,1)S(1)}, u32[]{:S(2)}, u32[]{:S(2)}) collective-permute-start(bf16[2,40,1024]{2,1,0:T(8,128)(2,1)S(1)} %get-tuple-element.23), channel_id=1, source_target_pairs={{0,12},{4,0},{8,4},{12,8},{1,13},{5,1},{9,5},{13,9},{2,14},{6,2},{... | collective-permute-start | bytes 491528 | tf_op jit(solution)/shard_map/ppermute | solution.py:150
  73.7 13.5 %all-to-all-done.1.parts_ref = bf16[12,32,640]{2,1,0:T(8,128)(2,1)S(1)} async-done(((bf16[12,32,640]{2,1,0:T(8,128)(2,1)}), bf16[12,32,640]{2,1,0:T(8,128)(2,1)S(1)}, u32[]{:S(2)}, u32[]{:S(2)}) %all-to-all-start.1) | async-done | bytes 491552 | tf_op jit(solution)/shard_map/all_to_all | solution.py:141
  87.9 4.2 %all-to-all-start.2 = ((f32[4,32,640]{2,1,0:T(8,128)}), f32[4,32,640]{2,1,0:T(8,128)S(1)}, u32[]{:S(2)}, u32[]{:S(2)}) async-start(f32[4,32,640]{2,1,0:T(8,128)} %sum_z.1), calls=%async_computation.2 | async-start | bytes 655360 | tf_op jit(solution)/shard_map/all_to_all | solution.py:168
  92.9 1.9 %collective-permute-start.5 = (bf16[40,1024]{1,0:T(8,128)(2,1)S(1)}, bf16[40,1024]{1,0:T(8,128)(2,1)S(1)}, u32[]{:S(2)}, u32[]{:S(2)}) collective-permute-start(bf16[40,1024]{1,0:T(8,128)(2,1)S(1)} %get-tuple-element.25), channel_id=1, source_target_pairs={{0,2},{2,0},{1,3},{3,1},{4,6},{6,4},{5,7},{7,5},{8,10},{10,8},{9,1... | collective-permute-start | bytes 245768 | tf_op jit(solution)/shard_map/ppermute | solution.py:155
  94.8 8.7 %collective-permute-done.5.taken_ref = bf16[40,1024]{1,0:T(8,128)(2,1)S(1)} collective-permute-done((bf16[40,1024]{1,0:T(8,128)(2,1)S(1)}, bf16[40,1024]{1,0:T(8,128)(2,1)S(1)}, u32[]{:S(2)}, u32[]{:S(2)}) %collective-permute-start.5) | collective-permute-done | bytes 81952 | tf_op jit(solution)/shard_map/ppermute | solution.py:155
  104.1 2.1 %back.1 = f32[40,1024]{1,0:T(8,128)} custom-call(bf16[40,1024]{1,0:T(8,128)(2,1)} %get-tuple-element.26.keep_ref, bf16[40,1024]{1,0:T(8,128)(2,1)} %copy-done.7, f32[40,1024]{1,0:T(8,128)} %get-tuple-element.16.normed_ref, f32[40,1024]{1,0:T(8,128)} %get-tuple-element.17.pre_ref, f32[8,128]{1,0:T(8,128)} %get-tuple-element.18.inv_ref, f32[1,40]{1,0:T(1,128)} %bitcast.50, ...), custom_call_target="tpu_custom_call" | custom-call | tf_op jit(solution)/shard_map/back/pallas_call | solution.py:159
  106.2 3.1 %forward.1 = f32[40,1024]{1,0:T(8,128)} custom-call(bf16[360,640]{1,0:T(8,128)(2,1)} %bitcast.44, bf16[640,1024]{1,0:T(8,128)(2,1)} %copy-done.1, f32[40,1024]{1,0:T(8,128)} %x_ref.3), custom_call_target="tpu_custom_call" | custom-call | tf_op jit(solution)/shard_map/forward/pallas_call | solution.py:143
  109.3 25.6 %all_gather.3 = bf16[384,640]{1,0:T(8,128)(2,1)S(1)} all-gather(bf16[32,640]{1,0:T(8,128)(2,1)S(1)} %multiply_convert_fusion), channel_id=1, replica_groups=mesh['z'=12,'yl'=4,'x'=4,'yh'=2,'c'=2] {'z'}, dimensions={0}, use_global_device_ids=true | all-gather | bytes 532480 | tf_op jit(solution)/shard_map/all_gather | solution.py:170
  135.0 1.9 %divide_subtract_fusion = (f32[9,40,640]{2,1,0:T(8,128)}, f32[9,40,640]{2,1,0:T(8,128)}, f32[9,40,640]{2,1,0:T(8,128)}) fusion(f32[9,40,640]{2,1,0:T(8,128)S(1)} %copy-done.3, bf16[9,40,640]{2,1,0:T(8,128)(2,1)S(1)} %bitcast.48, f32[9,40,640]{2,1,0:T(8,128)S(1)} %copy-done.5, f32[9,40,640]{2,1,0:T(8,128)S(1)} %copy-done.6), kind=kLoop, calls=%fused_computation.10 | loop fusion | flops 2995200 | bytes 5990400 | tf_op jit(solution)/shard_map/sub | solution.py:175
  (33 shorter events, 4.5 us)
Async XLA Ops:
  0.6 3.1 %copy-start = (f32[40,1024]{1,0:T(8,128)S(1)}, f32[40,1024]{1,0:T(8,128)}, u32[]{:S(2)}) copy-start(f32[40,1024]{1,0:T(8,128)} %grad_ref.1) | copy-start | bytes 491524
  1.9 0.8 copy-start.2
  7.0 11.8 %collective-permute-start = (f32[8,40,1024]{2,1,0:T(8,128)}, f32[8,40,1024]{2,1,0:T(8,128)}, u32[]{:S(2)}, u32[]{:S(2)}) collective-permute-start(f32[8,40,1024]{2,1,0:T(8,128)} %dynamic-slice_bitcast_fusion), channel_id=1, source_target_pairs={{0,1},{1,0},{2,3},{3,2},{4,5},{5,4},{6,7},{7,6},{8,9},{9,8},{10,11... | collective-permute-start | bytes 3932168 | tf_op jit(solution)/shard_map/ppermute | solution.py:128
  11.0 24.1 %all-to-all-start = ((bf16[8,40,1024]{2,1,0:T(8,128)(2,1)}), bf16[8,40,1024]{2,1,0:T(8,128)(2,1)}, u32[]{:S(2)}, u32[]{:S(2)}) async-start(bf16[8,40,1024]{2,1,0:T(8,128)(2,1)} %get-tuple-element.12), calls=%async_computation | async-start | bytes 1310720 | tf_op jit(solution)/shard_map/all_to_all | solution.py:121
  35.1 4.2 %collective-permute-start.1 = (bf16[8,40,1024]{2,1,0:T(8,128)(2,1)}, bf16[8,40,1024]{2,1,0:T(8,128)(2,1)S(1)}, u32[]{:S(2)}, u32[]{:S(2)}) collective-permute-start(bf16[8,40,1024]{2,1,0:T(8,128)(2,1)} %all-to-all-done), channel_id=1, source_target_pairs={{0,1},{1,0},{2,3},{3,2},{4,5},{5,4},{6,7},{7,6},{8,9},{9,8},{10,11... | collective-permute-start | bytes 1966088 | tf_op jit(solution)/shard_map/ppermute | solution.py:132
  40.6 1.6 %copy-start.1 = (bf16[640,1024]{1,0:T(8,128)(2,1)}, bf16[640,1024]{1,0:T(8,128)(2,1)S(1)}, u32[]{:S(2)}) copy-start(bf16[640,1024]{1,0:T(8,128)(2,1)S(1)} %bitcast_select_fusion.act_ref) | copy-start | bytes 3932164
  42.2 22.2 %copy-start.4 = (bf16[8,40,1024]{2,1,0:T(8,128)(2,1)S(1)}, bf16[8,40,1024]{2,1,0:T(8,128)(2,1)}, u32[]{:S(2)}) copy-start(bf16[8,40,1024]{2,1,0:T(8,128)(2,1)} %fusion) | copy-start | bytes 1966084
  42.2 45.0 %all-to-all-start.1 = ((bf16[12,32,640]{2,1,0:T(8,128)(2,1)}), bf16[12,32,640]{2,1,0:T(8,128)(2,1)S(1)}, u32[]{:S(2)}, u32[]{:S(2)}) async-start(bf16[12,32,640]{2,1,0:T(8,128)(2,1)} %bitcast.19), calls=%async_computation.1 | async-start | bytes 983040 | tf_op jit(solution)/shard_map/all_to_all | solution.py:141
  64.4 27.7 %collective-permute-start.2 = (bf16[2,40,1024]{2,1,0:T(8,128)(2,1)S(1)}, bf16[2,40,1024]{2,1,0:T(8,128)(2,1)S(1)}, u32[]{:S(2)}, u32[]{:S(2)}) collective-permute-start(bf16[2,40,1024]{2,1,0:T(8,128)(2,1)S(1)} %get-tuple-element.22), channel_id=1, source_target_pairs={{0,4},{4,8},{8,12},{12,0},{1,5},{5,9},{9,13},{13,1},{2,6},{6,10},{... | collective-permute-start | bytes 491528 | tf_op jit(solution)/shard_map/ppermute | solution.py:150
  66.4 25.8 %collective-permute-start.3 = (bf16[2,40,1024]{2,1,0:T(8,128)(2,1)S(1)}, bf16[2,40,1024]{2,1,0:T(8,128)(2,1)S(1)}, u32[]{:S(2)}, u32[]{:S(2)}) collective-permute-start(bf16[2,40,1024]{2,1,0:T(8,128)(2,1)S(1)} %get-tuple-element.24), channel_id=1, source_target_pairs={{0,8},{4,12},{8,0},{12,4},{1,9},{5,13},{9,1},{13,5},{2,10},{6,14},... | collective-permute-start | bytes 491528 | tf_op jit(solution)/shard_map/ppermute | solution.py:150
  70.6 21.6 %collective-permute-start.4 = (bf16[2,40,1024]{2,1,0:T(8,128)(2,1)S(1)}, bf16[2,40,1024]{2,1,0:T(8,128)(2,1)S(1)}, u32[]{:S(2)}, u32[]{:S(2)}) collective-permute-start(bf16[2,40,1024]{2,1,0:T(8,128)(2,1)S(1)} %get-tuple-element.23), channel_id=1, source_target_pairs={{0,12},{4,0},{8,4},{12,8},{1,13},{5,1},{9,5},{13,9},{2,14},{6,2},{... | collective-permute-start | bytes 491528 | tf_op jit(solution)/shard_map/ppermute | solution.py:150
  87.9 21.4 %all-to-all-start.2 = ((f32[4,32,640]{2,1,0:T(8,128)}), f32[4,32,640]{2,1,0:T(8,128)S(1)}, u32[]{:S(2)}, u32[]{:S(2)}) async-start(f32[4,32,640]{2,1,0:T(8,128)} %sum_z.1), calls=%async_computation.2 | async-start | bytes 655360 | tf_op jit(solution)/shard_map/all_to_all | solution.py:168
  92.9 10.6 %collective-permute-start.5 = (bf16[40,1024]{1,0:T(8,128)(2,1)S(1)}, bf16[40,1024]{1,0:T(8,128)(2,1)S(1)}, u32[]{:S(2)}, u32[]{:S(2)}) collective-permute-start(bf16[40,1024]{1,0:T(8,128)(2,1)S(1)} %get-tuple-element.25), channel_id=1, source_target_pairs={{0,2},{2,0},{1,3},{3,1},{4,6},{6,4},{5,7},{7,5},{8,10},{10,8},{9,1... | collective-permute-start | bytes 245768 | tf_op jit(solution)/shard_map/ppermute | solution.py:155
  103.5 0.6 copy-start.7
  106.2 28.8 %copy-start.6 = (f32[9,40,640]{2,1,0:T(8,128)S(1)}, f32[9,40,640]{2,1,0:T(8,128)}, u32[]{:S(2)}) copy-start(f32[9,40,640]{2,1,0:T(8,128)} %param.12) | copy-start | bytes 2764804
  109.3 25.7 %copy-start.3 = (f32[9,40,640]{2,1,0:T(8,128)S(1)}, f32[9,40,640]{2,1,0:T(8,128)}, u32[]{:S(2)}) copy-start(f32[9,40,640]{2,1,0:T(8,128)} %param.10) | copy-start | bytes 2764804
  109.3 25.7 %copy-start.5 = (f32[9,40,640]{2,1,0:T(8,128)S(1)}, f32[9,40,640]{2,1,0:T(8,128)}, u32[]{:S(2)}) copy-start(f32[9,40,640]{2,1,0:T(8,128)} %param.11) | copy-start | bytes 2764804

commit v8 on v7

--- a/solution.py
+++ b/solution.py
@@ -39,7 +39,7 @@
     return jnp.sum(jnp.where(eye, row, 0.0), axis=1, keepdims=True)
 
 
-def norm_kernel(x_ref, gain_ref, bias_ref, act_ref, normed_ref, pre_ref, inv_ref):
+def norm_kernel(x_ref, gain_ref, bias_ref, act_ref, normed_ref, inv_ref):
     x = x_ref[...]
     count = x.shape[0] * x.shape[1]
     mean = jnp.sum(jnp.sum(x, axis=0, keepdims=True), axis=1, keepdims=True) / count
@@ -49,7 +49,6 @@
     normed = centred * inv
     pre = normed * column(gain_ref[...]) + column(bias_ref[...])
     normed_ref[...] = normed
-    pre_ref[...] = pre
     inv_ref[...] = jnp.broadcast_to(inv, inv_ref.shape)
     act = (pre * jax.nn.sigmoid(pre)).astype(jnp.bfloat16)
     for copy in range(act_ref.shape[0]):
@@ -80,11 +79,12 @@
         out_ref[copy] = total
 
 
-def back_kernel(keep_ref, taken_ref, normed_ref, pre_ref, inv_ref, gain_ref, grad_ref, out_ref):
+def back_kernel(keep_ref, taken_ref, normed_ref, inv_ref, gain_ref, bias_ref, grad_ref, out_ref):
     grad_act = keep_ref[...].astype(jnp.float32) + taken_ref[...].astype(jnp.float32)
-    pre, normed = pre_ref[...], normed_ref[...]
+    normed, gain = normed_ref[...], column(gain_ref[...])
+    pre = normed * gain + column(bias_ref[...])
     s = jax.nn.sigmoid(pre)
-    gn = grad_act * s * (1.0 + pre * (1.0 - s)) * column(gain_ref[...])
+    gn = grad_act * s * (1.0 + pre * (1.0 - s)) * gain
     count = gn.shape[0] * gn.shape[1]
     first = jnp.sum(jnp.sum(gn, axis=0, keepdims=True), axis=1, keepdims=True) / count
     second = jnp.sum(jnp.sum(gn * normed, axis=0, keepdims=True), axis=1, keepdims=True) / count
@@ -104,10 +104,10 @@
     gain_row, bias_row = norm_gain[None, :], norm_bias[None, :]
 
     tile = jax.ShapeDtypeStruct((local_ch, width), f32)
-    act, normed, pre_act, inv = pl.pallas_call(
+    act, normed, inv = pl.pallas_call(
         norm_kernel,
         out_shape=(
-            jax.ShapeDtypeStruct((n_xy, local_ch, width), bf16), tile, tile,
+            jax.ShapeDtypeStruct((n_xy, local_ch, width), bf16), tile,
             jax.ShapeDtypeStruct((8, 128), f32),
         ),
         name="norm",
@@ -157,7 +157,7 @@
     )
     keep = lax.dynamic_index_in_dim(pair, row, 0, keepdims=False)
     input_grad = pl.pallas_call(back_kernel, out_shape=tile, name="back")(
-        keep, taken, normed, pre_act, inv, gain_row, out_grad
+        keep, taken, normed, inv, gain_row, bias_row, out_grad
     )
 
     z_sum = pl.pallas_call(

time: 138 us -> 138 us (level)
  no operation moved by 1% of the time
where the time goes in v8:
time: 138 us; the launch traced here: 137 us
  starting transfers between devices  49.1 us (36%)
  waiting for transfers between devices  38.2 us (28%)
  blocking collectives  25.6 us (19%)
  Pallas kernels  8.27 us (6%)
  other arithmetic  6.89 us (5%)
  local copies, waits for them, and re-layouts  4.49 us (3%)
  matrix products  3.48 us (3%)
    all_gather x1, blocking collectives, step(): total = lax.all_gather(total, 'z', axis=0, tiled=True)  25.6 us
    all_to_all x1, starting transfers between devices, step(): by_z = lax.all_to_all(taps, 'z', 0, 0, tiled=True)  22.2 us
    all_to_all x1, waiting for transfers between devices, step(): by_xy = lax.all_to_all(act, XY, 0, 0, tiled=True)  14 us
    all_to_all x1, waiting for transfers between devices, step(): by_z = lax.all_to_all(taps, 'z', 0, 0, tiled=True)  13.5 us
    ppermute x3, starting transfers between devices, step(): lax.ppermute(pick(k), 'x', [(i, (i + k) % n_x) for i in range(n_x)])  9.21 us
    ppermute x1, waiting for transfers between devices, step(): lax.ppermute(lax.dynamic_index_in_dim(pair, 1 - row, 0, keepdims=False),...  8.68 us
    all_to_all x1, starting transfers between devices, step(): by_xy = lax.all_to_all(act, XY, 0, 0, tiled=True)  7.77 us
    all_to_all x1, starting transfers between devices, step(): by_yl = lax.all_to_all(z_sum, 'yl', 0, 0, tiled=True)  4.19 us
  transfers between devices with their start and end apart: 9, of which 4 were waited for; matrix products, arithmetic and copies ran while one was open for 2% of the time, Pallas kernels for 6%

profile of v8, /device:TPU:16, one launch (start us, length us, event | category | flops | bytes accessed | tf_op | source)
XLA Modules:
  0.0 136.9 jit_solution(3651430637787485396)
XLA Ops:
  0.6 1.3 convert_element_type.39
  3.9 1.9 %fusion.3 = f32[8,2,40,1024]{3,2,1,0:T(8,128)S(1)} fusion(bf16[8,2,40,360]{3,2,1,0:T(8,128)(2,1)} %bitcast.47, bf16[384,1024]{1,0:T(8,128)(2,1)S(1)} %nine.1), kind=kOutput, calls=%fused_computation.12 | convolution fusion | flops 471859200 | bytes 3819520 | tf_op jit(solution)/shard_map/dot_general | solution.py:123
  5.8 1.2 dynamic-slice_bitcast_fusion
  7.0 1.9 %collective-permute-start = (f32[8,40,1024]{2,1,0:T(8,128)}, f32[8,40,1024]{2,1,0:T(8,128)}, u32[]{:S(2)}, u32[]{:S(2)}) collective-permute-start(f32[8,40,1024]{2,1,0:T(8,128)} %dynamic-slice_bitcast_fusion), channel_id=1, source_target_pairs={{0,1},{1,0},{2,3},{3,2},{4,5},{5,4},{6,7},{7,6},{8,9},{9,8},{10,11... | collective-permute-start | bytes 3932168 | tf_op jit(solution)/shard_map/ppermute | solution.py:128
  8.9 2.1 %norm.1 = (bf16[8,40,1024]{2,1,0:T(8,128)(2,1)}, f32[40,1024]{1,0:T(8,128)}, f32[8,128]{1,0:T(8,128)}) custom-call(f32[40,1024]{1,0:T(8,128)} %x_ref.3, f32[1,40]{1,0:T(1,128)} %bitcast.49, f32[1,40]{1,0:T(1,128)} %bitcast.51), custom_call_target="tpu_custom_call" | custom-call | tf_op jit(solution)/shard_map/norm/pallas_call | solution.py:107
  11.0 7.8 %all-to-all-start = ((bf16[8,40,1024]{2,1,0:T(8,128)(2,1)}), bf16[8,40,1024]{2,1,0:T(8,128)(2,1)}, u32[]{:S(2)}, u32[]{:S(2)}) async-start(bf16[8,40,1024]{2,1,0:T(8,128)(2,1)} %get-tuple-element.11), calls=%async_computation | async-start | bytes 1310720 | tf_op jit(solution)/shard_map/all_to_all | solution.py:121
  18.8 2.3 %fusion = bf16[8,40,1024]{2,1,0:T(8,128)(2,1)} fusion(f32[8,40,1024]{2,1,0:T(8,128)} %collective-permute-done, f32[8,2,40,1024]{3,2,1,0:T(8,128)S(1)} %fusion.3, s32[]{:T(128)S(6)} %select_n.32), kind=kLoop, calls=%fused_computation.5 | loop fusion | flops 655360 | bytes 3276804 | tf_op jit(solution)/shard_map/convert_element_type | solution.py:130
  21.1 14.0 %all-to-all-done = bf16[8,40,1024]{2,1,0:T(8,128)(2,1)} async-done(((bf16[8,40,1024]{2,1,0:T(8,128)(2,1)}), bf16[8,40,1024]{2,1,0:T(8,128)(2,1)}, u32[]{:S(2)}, u32[]{:S(2)}) %all-to-all-start) | async-done | bytes 655392 | tf_op jit(solution)/shard_map/all_to_all | solution.py:121
  35.1 1.9 %collective-permute-start.1 = (bf16[8,40,1024]{2,1,0:T(8,128)(2,1)}, bf16[8,40,1024]{2,1,0:T(8,128)(2,1)S(1)}, u32[]{:S(2)}, u32[]{:S(2)}) collective-permute-start(bf16[8,40,1024]{2,1,0:T(8,128)(2,1)} %all-to-all-done), channel_id=1, source_target_pairs={{0,1},{1,0},{2,3},{3,2},{4,5},{5,4},{6,7},{7,6},{8,9},{9,8},{10,11... | collective-permute-start | bytes 1966088 | tf_op jit(solution)/shard_map/ppermute | solution.py:132
  37.2 2.1 %collective-permute-done.1 = bf16[8,40,1024]{2,1,0:T(8,128)(2,1)S(1)} collective-permute-done((bf16[8,40,1024]{2,1,0:T(8,128)(2,1)}, bf16[8,40,1024]{2,1,0:T(8,128)(2,1)S(1)}, u32[]{:S(2)}, u32[]{:S(2)}) %collective-permute-start.1) | collective-permute-done | bytes 655392 | tf_op jit(solution)/shard_map/ppermute | solution.py:132
  39.3 1.2 bitcast_select_fusion.act_ref
  40.5 1.6 %convolution_convert_fusion = bf16[640,384]{0,1:T(8,128)(2,1)} fusion(bf16[640,1024]{1,0:T(8,128)(2,1)S(1)} %bitcast_select_fusion.act_ref, bf16[384,1024]{1,0:T(8,128)(2,1)S(1)} %nine.1), kind=kOutput, calls=%fused_computation.7 | convolution fusion | flops 503562240 | bytes 2588672 | tf_op jit(solution)/shard_map/dot_general | solution.py:137
  42.1 22.2 %all-to-all-start.1 = ((bf16[12,32,640]{2,1,0:T(8,128)(2,1)}), bf16[12,32,640]{2,1,0:T(8,128)(2,1)S(1)}, u32[]{:S(2)}, u32[]{:S(2)}) async-start(bf16[12,32,640]{2,1,0:T(8,128)(2,1)} %bitcast.19), calls=%async_computation.1 | async-start | bytes 983040 | tf_op jit(solution)/shard_map/all_to_all | solution.py:141
  64.4 1.9 %collective-permute-start.2 = (bf16[2,40,1024]{2,1,0:T(8,128)(2,1)S(1)}, bf16[2,40,1024]{2,1,0:T(8,128)(2,1)S(1)}, u32[]{:S(2)}, u32[]{:S(2)}) collective-permute-start(bf16[2,40,1024]{2,1,0:T(8,128)(2,1)S(1)} %get-tuple-element.20), channel_id=1, source_target_pairs={{0,4},{4,8},{8,12},{12,0},{1,5},{5,9},{9,13},{13,1},{2,6},{6,10},{... | collective-permute-start | bytes 491528 | tf_op jit(solution)/shard_map/ppermute | solution.py:150
  66.3 4.2 %collective-permute-start.3 = (bf16[2,40,1024]{2,1,0:T(8,128)(2,1)S(1)}, bf16[2,40,1024]{2,1,0:T(8,128)(2,1)S(1)}, u32[]{:S(2)}, u32[]{:S(2)}) collective-permute-start(bf16[2,40,1024]{2,1,0:T(8,128)(2,1)S(1)} %get-tuple-element.22), channel_id=1, source_target_pairs={{0,8},{4,12},{8,0},{12,4},{1,9},{5,13},{9,1},{13,5},{2,10},{6,14},... | collective-permute-start | bytes 491528 | tf_op jit(solution)/shard_map/ppermute | solution.py:150
  70.5 3.1 %collective-permute-start.4 = (bf16[2,40,1024]{2,1,0:T(8,128)(2,1)S(1)}, bf16[2,40,1024]{2,1,0:T(8,128)(2,1)S(1)}, u32[]{:S(2)}, u32[]{:S(2)}) collective-permute-start(bf16[2,40,1024]{2,1,0:T(8,128)(2,1)S(1)} %get-tuple-element.21), channel_id=1, source_target_pairs={{0,12},{4,0},{8,4},{12,8},{1,13},{5,1},{9,5},{13,9},{2,14},{6,2},{... | collective-permute-start | bytes 491528 | tf_op jit(solution)/shard_map/ppermute | solution.py:150
  73.6 13.5 %all-to-all-done.1.parts_ref = bf16[12,32,640]{2,1,0:T(8,128)(2,1)S(1)} async-done(((bf16[12,32,640]{2,1,0:T(8,128)(2,1)}), bf16[12,32,640]{2,1,0:T(8,128)(2,1)S(1)}, u32[]{:S(2)}, u32[]{:S(2)}) %all-to-all-start.1) | async-done | bytes 491552 | tf_op jit(solution)/shard_map/all_to_all | solution.py:141
  87.9 4.2 %all-to-all-start.2 = ((f32[4,32,640]{2,1,0:T(8,128)}), f32[4,32,640]{2,1,0:T(8,128)S(1)}, u32[]{:S(2)}, u32[]{:S(2)}) async-start(f32[4,32,640]{2,1,0:T(8,128)} %sum_z.1), calls=%async_computation.2 | async-start | bytes 655360 | tf_op jit(solution)/shard_map/all_to_all | solution.py:168
  92.8 1.9 %collective-permute-start.5 = (bf16[40,1024]{1,0:T(8,128)(2,1)S(1)}, bf16[40,1024]{1,0:T(8,128)(2,1)S(1)}, u32[]{:S(2)}, u32[]{:S(2)}) collective-permute-start(bf16[40,1024]{1,0:T(8,128)(2,1)S(1)} %get-tuple-element.23), channel_id=1, source_target_pairs={{0,2},{2,0},{1,3},{3,1},{4,6},{6,4},{5,7},{7,5},{8,10},{10,8},{9,1... | collective-permute-start | bytes 245768 | tf_op jit(solution)/shard_map/ppermute | solution.py:155
  94.8 8.7 %collective-permute-done.5.taken_ref = bf16[40,1024]{1,0:T(8,128)(2,1)S(1)} collective-permute-done((bf16[40,1024]{1,0:T(8,128)(2,1)S(1)}, bf16[40,1024]{1,0:T(8,128)(2,1)S(1)}, u32[]{:S(2)}, u32[]{:S(2)}) %collective-permute-start.5) | collective-permute-done | bytes 81952 | tf_op jit(solution)/shard_map/ppermute | solution.py:155
  104.1 2.1 %back.1 = f32[40,1024]{1,0:T(8,128)} custom-call(bf16[40,1024]{1,0:T(8,128)(2,1)} %get-tuple-element.24.keep_ref, bf16[40,1024]{1,0:T(8,128)(2,1)} %copy-done.7, f32[40,1024]{1,0:T(8,128)} %get-tuple-element.15.normed_ref, f32[8,128]{1,0:T(8,128)} %get-tuple-element.16.inv_ref, f32[1,40]{1,0:T(1,128)} %bitcast.50, f32[1,40]{1,0:T(1,128)} %bitcast.52, ...), custom_call_target="tpu_custom_call" | custom-call | tf_op jit(solution)/shard_map/back/pallas_call | solution.py:159
  106.1 3.1 %forward.1 = f32[40,1024]{1,0:T(8,128)} custom-call(bf16[360,640]{1,0:T(8,128)(2,1)} %bitcast.44, bf16[640,1024]{1,0:T(8,128)(2,1)} %copy-done.1, f32[40,1024]{1,0:T(8,128)} %x_ref.3), custom_call_target="tpu_custom_call" | custom-call | tf_op jit(solution)/shard_map/forward/pallas_call | solution.py:143
  109.3 25.6 %all_gather.3 = bf16[384,640]{1,0:T(8,128)(2,1)S(1)} all-gather(bf16[32,640]{1,0:T(8,128)(2,1)S(1)} %multiply_convert_fusion), channel_id=1, replica_groups=mesh['z'=12,'yl'=4,'x'=4,'yh'=2,'c'=2] {'z'}, dimensions={0}, use_global_device_ids=true | all-gather | bytes 532480 | tf_op jit(solution)/shard_map/all_gather | solution.py:170
  134.9 1.9 %divide_subtract_fusion = (f32[9,40,640]{2,1,0:T(8,128)}, f32[9,40,640]{2,1,0:T(8,128)}, f32[9,40,640]{2,1,0:T(8,128)}) fusion(f32[9,40,640]{2,1,0:T(8,128)S(1)} %copy-done.3, bf16[9,40,640]{2,1,0:T(8,128)(2,1)S(1)} %bitcast.48, f32[9,40,640]{2,1,0:T(8,128)S(1)} %copy-done.5, f32[9,40,640]{2,1,0:T(8,128)S(1)} %copy-done.6), kind=kLoop, calls=%fused_computation.10 | loop fusion | flops 2995200 | bytes 5990400 | tf_op jit(solution)/shard_map/sub | solution.py:175
  (33 shorter events, 4.5 us)
Async XLA Ops:
  0.6 3.1 %copy-start = (f32[40,1024]{1,0:T(8,128)S(1)}, f32[40,1024]{1,0:T(8,128)}, u32[]{:S(2)}) copy-start(f32[40,1024]{1,0:T(8,128)} %grad_ref.1) | copy-start | bytes 491524
  1.9 0.8 copy-start.2
  7.0 11.8 %collective-permute-start = (f32[8,40,1024]{2,1,0:T(8,128)}, f32[8,40,1024]{2,1,0:T(8,128)}, u32[]{:S(2)}, u32[]{:S(2)}) collective-permute-start(f32[8,40,1024]{2,1,0:T(8,128)} %dynamic-slice_bitcast_fusion), channel_id=1, source_target_pairs={{0,1},{1,0},{2,3},{3,2},{4,5},{5,4},{6,7},{7,6},{8,9},{9,8},{10,11... | collective-permute-start | bytes 3932168 | tf_op jit(solution)/shard_map/ppermute | solution.py:128
  11.0 24.1 %all-to-all-start = ((bf16[8,40,1024]{2,1,0:T(8,128)(2,1)}), bf16[8,40,1024]{2,1,0:T(8,128)(2,1)}, u32[]{:S(2)}, u32[]{:S(2)}) async-start(bf16[8,40,1024]{2,1,0:T(8,128)(2,1)} %get-tuple-element.11), calls=%async_computation | async-start | bytes 1310720 | tf_op jit(solution)/shard_map/all_to_all | solution.py:121
  35.1 4.2 %collective-permute-start.1 = (bf16[8,40,1024]{2,1,0:T(8,128)(2,1)}, bf16[8,40,1024]{2,1,0:T(8,128)(2,1)S(1)}, u32[]{:S(2)}, u32[]{:S(2)}) collective-permute-start(bf16[8,40,1024]{2,1,0:T(8,128)(2,1)} %all-to-all-done), channel_id=1, source_target_pairs={{0,1},{1,0},{2,3},{3,2},{4,5},{5,4},{6,7},{7,6},{8,9},{9,8},{10,11... | collective-permute-start | bytes 1966088 | tf_op jit(solution)/shard_map/ppermute | solution.py:132
  40.5 1.6 %copy-start.1 = (bf16[640,1024]{1,0:T(8,128)(2,1)}, bf16[640,1024]{1,0:T(8,128)(2,1)S(1)}, u32[]{:S(2)}) copy-start(bf16[640,1024]{1,0:T(8,128)(2,1)S(1)} %bitcast_select_fusion.act_ref) | copy-start | bytes 3932164
  42.1 22.2 %copy-start.4 = (bf16[8,40,1024]{2,1,0:T(8,128)(2,1)S(1)}, bf16[8,40,1024]{2,1,0:T(8,128)(2,1)}, u32[]{:S(2)}) copy-start(bf16[8,40,1024]{2,1,0:T(8,128)(2,1)} %fusion) | copy-start | bytes 1966084
  42.1 45.0 %all-to-all-start.1 = ((bf16[12,32,640]{2,1,0:T(8,128)(2,1)}), bf16[12,32,640]{2,1,0:T(8,128)(2,1)S(1)}, u32[]{:S(2)}, u32[]{:S(2)}) async-start(bf16[12,32,640]{2,1,0:T(8,128)(2,1)} %bitcast.19), calls=%async_computation.1 | async-start | bytes 983040 | tf_op jit(solution)/shard_map/all_to_all | solution.py:141
  64.4 27.7 %collective-permute-start.2 = (bf16[2,40,1024]{2,1,0:T(8,128)(2,1)S(1)}, bf16[2,40,1024]{2,1,0:T(8,128)(2,1)S(1)}, u32[]{:S(2)}, u32[]{:S(2)}) collective-permute-start(bf16[2,40,1024]{2,1,0:T(8,128)(2,1)S(1)} %get-tuple-element.20), channel_id=1, source_target_pairs={{0,4},{4,8},{8,12},{12,0},{1,5},{5,9},{9,13},{13,1},{2,6},{6,10},{... | collective-permute-start | bytes 491528 | tf_op jit(solution)/shard_map/ppermute | solution.py:150
  66.3 25.8 %collective-permute-start.3 = (bf16[2,40,1024]{2,1,0:T(8,128)(2,1)S(1)}, bf16[2,40,1024]{2,1,0:T(8,128)(2,1)S(1)}, u32[]{:S(2)}, u32[]{:S(2)}) collective-permute-start(bf16[2,40,1024]{2,1,0:T(8,128)(2,1)S(1)} %get-tuple-element.22), channel_id=1, source_target_pairs={{0,8},{4,12},{8,0},{12,4},{1,9},{5,13},{9,1},{13,5},{2,10},{6,14},... | collective-permute-start | bytes 491528 | tf_op jit(solution)/shard_map/ppermute | solution.py:150
  70.5 21.6 %collective-permute-start.4 = (bf16[2,40,1024]{2,1,0:T(8,128)(2,1)S(1)}, bf16[2,40,1024]{2,1,0:T(8,128)(2,1)S(1)}, u32[]{:S(2)}, u32[]{:S(2)}) collective-permute-start(bf16[2,40,1024]{2,1,0:T(8,128)(2,1)S(1)} %get-tuple-element.21), channel_id=1, source_target_pairs={{0,12},{4,0},{8,4},{12,8},{1,13},{5,1},{9,5},{13,9},{2,14},{6,2},{... | collective-permute-start | bytes 491528 | tf_op jit(solution)/shard_map/ppermute | solution.py:150
  87.9 21.4 %all-to-all-start.2 = ((f32[4,32,640]{2,1,0:T(8,128)}), f32[4,32,640]{2,1,0:T(8,128)S(1)}, u32[]{:S(2)}, u32[]{:S(2)}) async-start(f32[4,32,640]{2,1,0:T(8,128)} %sum_z.1), calls=%async_computation.2 | async-start | bytes 655360 | tf_op jit(solution)/shard_map/all_to_all | solution.py:168
  92.8 10.6 %collective-permute-start.5 = (bf16[40,1024]{1,0:T(8,128)(2,1)S(1)}, bf16[40,1024]{1,0:T(8,128)(2,1)S(1)}, u32[]{:S(2)}, u32[]{:S(2)}) collective-permute-start(bf16[40,1024]{1,0:T(8,128)(2,1)S(1)} %get-tuple-element.23), channel_id=1, source_target_pairs={{0,2},{2,0},{1,3},{3,1},{4,6},{6,4},{5,7},{7,5},{8,10},{10,8},{9,1... | collective-permute-start | bytes 245768 | tf_op jit(solution)/shard_map/ppermute | solution.py:155
  103.4 0.6 copy-start.7
  106.1 28.8 %copy-start.6 = (f32[9,40,640]{2,1,0:T(8,128)S(1)}, f32[9,40,640]{2,1,0:T(8,128)}, u32[]{:S(2)}) copy-start(f32[9,40,640]{2,1,0:T(8,128)} %param.12) | copy-start | bytes 2764804
  109.2 25.7 %copy-start.3 = (f32[9,40,640]{2,1,0:T(8,128)S(1)}, f32[9,40,640]{2,1,0:T(8,128)}, u32[]{:S(2)}) copy-start(f32[9,40,640]{2,1,0:T(8,128)} %param.10) | copy-start | bytes 2764804
  109.2 25.7 %copy-start.5 = (f32[9,40,640]{2,1,0:T(8,128)S(1)}, f32[9,40,640]{2,1,0:T(8,128)}, u32[]{:S(2)}) copy-start(f32[9,40,640]{2,1,0:T(8,128)} %param.11) | copy-start | bytes 2764804
